TPU v7x, 256 devices: a whole 4x4x8 slice. The times are simulated.
256 devices in a mesh: row: 16 (over z, core), cuts: 16 (over x, y).
Axes of the slice: x: 4, y: 4, z: 8, core: 2. Of those that a mesh axis runs over, the one named last changes fastest.
Arguments:
- ham_blocks: bfloat16 [384, 11, 128, 128], P('row'), may hold values from -0.078125 to 0.078125
- neighbors: int32 [384, 11], P('row'), may hold values from 0 to 383, as said below
- slice_widths: int32 [12], replicated, may hold values from 128 to 256, as said below
- interval_index: int32 [12], replicated, may hold values from 0 to 7
- start_vectors: bfloat16 [49152, 2048], P(('row', 'cuts'))
Outputs:
- corrected: bfloat16 [49152, 2048], P(('row', 'cuts'))
Inputs may be any that keep to these rules, and one draw needn't show every extreme that they name: `neighbors`: slot 0 of row block b is b, slots 1 and 2 are b + 8 and b - 8 modulo 384, every slot lies within 8 blocks of b modulo 384, and the 11 slots of a row block name distinct block columns. `slice_widths`: every slice holds 128 or 256 vectors, exactly four hold 256, and two of those stand side by side.
All inputs are finite; a program needn't handle non-finite values.
Results may differ from a plain program's by a relative error of at most 0.018.
Values may be sent and summed in bfloat16 or wider, within the bound.
No kernel may reach another device: no remote copies, remote signals or barrier semaphores. Data moves between devices by JAX's collectives and lax.ppermute only.
A program may use at most 64 MiB of HBM per device.

v0:
```python
import jax
import jax.numpy as jnp
from jax import lax
from jax.sharding import PartitionSpec as P

HB = 8
NV = 2048
SLICE_MAX = 256
NINT = 8


def passed_along(block, axis, distance):
    devices = range(lax.axis_size(axis))
    route = [(i - distance, i) for i in devices if i - distance in devices]
    return lax.ppermute(block, axis, route)


def extended(block, sides, width):
    for axis, dim in sides:
        count = lax.axis_size(axis)
        forward = [(i, i + 1) for i in range(count - 1)]
        forward.append((count - 1, 0))
        backward = [(target, source) for source, target in forward]
        low = lax.ppermute(
            lax.slice_in_dim(block, block.shape[dim] - width, None, axis=dim), axis, forward
        )
        high = lax.ppermute(lax.slice_in_dim(block, 0, width, axis=dim), axis, backward)
        block = jnp.concatenate([low, block, high], axis=dim)
    return block


def total_of_pieces(array, axis):
    return lax.all_gather(array, axis).astype(jnp.float32).sum(0)


def slice_index(columns, bounds):
    return jnp.sum((columns[:, None] >= bounds[None, :]).astype(jnp.int32), axis=1)


def take_tile(field, offset):
    return passed_along(field, "cuts", offset)


def body(ham_blocks, neighbors, slice_widths, interval_index, start_vectors):
    panel = lax.all_to_all(start_vectors, "cuts", split_axis=1, concat_axis=0, tiled=True)
    rows_here, tile_width = panel.shape
    blocks_here = ham_blocks.shape[0]
    block_rows = ham_blocks.shape[2]
    total_blocks = blocks_here * lax.axis_size("row")
    first_block = lax.axis_index("row") * blocks_here
    cut_index = lax.axis_index("cuts")
    bounds = jnp.cumsum(slice_widths)
    own_cols = cut_index * tile_width + jnp.arange(tile_width, dtype=jnp.int32)
    own_slice = slice_index(own_cols, bounds)
    onehot = (
        own_slice[:, None] == jnp.arange(slice_widths.shape[0], dtype=jnp.int32)[None, :]
    ).astype(jnp.float32)
    centre = -0.5 + jnp.dot(
        onehot, interval_index.astype(jnp.float32), precision=lax.Precision.HIGHEST
    ) / (NINT - 1)
    position = jnp.mod(neighbors - first_block + HB, total_blocks)

    def apply_ham(field):
        padded = extended(field, (("row", 0),), HB * block_rows)
        stacked = padded.reshape(blocks_here + 2 * HB, block_rows, tile_width)
        picked = stacked[position]
        result = jnp.einsum(
            "bnij,bnjw->biw", ham_blocks, picked, preferred_element_type=jnp.float32
        )
        return result.reshape(rows_here, tile_width)

    first = (apply_ham(panel) - centre[None, :] * panel.astype(jnp.float32)).astype(jnp.bfloat16)
    second = (
        2.0 * (apply_ham(first) - centre[None, :] * first.astype(jnp.float32))
        - panel.astype(jnp.float32)
    ).astype(jnp.bfloat16)
    filtered = (
        2.0 * (apply_ham(second) - centre[None, :] * second.astype(jnp.float32))
        - first.astype(jnp.float32)
    ).astype(jnp.bfloat16)
    reach_tiles = (2 * SLICE_MAX - 128 + tile_width - 1) // tile_width
    window_width = (2 * reach_tiles + 1) * tile_width
    lower_tiles = [take_tile(filtered, offset) for offset in range(reach_tiles, 0, -1)]
    upper_tiles = [take_tile(filtered, -offset) for offset in range(1, reach_tiles + 1)]
    window = jnp.concatenate(lower_tiles + [filtered] + upper_tiles, axis=1)
    window_cols = (cut_index - reach_tiles) * tile_width + jnp.arange(window_width, dtype=jnp.int32)
    valid_cols = (window_cols >= 0) & (window_cols < NV)
    window_slice = slice_index(window_cols, bounds)
    adjacent = valid_cols[None, :] & (jnp.abs(own_slice[:, None] - window_slice[None, :]) <= 1)
    local_gram = lax.dot_general(
        filtered, window, (((0,), (0,)), ((), ())), preferred_element_type=jnp.float32
    )
    local_squares = jnp.sum(jnp.square(window.astype(jnp.float32)), axis=0)
    gram, squares = (
        total_of_pieces(local_gram.astype(jnp.bfloat16), "row").astype(jnp.float32),
        total_of_pieces(local_squares.astype(jnp.bfloat16), "row").astype(jnp.float32),
    )
    rows_all = rows_here * lax.axis_size("row")
    inv_norm = lax.rsqrt(squares / rows_all + 1e-05)
    own_norm = inv_norm[reach_tiles * tile_width : (reach_tiles + 1) * tile_width]
    normed = gram * own_norm[:, None] * inv_norm[None, :] / rows_all
    diagonal_mask = (own_cols[:, None] == window_cols[None, :]).astype(jnp.float32)
    coefficients = jnp.where(adjacent, 1.5 * diagonal_mask - 0.5 * normed, 0.0)
    weights = (coefficients * inv_norm[None, :]).astype(jnp.bfloat16)
    corrected = lax.dot_general(
        window, weights, (((1,), (1,)), ((), ())), preferred_element_type=jnp.float32
    ).astype(jnp.bfloat16)
    return lax.all_to_all(corrected, "cuts", split_axis=0, concat_axis=1, tiled=True)


def solution(mesh):
    return jax.shard_map(
        body,
        mesh=mesh,
        in_specs=(P("row", None, None, None), P("row", None), P(), P(), P(("row", "cuts"), None)),
        out_specs=P(("row", "cuts"), None),
        check_vma=False,
    )
```

profile of v0, /device:TPU:33, one launch (start us, length us, event | category | flops | bytes accessed | tf_op | source)
XLA Modules:
  0.0 281.1 jit_solution(10266406394125243742)
XLA Ops:
  6.5 1.1 copy-done
  7.7 1.1 copy_bitcast_fusion.1
  8.8 6.8 %all-to-all-start = ((bf16[192,16,128]{2,0,1:T(8,128)(2,1)}), bf16[192,16,128]{2,0,1:T(8,128)(2,1)S(1)}, u32[]{:S(2)}, u32[]{:S(2)}) async-start(bf16[192,16,128]{2,0,1:T(8,128)(2,1)} %copy_bitcast_fusion.1), calls=%async_computation | async-start | bytes 1572864 | tf_op jit(solution)/shard_map/all_to_all | solution.py:45
  15.5 0.0 all-gather.5.cloned.1.call-start
  15.6 0.7 compare_select_fusion
  16.3 0.1 copy.17
  16.4 0.1 reshape.92
  16.5 0.8 reduce-window.8
  17.3 0.1 convert_reduce_fusion.3
  17.4 10.9 %all-to-all-done = bf16[192,16,128]{2,0,1:T(8,128)(2,1)S(1)} async-done(((bf16[192,16,128]{2,0,1:T(8,128)(2,1)}), bf16[192,16,128]{2,0,1:T(8,128)(2,1)S(1)}, u32[]{:S(2)}, u32[]{:S(2)}) %all-to-all-start) | async-done | bytes 786464 | tf_op jit(solution)/shard_map/all_to_all | solution.py:45
  28.4 4.1 %collective-permute-start = (bf16[1024,128]{1,0:T(8,128)(2,1)S(1)}, bf16[1024,128]{1,0:T(8,128)(2,1)S(1)}, u32[]{:S(2)}, u32[]{:S(2)}) collective-permute-start(bf16[1024,128]{1,0:T(8,128)(2,1)S(1)} %get-tuple-element.9), channel_id=1, source_target_pairs={{0,16},{16,32},{32,48},{48,64},{64,80},{80,96},{96,112},{112,128},... | collective-permute-start | bytes 786440 | tf_op jit(solution)/shard_map/ppermute | solution.py:24
  32.5 0.2 fusion.8
  32.7 3.1 %collective-permute-done = bf16[1024,128]{1,0:T(8,128)(2,1)S(1)} collective-permute-done((bf16[1024,128]{1,0:T(8,128)(2,1)S(1)}, bf16[1024,128]{1,0:T(8,128)(2,1)S(1)}, u32[]{:S(2)}, u32[]{:S(2)}) %collective-permute-start) | collective-permute-done | bytes 262176 | tf_op jit(solution)/shard_map/ppermute | solution.py:24
  35.8 2.5 collective-permute-done.1
  38.3 0.1 pad_maximum_fusion
  38.3 10.2 %gather_fusion = bf16[264,128,128]{2,1,0:T(8,128)(2,1)} fusion(bf16[40,128,128]{2,1,0:T(8,128)(2,1)S(1)} %bitcast.71, s32[1024]{0:T(1024)S(1)} %pad_clamp_fusion), kind=kCustom, calls=%fused_computation | custom fusion | bytes 17302560 | tf_op jit(solution)/shard_map/gather | solution.py:66
  48.5 8.3 %fusion.31 = f32[24,128,128,1]{1,2,3,0:T(8,128)S(1)} fusion(bf16[24,11,128,128]{3,2,1,0:T(8,128)(2,1)} %param.5, bf16[24,11,128,128]{3,2,1,0:T(8,128)(2,1)} %bitcast.74), kind=kOutput, calls=%fused_computation.70 | convolution fusion | flops 1107296256 | bytes 18874368 | tf_op jit(solution)/shard_map/bnij,bnjw->biw/dot_general | solution.py:67
  56.9 0.3 fusion.1
  57.2 0.0 collective-permute-start.2
  57.2 0.5 collective-permute-start.3
  57.7 2.8 %collective-permute-done.2 = bf16[1024,128]{1,0:T(8,128)(2,1)S(1)} collective-permute-done((bf16[1024,128]{1,0:T(8,128)(2,1)S(1)}, bf16[1024,128]{1,0:T(8,128)(2,1)S(1)}, u32[]{:S(2)}, u32[]{:S(2)}) %collective-permute-start.2) | collective-permute-done | bytes 262176 | tf_op jit(solution)/shard_map/ppermute | solution.py:24
  60.5 2.8 collective-permute-done.3
  63.3 0.1 pad_maximum_fusion.1
  63.4 10.2 %gather_fusion.1 = bf16[264,128,128]{2,1,0:T(8,128)(2,1)} fusion(bf16[40,128,128]{2,1,0:T(8,128)(2,1)S(1)} %bitcast.72, s32[1024]{0:T(1024)S(1)} %pad_clamp_fusion), kind=kCustom, calls=%fused_computation.1 | custom fusion | bytes 17302560 | tf_op jit(solution)/shard_map/gather | solution.py:66
  73.5 8.3 %fusion.32 = f32[24,128,128,1]{1,2,3,0:T(8,128)S(1)} fusion(bf16[24,11,128,128]{3,2,1,0:T(8,128)(2,1)} %param.5, bf16[24,11,128,128]{3,2,1,0:T(8,128)(2,1)} %bitcast.75), kind=kOutput, calls=%fused_computation.71 | convolution fusion | flops 1107296256 | bytes 18874368 | tf_op jit(solution)/shard_map/bnij,bnjw->biw/dot_general | solution.py:67
  81.9 0.4 fusion.2
  82.4 0.0 collective-permute-start.4
  82.4 0.5 collective-permute-start.5
  82.9 2.8 %collective-permute-done.4 = bf16[1024,128]{1,0:T(8,128)(2,1)S(1)} collective-permute-done((bf16[1024,128]{1,0:T(8,128)(2,1)S(1)}, bf16[1024,128]{1,0:T(8,128)(2,1)S(1)}, u32[]{:S(2)}, u32[]{:S(2)}) %collective-permute-start.4) | collective-permute-done | bytes 262176 | tf_op jit(solution)/shard_map/ppermute | solution.py:24
  85.7 5.2 %collective-permute-done.5 = bf16[1024,128]{1,0:T(8,128)(2,1)S(1)} collective-permute-done((bf16[1024,128]{1,0:T(8,128)(2,1)S(1)}, bf16[1024,128]{1,0:T(8,128)(2,1)S(1)}, u32[]{:S(2)}, u32[]{:S(2)}) %collective-permute-start.5) | collective-permute-done | bytes 262176 | tf_op jit(solution)/shard_map/ppermute | solution.py:27
  90.9 0.1 pad_maximum_fusion.2
  91.0 10.3 %gather_fusion.2 = bf16[264,128,128]{2,1,0:T(8,128)(2,1)} fusion(bf16[40,128,128]{2,1,0:T(8,128)(2,1)S(1)} %bitcast.70, s32[1024]{0:T(1024)S(1)} %pad_clamp_fusion), kind=kCustom, calls=%fused_computation.2 | custom fusion | bytes 17302560 | tf_op jit(solution)/shard_map/gather | solution.py:66
  101.3 0.0 copy-start.4
  101.3 8.4 %fusion.33 = f32[24,128,128,1]{1,2,3,0:T(8,128)S(1)} fusion(bf16[24,11,128,128]{3,2,1,0:T(8,128)(2,1)} %param.5, bf16[24,11,128,128]{3,2,1,0:T(8,128)(2,1)} %bitcast.73), kind=kOutput, calls=%fused_computation.72 | convolution fusion | flops 1107296256 | bytes 18874368 | tf_op jit(solution)/shard_map/bnij,bnjw->biw/dot_general | solution.py:67
  109.7 0.4 fusion.5
  110.1 2.2 collective-permute-start.6
  112.3 2.6 collective-permute-start.7
  115.0 2.5 collective-permute-start.8
  117.5 1.3 collective-permute-start.9
  118.8 1.3 collective-permute-start.10
  120.1 56.7 %collective-permute-done.6 = bf16[3072,128]{1,0:T(8,128)(2,1)S(1)} collective-permute-done((bf16[3072,128]{1,0:T(8,128)(2,1)S(1)}, bf16[3072,128]{1,0:T(8,128)(2,1)S(1)}, u32[]{:S(2)}, u32[]{:S(2)}) %collective-permute-start.6) | collective-permute-done | bytes 786464 | tf_op jit(solution)/shard_map/ppermute | solution.py:15
  176.8 1.3 collective-permute-start.11
  178.0 0.1 constant_dynamic-update-slice_fusion.6
  178.2 0.2 constant_dynamic-update-slice_fusion.5
  178.4 0.2 constant_dynamic-update-slice_fusion.4
  178.6 0.2 constant_dynamic-update-slice_fusion.3
  178.8 2.2 collective-permute-done.9
  181.0 0.2 constant_dynamic-update-slice_fusion.2
  181.2 0.2 constant_dynamic-update-slice_fusion.1
  181.4 15.8 %collective-permute-done.11 = bf16[3072,128]{1,0:T(8,128)(2,1)S(1)} collective-permute-done((bf16[3072,128]{1,0:T(8,128)(2,1)S(1)}, bf16[3072,128]{1,0:T(8,128)(2,1)S(1)}, u32[]{:S(2)}, u32[]{:S(2)}) %collective-permute-start.11) | collective-permute-done | bytes 786464 | tf_op jit(solution)/shard_map/ppermute | solution.py:15
  197.2 0.2 constant_dynamic-update-slice_fusion
  197.4 2.4 copy-done.2
  199.8 1.7 convolution_convert_fusion.1
  201.5 0.0 all-gather.5.cloned.1.call-update
  201.5 0.1 convert_reduce_fusion.2
  201.6 3.7 %multiply_reduce_fusion = bf16[896]{0:T(1024)(128)(2,1)S(1)} fusion(bf16[3072,896]{1,0:T(8,128)(2,1)} %copy-done.2), kind=kLoop, calls=%fused_computation.3 | loop fusion | flops 8256640 | bytes 5506816 | tf_op jit(solution)/shard_map/reduce_sum | solution.py:93
  205.4 20.6 %all-gather.2 = bf16[16,1,896]{2,1,0:T(2,128)(2,1)S(1)} all-gather(bf16[1,1,896]{2,1,0:T(2,128)(2,1)S(1)} %reshape.124), channel_id=3, replica_groups=mesh['row'=16,'cuts'=16] {'row'}, dimensions={0}, use_global_device_ids=true | all-gather | bytes 30464 | tf_op jit(solution)/shard_map/all_gather | solution.py:33
  226.0 0.1 convert_reduce_fusion.1
  226.1 20.5 %all-gather.5.cloned.1.call-done = bf16[2048,896]{1,0:T(8,128)(2,1)} async-done(((bf16[128,896]{1,0:T(8,128)(2,1)}), bf16[2048,896]{1,0:T(8,128)(2,1)}) %all-gather.5.cloned.1.call-update) | async-done | bytes 3670032 | tf_op jit(solution)/shard_map/all_gather | solution.py:33
  246.6 2.6 convert_reduce_fusion
  249.2 0.0 copy-start.1
  249.2 4.4 %convolution_convert_fusion = bf16[3072,128]{1,0:T(8,128)(2,1)S(1)} fusion(bf16[3072,896]{1,0:T(8,128)(2,1)} %copy-done.2, f32[128,896]{1,0:T(8,128)S(1)} %convert_reduce_fusion, f32[896]{0:T(1024)S(1)} %add_rsqrt_fusion, f32[128]{0:T(128)S(1)} %slice.27, s32[896]{0:T(1024)S(1)} %iota_add_fusion, s32[896]{0:T(1024)S(1)} %convert_reduce_fusion.2, ...), kind=kOutput, calls=%fused_computation.5 | convolution fusion | flops 706527232 | bytes 6763392 | tf_op jit(solution)/shard_map/dot_general | solution.py:105
  253.7 19.6 %all_to_all.38 = bf16[16,192,128]{2,1,0:T(8,128)(2,1)S(1)} all-to-all(bf16[16,192,128]{2,1,0:T(8,128)(2,1)S(1)} %bitcast.79), channel_id=1, replica_groups=mesh['row'=16,'cuts'=16] {'cuts'}, dimensions={0} | all-to-all | bytes 1572864 | tf_op jit(solution)/shard_map/all_to_all | solution.py:108
  273.3 1.0 copy_bitcast_fusion
  (22 shorter events, 0.2 us)
Async XLA Ops:
  6.5 1.1 copy-start
  6.5 25.9 %copy-start.5 = (s32[12]{0:T(128)S(1)}, s32[12]{0:T(128)}, u32[]{:S(2)}) copy-start(s32[12]{0:T(128)} %param.8) | copy-start | bytes 148
  8.8 19.6 %all-to-all-start = ((bf16[192,16,128]{2,0,1:T(8,128)(2,1)}), bf16[192,16,128]{2,0,1:T(8,128)(2,1)S(1)}, u32[]{:S(2)}, u32[]{:S(2)}) async-start(bf16[192,16,128]{2,0,1:T(8,128)(2,1)} %copy_bitcast_fusion.1), calls=%async_computation | async-start | bytes 1572864 | tf_op jit(solution)/shard_map/all_to_all | solution.py:45
  15.5 231.1 %all-gather.5.cloned.1.call-start = ((), (), s32[]{:S(2)}) async-start(), calls=%async_computation.2 | async-start | bytes 3899392 | tf_op jit(solution)/shard_map/all_gather | solution.py:33
  28.4 7.4 %collective-permute-start = (bf16[1024,128]{1,0:T(8,128)(2,1)S(1)}, bf16[1024,128]{1,0:T(8,128)(2,1)S(1)}, u32[]{:S(2)}, u32[]{:S(2)}) collective-permute-start(bf16[1024,128]{1,0:T(8,128)(2,1)S(1)} %get-tuple-element.9), channel_id=1, source_target_pairs={{0,16},{16,32},{32,48},{48,64},{64,80},{80,96},{96,112},{112,128},... | collective-permute-start | bytes 786440 | tf_op jit(solution)/shard_map/ppermute | solution.py:24
  32.5 5.8 %collective-permute-start.1 = (bf16[1024,128]{1,0:T(8,128)(2,1)S(1)}, bf16[1024,128]{1,0:T(8,128)(2,1)S(1)}, u32[]{:S(2)}, u32[]{:S(2)}) collective-permute-start(bf16[1024,128]{1,0:T(8,128)(2,1)S(1)} %get-tuple-element.10), channel_id=1, source_target_pairs={{16,0},{32,16},{48,32},{64,48},{80,64},{96,80},{112,96},{128,112},... | collective-permute-start | bytes 786440 | tf_op jit(solution)/shard_map/ppermute | solution.py:27
  57.2 3.3 %collective-permute-start.2 = (bf16[1024,128]{1,0:T(8,128)(2,1)S(1)}, bf16[1024,128]{1,0:T(8,128)(2,1)S(1)}, u32[]{:S(2)}, u32[]{:S(2)}) collective-permute-start(bf16[1024,128]{1,0:T(8,128)(2,1)S(1)} %get-tuple-element.7), channel_id=1, source_target_pairs={{0,16},{16,32},{32,48},{48,64},{64,80},{80,96},{96,112},{112,128},... | collective-permute-start | bytes 786440 | tf_op jit(solution)/shard_map/ppermute | solution.py:24
  57.2 6.1 %collective-permute-start.3 = (bf16[1024,128]{1,0:T(8,128)(2,1)S(1)}, bf16[1024,128]{1,0:T(8,128)(2,1)S(1)}, u32[]{:S(2)}, u32[]{:S(2)}) collective-permute-start(bf16[1024,128]{1,0:T(8,128)(2,1)S(1)} %get-tuple-element.8), channel_id=1, source_target_pairs={{16,0},{32,16},{48,32},{64,48},{80,64},{96,80},{112,96},{128,112},... | collective-permute-start | bytes 786440 | tf_op jit(solution)/shard_map/ppermute | solution.py:27
  82.3 8.6 %copy-start.3 = (bf16[3072,128]{1,0:T(8,128)(2,1)}, bf16[3072,128]{1,0:T(8,128)(2,1)S(1)}, u32[]{:S(2)}) copy-start(bf16[3072,128]{1,0:T(8,128)(2,1)S(1)} %fusion.2) | copy-start | bytes 2359300
  82.4 3.3 %collective-permute-start.4 = (bf16[1024,128]{1,0:T(8,128)(2,1)S(1)}, bf16[1024,128]{1,0:T(8,128)(2,1)S(1)}, u32[]{:S(2)}, u32[]{:S(2)}) collective-permute-start(bf16[1024,128]{1,0:T(8,128)(2,1)S(1)} %get-tuple-element.5), channel_id=1, source_target_pairs={{0,16},{16,32},{32,48},{48,64},{64,80},{80,96},{96,112},{112,128},... | collective-permute-start | bytes 786440 | tf_op jit(solution)/shard_map/ppermute | solution.py:24
  82.4 8.5 %collective-permute-start.5 = (bf16[1024,128]{1,0:T(8,128)(2,1)S(1)}, bf16[1024,128]{1,0:T(8,128)(2,1)S(1)}, u32[]{:S(2)}, u32[]{:S(2)}) collective-permute-start(bf16[1024,128]{1,0:T(8,128)(2,1)S(1)} %get-tuple-element.6), channel_id=1, source_target_pairs={{16,0},{32,16},{48,32},{64,48},{80,64},{96,80},{112,96},{128,112},... | collective-permute-start | bytes 786440 | tf_op jit(solution)/shard_map/ppermute | solution.py:27
  101.3 8.4 %copy-start.4 = (bf16[3072,128]{1,0:T(8,128)(2,1)S(1)}, bf16[3072,128]{1,0:T(8,128)(2,1)}, u32[]{:S(2)}) copy-start(bf16[3072,128]{1,0:T(8,128)(2,1)} %copy-done.3) | copy-start | bytes 2359300
  110.1 66.6 %collective-permute-start.6 = (bf16[3072,128]{1,0:T(8,128)(2,1)S(1)}, bf16[3072,128]{1,0:T(8,128)(2,1)S(1)}, u32[]{:S(2)}, u32[]{:S(2)}) collective-permute-start(bf16[3072,128]{1,0:T(8,128)(2,1)S(1)} %fusion.5), channel_id=1, source_target_pairs={{0,3},{1,4},{2,5},{3,6},{4,7},{5,8},{6,9},{7,10},{8,11},{9,12},{10... | collective-permute-start | bytes 2359304 | tf_op jit(solution)/shard_map/ppermute | solution.py:15
  112.3 65.9 %collective-permute-start.7 = (bf16[3072,128]{1,0:T(8,128)(2,1)S(1)}, bf16[3072,128]{1,0:T(8,128)(2,1)S(1)}, u32[]{:S(2)}, u32[]{:S(2)}) collective-permute-start(bf16[3072,128]{1,0:T(8,128)(2,1)S(1)} %fusion.5), channel_id=1, source_target_pairs={{0,2},{1,3},{2,4},{3,5},{4,6},{5,7},{6,8},{7,9},{8,10},{9,11},{10,... | collective-permute-start | bytes 2359304 | tf_op jit(solution)/shard_map/ppermute | solution.py:15
  115.0 63.4 %collective-permute-start.8 = (bf16[3072,128]{1,0:T(8,128)(2,1)S(1)}, bf16[3072,128]{1,0:T(8,128)(2,1)S(1)}, u32[]{:S(2)}, u32[]{:S(2)}) collective-permute-start(bf16[3072,128]{1,0:T(8,128)(2,1)S(1)} %fusion.5), channel_id=1, source_target_pairs={{0,1},{1,2},{2,3},{3,4},{4,5},{5,6},{6,7},{7,8},{8,9},{9,10},{10,1... | collective-permute-start | bytes 2359304 | tf_op jit(solution)/shard_map/ppermute | solution.py:15
  117.5 63.5 %collective-permute-start.9 = (bf16[3072,128]{1,0:T(8,128)(2,1)S(1)}, bf16[3072,128]{1,0:T(8,128)(2,1)S(1)}, u32[]{:S(2)}, u32[]{:S(2)}) collective-permute-start(bf16[3072,128]{1,0:T(8,128)(2,1)S(1)} %fusion.5), channel_id=1, source_target_pairs={{1,0},{2,1},{3,2},{4,3},{5,4},{6,5},{7,6},{8,7},{9,8},{10,9},{11,1... | collective-permute-start | bytes 2359304 | tf_op jit(solution)/shard_map/ppermute | solution.py:15
  118.8 62.4 %collective-permute-start.10 = (bf16[3072,128]{1,0:T(8,128)(2,1)S(1)}, bf16[3072,128]{1,0:T(8,128)(2,1)S(1)}, u32[]{:S(2)}, u32[]{:S(2)}) collective-permute-start(bf16[3072,128]{1,0:T(8,128)(2,1)S(1)} %fusion.5), channel_id=1, source_target_pairs={{2,0},{3,1},{4,2},{5,3},{6,4},{7,5},{8,6},{9,7},{10,8},{11,9},{12,... | collective-permute-start | bytes 2359304 | tf_op jit(solution)/shard_map/ppermute | solution.py:15
  176.8 20.4 %collective-permute-start.11 = (bf16[3072,128]{1,0:T(8,128)(2,1)S(1)}, bf16[3072,128]{1,0:T(8,128)(2,1)S(1)}, u32[]{:S(2)}, u32[]{:S(2)}) collective-permute-start(bf16[3072,128]{1,0:T(8,128)(2,1)S(1)} %fusion.5), channel_id=1, source_target_pairs={{3,0},{4,1},{5,2},{6,3},{7,4},{8,5},{9,6},{10,7},{11,8},{12,9},{13... | collective-permute-start | bytes 2359304 | tf_op jit(solution)/shard_map/ppermute | solution.py:15
  197.3 2.4 copy-start.2
  249.2 25.1 %copy-start.1 = (bf16[192,2048]{1,0:T(8,128)(2,1)S(1)}, bf16[192,2048]{1,0:T(8,128)(2,1)}, u32[]{:S(2)}) copy-start(bf16[192,2048]{1,0:T(8,128)(2,1)} %param.9) | copy-start | bytes 2359300
Sparse Core Ops, SparseCore 0:
  201.6 44.9 all-gather.4
where the time goes:
time: 283 us; the launch traced here: 281 us
  waiting for transfers between devices  125 us (44%)
  blocking collectives  40.3 us (14%)
  local copies, waits for them, and re-layouts  37.9 us (13%)
  matrix products  31.4 us (11%)
  starting transfers between devices  23.1 us (8%)
  between operations  13.7 us (5%)
  other arithmetic  9.49 us (3%)
    ppermute x6, waiting for transfers between devices, passed_along(): return lax.ppermute(block, axis, route)  74.7 us
    gather x3, local copies, waits for them, and re-layouts, apply_ham(): picked = stacked[position]  30.7 us
    dot_general x3, matrix products, apply_ham(): jnp.einsum('bnij,bnjw->biw', ham_blocks, picked, preferred_element_type=j...  25 us
    all_gather x1, blocking collectives, total_of_pieces(): return lax.all_gather(array, axis).astype(jnp.float32).sum(0)  20.6 us
    all_gather x1, waiting for transfers between devices, total_of_pieces(): return lax.all_gather(array, axis).astype(jnp.float32).sum(0)  20.5 us
    all_to_all x1, blocking collectives, body(): lax.all_to_all(corrected, 'cuts', split_axis=0, concat_axis=1, tiled=True)  19.6 us
    ppermute x6, starting transfers between devices, passed_along(): return lax.ppermute(block, axis, route)  11.2 us
    all_to_all x1, waiting for transfers between devices, body(): lax.all_to_all(start_vectors, 'cuts', split_axis=1, concat_axis=0, tiled=...  10.9 us
  transfers between devices with their start and end apart: 14, of which 11 were waited for; matrix products, arithmetic and copies ran while one was open for 2% of the time, Pallas kernels for 0%

commit v1 on v0

v1 whole, which is shorter than its diff:
```python
import functools

import jax
import jax.numpy as jnp
from jax import lax
from jax.experimental import pallas as pl
from jax.experimental.pallas import tpu as pltpu
from jax.sharding import PartitionSpec as P

HB = 8
BS = 128
NINT = 8
TILE = 128
PAIRS = 42
HALF = PAIRS // 2
REACH = 3
VMEM = pltpu.VMEM
SMEM = pltpu.SMEM


def vmem_spec():
    return pl.BlockSpec(memory_space=VMEM)


def smem_spec():
    return pl.BlockSpec(memory_space=SMEM)


def apply_kernel(scale, pos_ref, centre_ref, ham_ref, stack_ref, prev_ref, out_ref):
    blocks, slots = ham_ref.shape[:2]
    centre = centre_ref[0]

    def tile_at(b, n):
        start = pl.multiple_of(pos_ref[b, n] * BS, BS)
        return stack_ref[pl.ds(start, BS), :]

    def one_block(b, _):
        total = jnp.zeros((BS, TILE), jnp.float32)
        for n in range(0, slots, 2):
            if n + 1 < slots:
                left = jnp.concatenate([ham_ref[b, n], ham_ref[b, n + 1]], axis=1)
                right = jnp.concatenate([tile_at(b, n), tile_at(b, n + 1)], axis=0)
            else:
                left = ham_ref[b, n]
                right = tile_at(b, n)
            total += jnp.dot(left, right, preferred_element_type=jnp.float32)
        here = pl.ds(pl.multiple_of(b * BS, BS), BS)
        own = stack_ref[pl.ds(pl.multiple_of((b + HB) * BS, BS), BS), :].astype(jnp.float32)
        value = total - centre * own
        if scale != 1:
            value = scale * value - prev_ref[here, :].astype(jnp.float32)
        out_ref[here, :] = value.astype(jnp.bfloat16)
        return 0

    lax.fori_loop(0, blocks, one_block, 0)


def gram_kernel(table_ref, field_ref, keep_ref, send_ref, turned_ref):
    tiles = field_ref.shape[0]
    mine = table_ref[PAIRS + 1] * HALF
    for t in range(tiles):
        turned_ref[t] = field_ref[t].T

    def one_pair(m, _):
        def block(at):
            code = table_ref[at]
            low = code // 4
            return jnp.dot(
                turned_ref[low], field_ref[low + code % 4], preferred_element_type=jnp.float32
            )

        keep_ref[m] = block(mine + m)
        send_ref[m] = block(HALF - mine + m).astype(jnp.bfloat16)
        return 0

    lax.fori_loop(0, HALF, one_pair, 0)


def correct_kernel(rows_all, table_ref, field_ref, mine_ref, other_ref, out_ref, total_ref, row_ref, col_ref):
    tiles = field_ref.shape[0]
    count = table_ref[PAIRS]
    mine = table_ref[PAIRS + 1]
    at_row = lax.broadcasted_iota(jnp.int32, (TILE, TILE), 0)
    at_col = lax.broadcasted_iota(jnp.int32, (TILE, TILE), 1)
    eye = (at_row == at_col).astype(jnp.float32)

    def load(ref, m):
        return ref[m].astype(jnp.float32)

    def each(m, act):
        half = m // HALF
        index = m - half * HALF

        @pl.when(half == mine)
        def _():
            act(load(mine_ref, index))

        @pl.when(half != mine)
        def _():
            act(load(other_ref, index))

    total_ref[...] = jnp.zeros_like(total_ref)

    def norms(m, _):
        code = table_ref[m]
        low = code // 4

        @pl.when(code % 4 == 0)
        def _():
            def act(block):
                diagonal = block * eye
                across = jnp.sum(diagonal, axis=0, keepdims=True)
                down = jnp.sum(diagonal, axis=1, keepdims=True)
                row_ref[low] = jnp.broadcast_to(lax.rsqrt(across / rows_all + 1e-05), (8, TILE))
                col_ref[low] = jnp.broadcast_to(lax.rsqrt(down / rows_all + 1e-05), (TILE, TILE))

            each(m, act)

        return 0

    lax.fori_loop(0, count, norms, 0)

    def one_pair(m, _):
        code = table_ref[m]
        low = code // 4
        step = code % 4
        high = low + step

        def act(block):
            down = col_ref[low]
            across = row_ref[high][:1]
            normed = block * down * across / rows_all
            same = (step == 0).astype(jnp.float32)
            coefficient = 1.5 * (eye * same) - 0.5 * normed
            forward = (down * coefficient).astype(jnp.bfloat16)
            total_ref[high] += jnp.dot(field_ref[low], forward, preferred_element_type=jnp.float32)

            @pl.when(step != 0)
            def _():
                backward = (across * coefficient).astype(jnp.bfloat16)
                total_ref[low] += lax.dot_general(
                    field_ref[high],
                    backward,
                    (((1,), (1,)), ((), ())),
                    preferred_element_type=jnp.float32,
                )

        each(m, act)
        return 0

    lax.fori_loop(0, count, one_pair, 0)
    for t in range(tiles):
        out_ref[:, t * TILE : (t + 1) * TILE] = total_ref[t].astype(jnp.bfloat16)


def shift(array, distance):
    size = lax.axis_size("row")
    return lax.ppermute(array, "row", [(i, (i + distance) % size) for i in range(size)])


def exchange(array, bit):
    return lax.ppermute(array, "row", [(i, i ^ bit) for i in range(lax.axis_size("row"))])


def body(ham_blocks, neighbors, slice_widths, interval_index, start_vectors):
    rows_mine, columns = start_vectors.shape
    tiles = columns // TILE
    blocks, slots = ham_blocks.shape[:2]
    row_count = lax.axis_size("row")
    rows_all = blocks * BS * row_count
    panel = lax.all_to_all(start_vectors, "cuts", split_axis=1, concat_axis=0, tiled=True)

    first_block = lax.axis_index("row") * blocks
    position = jnp.mod(neighbors - first_block + HB, blocks * row_count)
    core = lax.axis_index("row") % 2
    ends = jnp.cumsum(slice_widths) // TILE
    tile = jnp.arange(tiles, dtype=jnp.int32)
    slice_of = jnp.sum((tile[:, None] >= ends[None, :]).astype(jnp.int32), axis=1)
    own_slice = jnp.sum(jnp.where(tile == lax.axis_index("cuts"), slice_of, 0))
    at_slice = jnp.arange(slice_widths.shape[0], dtype=jnp.int32)
    interval = jnp.sum(jnp.where(at_slice == own_slice, interval_index, 0))
    centre = (-0.5 + interval.astype(jnp.float32) / (NINT - 1)).reshape(1)

    code = jnp.arange(tiles * 4, dtype=jnp.int32)
    low, step = code // 4, code % 4
    def slice_at(index):
        return jnp.sum((index[:, None] * TILE >= (ends * TILE)[None, :]).astype(jnp.int32), axis=1)
    valid = (low + step < tiles) & (slice_at(low + step) - slice_at(low) <= 1)
    rank = jnp.sum((valid[None, :] & (code[None, :] < code[:, None])).astype(jnp.int32), axis=1)
    places = jnp.arange(PAIRS, dtype=jnp.int32)
    listed = jnp.sum(
        jnp.where(valid[None, :] & (rank[None, :] == places[:, None]), code[None, :], 0), axis=1
    )
    table = jnp.concatenate(
        [listed, jnp.sum(valid.astype(jnp.int32)).reshape(1), core.reshape(1)]
    ).astype(jnp.int32)

    def apply_ham(scale, field, before):
        width = HB * BS
        low_side = shift(field[-width:], 1)
        high_side = shift(field[:width], -1)
        stack = jnp.concatenate([low_side, field, high_side], axis=0)
        return pl.pallas_call(
            functools.partial(apply_kernel, scale),
            out_shape=jax.ShapeDtypeStruct(field.shape, jnp.bfloat16),
            in_specs=[smem_spec(), smem_spec(), vmem_spec(), vmem_spec(), vmem_spec()],
            out_specs=vmem_spec(),
        )(position, centre, ham_blocks, stack, before)

    first = apply_ham(1, panel, panel)
    second = apply_ham(2, first, panel)
    filtered = apply_ham(2, second, first)

    field = lax.all_to_all(filtered.reshape(tiles, rows_mine, TILE), "cuts", 0, 0)
    kept, sent = pl.pallas_call(
        gram_kernel,
        out_shape=(
            jax.ShapeDtypeStruct((HALF, TILE, TILE), jnp.float32),
            jax.ShapeDtypeStruct((HALF, TILE, TILE), jnp.bfloat16),
        ),
        in_specs=[smem_spec(), vmem_spec()],
        out_specs=(vmem_spec(), vmem_spec()),
        scratch_shapes=[VMEM((tiles, TILE, rows_mine), jnp.bfloat16)],
    )(table, field)
    partial = (kept + exchange(sent, 1).astype(jnp.float32)).astype(jnp.bfloat16)
    cut_count = lax.axis_size("cuts")
    share = HALF * TILE // cut_count
    pieces = lax.all_to_all(partial.reshape(cut_count, share, TILE), "cuts", 0, 0)
    total = jnp.sum(pieces.astype(jnp.float32), axis=0)
    bit = 2
    while bit < row_count:
        rounded = total.astype(jnp.bfloat16)
        total = rounded.astype(jnp.float32) + exchange(rounded, bit).astype(jnp.float32)
        bit *= 2
    spread = jnp.broadcast_to(total.astype(jnp.bfloat16)[None], (cut_count, share, TILE))
    mine = lax.all_to_all(spread, "cuts", 0, 0).reshape(HALF, TILE, TILE)
    other = exchange(mine, 1)
    return pl.pallas_call(
        functools.partial(correct_kernel, rows_all),
        out_shape=jax.ShapeDtypeStruct((rows_mine, columns), jnp.bfloat16),
        in_specs=[smem_spec(), vmem_spec(), vmem_spec(), vmem_spec()],
        out_specs=vmem_spec(),
        scratch_shapes=[
            VMEM((tiles, rows_mine, TILE), jnp.float32),
            VMEM((tiles, 8, TILE), jnp.float32),
            VMEM((tiles, TILE, TILE), jnp.float32),
        ],
    )(table, field, mine, other)


def solution(mesh):
    return jax.shard_map(
        body,
        mesh=mesh,
        in_specs=(P("row", None, None, None), P("row", None), P(), P(), P(("row", "cuts"), None)),
        out_specs=P(("row", "cuts"), None),
        check_vma=False,
    )
```

time: 283 us -> 184 us (0.65)
  waiting for transfers between devices: 125 us -> 49.1 us
  Pallas kernels: 0 us -> 55.9 us
  local copies, waits for them, and re-layouts: 37.9 us -> 6.48 us
  matrix products: 31.4 us -> 0 us
  between operations: 13.7 us -> 0.75 us
  blocking collectives: 40.3 us -> 28.7 us
  starting transfers between devices: 23.1 us -> 31.3 us
    ppermute x12 -> x11, waiting for transfers between devices: 93.8 us -> 28.5 us  [the longest x6 16.8 us: shift(): lax.ppermute(array, 'row', [(i, (i + distance) % size) for i in range(siz...]
    pallas_call x0 -> x5, Pallas kernels: none -> 55.9 us  [the longest x3 33.6 us: apply_ham(): pl.pallas_call(functools.partial(apply_kernel, scale), out_shape=jax.Shap...]
    dot_general x6 -> x0, matrix products: 31.4 us -> none  [the longest x3 25 us: apply_ham(): jnp.einsum('bnij,bnjw->biw', ham_blocks, picked, preferred_element_type=j...]
    gather x3 -> x0, local copies, waits for them, and re-layouts: 30.7 us -> none  [apply_ham(): picked = stacked[position]]
    all_gather x1 -> x0, blocking collectives: 20.6 us -> none  [total_of_pieces(): return lax.all_gather(array, axis).astype(jnp.float32).sum(0)]
    all_gather x1 -> x0, waiting for transfers between devices: 20.5 us -> none  [total_of_pieces(): return lax.all_gather(array, axis).astype(jnp.float32).sum(0)]
    all_to_all x1 -> x2, blocking collectives: 19.6 us -> 28.7 us  [the longest x1 15.6 us: body(): lax.all_to_all(partial.reshape(cut_count, share, TILE), 'cuts', 0, 0)]
    all_to_all x0 -> x1, waiting for transfers between devices: none -> 8.73 us  [body(): lax.all_to_all(filtered.reshape(tiles, rows_mine, TILE), 'cuts', 0, 0)]
  transfers between devices with their start and end apart: 14 -> 13, of which waited for: 11 -> 13; matrix products, arithmetic and copies ran while one was open for 2% -> 3% of each run, Pallas kernels for 0% -> 0%
where the time goes in v1:
time: 184 us; the launch traced here: 183 us
  Pallas kernels  55.9 us (30%)
  waiting for transfers between devices  49.1 us (27%)
  starting transfers between devices  31.3 us (17%)
  blocking collectives  28.7 us (16%)
  other arithmetic  10.3 us (6%)
  local copies, waits for them, and re-layouts  6.48 us (4%)
    pallas_call x3, Pallas kernels, apply_ham(): pl.pallas_call(functools.partial(apply_kernel, scale), out_shape=jax.Shap...  33.6 us
    ppermute x6, waiting for transfers between devices, shift(): lax.ppermute(array, 'row', [(i, (i + distance) % size) for i in range(siz...  16.8 us
    ppermute x5, starting transfers between devices, exchange(): lax.ppermute(array, 'row', [(i, i ^ bit) for i in range(lax.axis_size('ro...  15.7 us
    all_to_all x1, blocking collectives, body(): lax.all_to_all(partial.reshape(cut_count, share, TILE), 'cuts', 0, 0)  15.6 us
    pallas_call x1, Pallas kernels, body(): pl.pallas_call(functools.partial(correct_kernel, rows_all), out_shape=jax...  15.5 us
    all_to_all x1, blocking collectives, body(): mine = lax.all_to_all(spread, 'cuts', 0, 0).reshape(HALF, TILE, TILE)  13.1 us
    all_to_all x1, waiting for transfers between devices, body(): lax.all_to_all(start_vectors, 'cuts', split_axis=1, concat_axis=0, tiled=...  11.8 us
    ppermute x5, waiting for transfers between devices, exchange(): lax.ppermute(array, 'row', [(i, i ^ bit) for i in range(lax.axis_size('ro...  11.7 us
  transfers between devices with their start and end apart: 13, of which 13 were waited for; matrix products, arithmetic and copies ran while one was open for 3% of the time, Pallas kernels for 0%

profile of v1, /device:TPU:33, one launch (start us, length us, event | category | flops | bytes accessed | tf_op | source)
XLA Modules:
  0.0 182.6 jit_solution(761487137910287528)
XLA Ops:
  0.0 0.0 copy-start
  0.0 1.1 copy-done
  1.1 1.1 copy_bitcast_fusion
  2.2 6.9 %all-to-all-start = ((bf16[192,16,128]{2,0,1:T(8,128)(2,1)}), bf16[192,16,128]{2,0,1:T(8,128)(2,1)S(1)}, u32[]{:S(2)}, u32[]{:S(2)}) async-start(bf16[192,16,128]{2,0,1:T(8,128)(2,1)} %copy_bitcast_fusion), calls=%async_computation | async-start | bytes 1572864 | tf_op jit(solution)/shard_map/all_to_all | solution.py:171
  9.1 0.0 copy-done.8
  9.1 0.2 reduce-window.7
  9.3 0.1 convert_reduce_fusion.1
  9.4 0.7 fusion.3
  10.1 11.8 %all-to-all-done = bf16[192,16,128]{2,0,1:T(8,128)(2,1)S(1)} async-done(((bf16[192,16,128]{2,0,1:T(8,128)(2,1)}), bf16[192,16,128]{2,0,1:T(8,128)(2,1)S(1)}, u32[]{:S(2)}, u32[]{:S(2)}) %all-to-all-start) | async-done | bytes 786464 | tf_op jit(solution)/shard_map/all_to_all | solution.py:171
  22.0 4.1 %collective-permute-start = (bf16[1024,128]{1,0:T(8,128)(2,1)S(1)}, bf16[1024,128]{1,0:T(8,128)(2,1)S(1)}, u32[]{:S(2)}, u32[]{:S(2)}) collective-permute-start(bf16[1024,128]{1,0:T(8,128)(2,1)S(1)} %get-tuple-element.19), channel_id=1, source_target_pairs={{0,16},{16,32},{32,48},{48,64},{64,80},{80,96},{96,112},{112,128},... | collective-permute-start | bytes 786440 | tf_op jit(solution)/shard_map/ppermute | solution.py:158
  26.1 0.0 collective-permute-start.1
  26.1 0.0 copy-done.9
  26.1 1.2 fusion.4
  27.9 0.0 copy-done.7
  28.0 0.1 copy.8
  28.0 0.6 add_select_fusion.pos_ref
  28.6 0.7 collective-permute-done
  29.4 2.5 %collective-permute-done.1 = bf16[1024,128]{1,0:T(8,128)(2,1)S(1)} collective-permute-done((bf16[1024,128]{1,0:T(8,128)(2,1)S(1)}, bf16[1024,128]{1,0:T(8,128)(2,1)S(1)}, u32[]{:S(2)}, u32[]{:S(2)}) %collective-permute-start.1) | collective-permute-done | bytes 262176 | tf_op jit(solution)/shard_map/ppermute | solution.py:158
  31.9 1.1 pad_maximum_fusion.stack_ref
  33.0 0.0 copy-done.1
  33.0 11.2 %shard_map.55.prev_ref = bf16[3072,128]{1,0:T(8,128)(2,1)} custom-call(s32[24,11]{1,0:T(8,128)} %add_select_fusion.pos_ref, f32[1]{0:T(128)} %bitcast.4.centre_ref, bf16[24,11,128,128]{3,2,1,0:T(8,128)(2,1)} %ham_ref.5, bf16[5120,128]{1,0:T(8,128)(2,1)} %pad_maximum_fusion.stack_ref, bf16[3072,128]{1,0:T(8,128)(2,1)} %bitcast.26), custom_call_target="tpu_custom_call" | custom-call | tf_op jit(solution)/shard_map/pallas_call | solution.py:203
  44.2 1.1 fusion.6
  45.3 0.0 collective-permute-start.2
  45.4 0.5 collective-permute-start.3
  45.9 2.8 %collective-permute-done.2 = bf16[1024,128]{1,0:T(8,128)(2,1)S(1)} collective-permute-done((bf16[1024,128]{1,0:T(8,128)(2,1)S(1)}, bf16[1024,128]{1,0:T(8,128)(2,1)S(1)}, u32[]{:S(2)}, u32[]{:S(2)}) %collective-permute-start.2) | collective-permute-done | bytes 262176 | tf_op jit(solution)/shard_map/ppermute | solution.py:158
  48.7 2.8 %collective-permute-done.3 = bf16[1024,128]{1,0:T(8,128)(2,1)S(1)} collective-permute-done((bf16[1024,128]{1,0:T(8,128)(2,1)S(1)}, bf16[1024,128]{1,0:T(8,128)(2,1)S(1)}, u32[]{:S(2)}, u32[]{:S(2)}) %collective-permute-start.3) | collective-permute-done | bytes 262176 | tf_op jit(solution)/shard_map/ppermute | solution.py:158
  51.4 0.0 copy-done.2
  51.4 1.1 pad_maximum_fusion.1.stack_ref
  52.6 11.2 %shard_map.56 = bf16[3072,128]{1,0:T(8,128)(2,1)} custom-call(s32[24,11]{1,0:T(8,128)} %add_select_fusion.pos_ref, f32[1]{0:T(128)} %bitcast.4.centre_ref, bf16[24,11,128,128]{3,2,1,0:T(8,128)(2,1)} %ham_ref.5, bf16[5120,128]{1,0:T(8,128)(2,1)} %pad_maximum_fusion.1.stack_ref, bf16[3072,128]{1,0:T(8,128)(2,1)} %bitcast.27), custom_call_target="tpu_custom_call" | custom-call | tf_op jit(solution)/shard_map/pallas_call | solution.py:203
  63.8 1.1 fusion.5
  64.9 0.0 collective-permute-start.4
  65.0 0.5 collective-permute-start.5
  65.5 2.8 %collective-permute-done.4 = bf16[1024,128]{1,0:T(8,128)(2,1)S(1)} collective-permute-done((bf16[1024,128]{1,0:T(8,128)(2,1)S(1)}, bf16[1024,128]{1,0:T(8,128)(2,1)S(1)}, u32[]{:S(2)}, u32[]{:S(2)}) %collective-permute-start.4) | collective-permute-done | bytes 262176 | tf_op jit(solution)/shard_map/ppermute | solution.py:158
  68.3 5.2 %collective-permute-done.5 = bf16[1024,128]{1,0:T(8,128)(2,1)S(1)} collective-permute-done((bf16[1024,128]{1,0:T(8,128)(2,1)S(1)}, bf16[1024,128]{1,0:T(8,128)(2,1)S(1)}, u32[]{:S(2)}, u32[]{:S(2)}) %collective-permute-start.5) | collective-permute-done | bytes 262176 | tf_op jit(solution)/shard_map/ppermute | solution.py:158
  73.5 0.0 copy-done.4
  73.5 1.1 pad_maximum_fusion.2.stack_ref
  74.6 11.2 %shard_map.57 = bf16[3072,128]{1,0:T(8,128)(2,1)} custom-call(s32[24,11]{1,0:T(8,128)} %add_select_fusion.pos_ref, f32[1]{0:T(128)} %bitcast.4.centre_ref, bf16[24,11,128,128]{3,2,1,0:T(8,128)(2,1)} %ham_ref.5, bf16[5120,128]{1,0:T(8,128)(2,1)} %pad_maximum_fusion.2.stack_ref, bf16[3072,128]{1,0:T(8,128)(2,1)} %shard_map.55.prev_ref), custom_call_target="tpu_custom_call" | custom-call | tf_op jit(solution)/shard_map/pallas_call | solution.py:203
  85.8 3.6 %all-to-all-start.1 = ((bf16[16,192,128]{2,1,0:T(8,128)(2,1)}), bf16[16,192,128]{2,1,0:T(8,128)(2,1)S(1)}, u32[]{:S(2)}, u32[]{:S(2)}) async-start(bf16[16,192,128]{2,1,0:T(8,128)(2,1)} %bitcast.28), calls=%async_computation.1 | async-start | bytes 1572864 | tf_op jit(solution)/shard_map/all_to_all | solution.py:214
  89.5 0.1 convert_reduce_fusion.2
  89.5 0.7 convert_reduce_fusion.4
  90.3 0.1 convert_reduce_fusion
  90.4 0.1 select_reduce_fusion
  90.5 1.3 pad_add_fusion.table_ref
  91.8 8.7 %all-to-all-done.1.field_ref = bf16[16,192,128]{2,1,0:T(8,128)(2,1)S(1)} async-done(((bf16[16,192,128]{2,1,0:T(8,128)(2,1)}), bf16[16,192,128]{2,1,0:T(8,128)(2,1)S(1)}, u32[]{:S(2)}, u32[]{:S(2)}) %all-to-all-start.1) | async-done | bytes 786464 | tf_op jit(solution)/shard_map/all_to_all | solution.py:214
  100.5 0.9 copy-done.3
  101.4 6.8 %shard_map.58 = (f32[21,128,128]{2,1,0:T(8,128)}, bf16[21,128,128]{2,1,0:T(8,128)(2,1)}) custom-call(s32[44]{0:T(128)} %pad_add_fusion.table_ref, bf16[16,192,128]{2,1,0:T(8,128)(2,1)} %copy-done.3), custom_call_target="tpu_custom_call" | custom-call | tf_op jit(solution)/shard_map/pallas_call | solution.py:215
  108.3 0.0 collective-permute-start.6
  108.3 2.4 %collective-permute-done.6 = bf16[21,128,128]{2,1,0:T(8,128)(2,1)S(1)} collective-permute-done((bf16[21,128,128]{2,1,0:T(8,128)(2,1)}, bf16[21,128,128]{2,1,0:T(8,128)(2,1)S(1)}, u32[]{:S(2)}, u32[]{:S(2)}) %collective-permute-start.6) | collective-permute-done | bytes 688160 | tf_op jit(solution)/shard_map/ppermute | solution.py:162
  110.6 1.6 add_convert_fusion
  112.2 15.6 %all_to_all.34 = bf16[16,168,128]{2,1,0:T(8,128)(2,1)S(1)} all-to-all(bf16[16,168,128]{2,1,0:T(8,128)(2,1)S(1)} %bitcast.31), channel_id=1, replica_groups=mesh['row'=16,'cuts'=16] {'cuts'}, dimensions={0} | all-to-all | bytes 1376256 | tf_op jit(solution)/shard_map/all_to_all | solution.py:228
  127.8 0.1 reduce_sum.92
  127.9 1.4 collective-permute-start.7
  129.2 1.6 collective-permute-done.7
  130.9 6.3 %collective-permute-start.8 = (bf16[168,128]{1,0:T(8,128)(2,1)S(1)}, bf16[168,128]{1,0:T(8,128)(2,1)S(1)}, u32[]{:S(2)}, u32[]{:S(2)}) collective-permute-start(bf16[168,128]{1,0:T(8,128)(2,1)S(1)} %add_convert_fusion.3), channel_id=1, source_target_pairs={{0,64},{16,80},{32,96},{48,112},{64,0},{80,16},{96,32},{112,48},{1... | collective-permute-start | bytes 129032 | tf_op jit(solution)/shard_map/ppermute | solution.py:162
  137.1 1.4 collective-permute-done.8
  138.6 2.3 %collective-permute-start.9 = (bf16[168,128]{1,0:T(8,128)(2,1)S(1)}, bf16[168,128]{1,0:T(8,128)(2,1)S(1)}, u32[]{:S(2)}, u32[]{:S(2)}) collective-permute-start(bf16[168,128]{1,0:T(8,128)(2,1)S(1)} %add_convert_fusion.2), channel_id=1, source_target_pairs={{0,128},{16,144},{32,160},{48,176},{64,192},{80,208},{96,224},{112... | collective-permute-start | bytes 129032 | tf_op jit(solution)/shard_map/ppermute | solution.py:162
  140.8 4.6 %collective-permute-done.9 = bf16[168,128]{1,0:T(8,128)(2,1)S(1)} collective-permute-done((bf16[168,128]{1,0:T(8,128)(2,1)S(1)}, bf16[168,128]{1,0:T(8,128)(2,1)S(1)}, u32[]{:S(2)}, u32[]{:S(2)}) %collective-permute-start.9) | collective-permute-done | bytes 43040 | tf_op jit(solution)/shard_map/ppermute | solution.py:162
  145.5 0.1 broadcast_in_dim.19
  145.6 13.1 %all_to_all.35 = bf16[16,168,128]{2,1,0:T(8,128)(2,1)S(1)} all-to-all(bf16[16,168,128]{2,1,0:T(8,128)(2,1)S(1)} %broadcast_in_dim.19), channel_id=1, replica_groups=mesh['row'=16,'cuts'=16] {'cuts'}, dimensions={0} | all-to-all | bytes 1376256 | tf_op jit(solution)/shard_map/all_to_all | solution.py:236
  158.7 5.8 %collective-permute-start.10 = (bf16[21,128,128]{2,1,0:T(8,128)(2,1)S(1)}, bf16[21,128,128]{2,1,0:T(8,128)(2,1)S(1)}, u32[]{:S(2)}, u32[]{:S(2)}) collective-permute-start(bf16[21,128,128]{2,1,0:T(8,128)(2,1)S(1)} %bitcast.29), channel_id=1, source_target_pairs={{0,16},{16,0},{32,48},{48,32},{64,80},{80,64},{96,112},{112,96},{1... | collective-permute-start | bytes 2064392 | tf_op jit(solution)/shard_map/ppermute | solution.py:162
  164.5 1.8 collective-permute-done.10.other_ref
  166.2 0.0 copy-done.5
  166.3 0.8 copy-done.6
  167.1 15.5 %shard_map.59 = bf16[192,2048]{1,0:T(8,128)(2,1)} custom-call(s32[44]{0:T(128)} %pad_add_fusion.table_ref, bf16[16,192,128]{2,1,0:T(8,128)(2,1)} %copy-done.3, bf16[21,128,128]{2,1,0:T(8,128)(2,1)} %bitcast.30, bf16[21,128,128]{2,1,0:T(8,128)(2,1)} %copy-done.6), custom_call_target="tpu_custom_call" | custom-call | tf_op jit(solution)/shard_map/pallas_call | solution.py:238
  (15 shorter events, 0.1 us)
Async XLA Ops:
  0.0 1.1 copy-start
  0.0 9.1 %copy-start.8 = (s32[12]{0:T(128)S(1)}, s32[12]{0:T(128)}, u32[]{:S(2)}) copy-start(s32[12]{0:T(128)} %param.7) | copy-start | bytes 148
  2.2 23.9 %copy-start.9 = (s32[12]{0:T(128)S(1)}, s32[12]{0:T(128)}, u32[]{:S(2)}) copy-start(s32[12]{0:T(128)} %param.8) | copy-start | bytes 148
  2.2 25.7 %copy-start.7 = (s32[24,11]{0,1:T(8,128)S(1)}, s32[24,11]{0,1:T(8,128)}, u32[]{:S(2)}) copy-start(s32[24,11]{0,1:T(8,128)} %param.6) | copy-start | bytes 3172
  2.2 19.7 %all-to-all-start = ((bf16[192,16,128]{2,0,1:T(8,128)(2,1)}), bf16[192,16,128]{2,0,1:T(8,128)(2,1)S(1)}, u32[]{:S(2)}, u32[]{:S(2)}) async-start(bf16[192,16,128]{2,0,1:T(8,128)(2,1)} %copy_bitcast_fusion), calls=%async_computation | async-start | bytes 1572864 | tf_op jit(solution)/shard_map/all_to_all | solution.py:171
  21.9 11.1 %copy-start.1 = (bf16[192,16,128]{2,0,1:T(8,128)(2,1)}, bf16[192,16,128]{2,0,1:T(8,128)(2,1)S(1)}, u32[]{:S(2)}) copy-start(bf16[192,16,128]{2,0,1:T(8,128)(2,1)S(1)} %all-to-all-done) | copy-start | bytes 2359300
  22.0 7.4 %collective-permute-start = (bf16[1024,128]{1,0:T(8,128)(2,1)S(1)}, bf16[1024,128]{1,0:T(8,128)(2,1)S(1)}, u32[]{:S(2)}, u32[]{:S(2)}) collective-permute-start(bf16[1024,128]{1,0:T(8,128)(2,1)S(1)} %get-tuple-element.19), channel_id=1, source_target_pairs={{0,16},{16,32},{32,48},{48,64},{64,80},{80,96},{96,112},{112,128},... | collective-permute-start | bytes 786440 | tf_op jit(solution)/shard_map/ppermute | solution.py:158
  26.1 5.8 %collective-permute-start.1 = (bf16[1024,128]{1,0:T(8,128)(2,1)S(1)}, bf16[1024,128]{1,0:T(8,128)(2,1)S(1)}, u32[]{:S(2)}, u32[]{:S(2)}) collective-permute-start(bf16[1024,128]{1,0:T(8,128)(2,1)S(1)} %get-tuple-element.20), channel_id=1, source_target_pairs={{0,240},{16,0},{32,16},{48,32},{64,48},{80,64},{96,80},{112,96},{1... | collective-permute-start | bytes 786440 | tf_op jit(solution)/shard_map/ppermute | solution.py:158
  44.2 7.2 %copy-start.2 = (bf16[3072,128]{1,0:T(8,128)(2,1)S(1)}, bf16[3072,128]{1,0:T(8,128)(2,1)}, u32[]{:S(2)}) copy-start(bf16[3072,128]{1,0:T(8,128)(2,1)} %shard_map.55.prev_ref) | copy-start | bytes 2359300
  45.3 3.3 %collective-permute-start.2 = (bf16[1024,128]{1,0:T(8,128)(2,1)S(1)}, bf16[1024,128]{1,0:T(8,128)(2,1)S(1)}, u32[]{:S(2)}, u32[]{:S(2)}) collective-permute-start(bf16[1024,128]{1,0:T(8,128)(2,1)S(1)} %get-tuple-element.17), channel_id=1, source_target_pairs={{0,16},{16,32},{32,48},{48,64},{64,80},{80,96},{96,112},{112,128},... | collective-permute-start | bytes 786440 | tf_op jit(solution)/shard_map/ppermute | solution.py:158
  45.4 6.1 %collective-permute-start.3 = (bf16[1024,128]{1,0:T(8,128)(2,1)S(1)}, bf16[1024,128]{1,0:T(8,128)(2,1)S(1)}, u32[]{:S(2)}, u32[]{:S(2)}) collective-permute-start(bf16[1024,128]{1,0:T(8,128)(2,1)S(1)} %get-tuple-element.18), channel_id=1, source_target_pairs={{0,240},{16,0},{32,16},{48,32},{64,48},{80,64},{96,80},{112,96},{1... | collective-permute-start | bytes 786440 | tf_op jit(solution)/shard_map/ppermute | solution.py:158
  63.8 9.7 %copy-start.4 = (bf16[3072,128]{1,0:T(8,128)(2,1)S(1)}, bf16[3072,128]{1,0:T(8,128)(2,1)}, u32[]{:S(2)}) copy-start(bf16[3072,128]{1,0:T(8,128)(2,1)} %shard_map.56) | copy-start | bytes 2359300
  64.9 3.3 %collective-permute-start.4 = (bf16[1024,128]{1,0:T(8,128)(2,1)S(1)}, bf16[1024,128]{1,0:T(8,128)(2,1)S(1)}, u32[]{:S(2)}, u32[]{:S(2)}) collective-permute-start(bf16[1024,128]{1,0:T(8,128)(2,1)S(1)} %get-tuple-element.15), channel_id=1, source_target_pairs={{0,16},{16,32},{32,48},{48,64},{64,80},{80,96},{96,112},{112,128},... | collective-permute-start | bytes 786440 | tf_op jit(solution)/shard_map/ppermute | solution.py:158
  65.0 8.5 %collective-permute-start.5 = (bf16[1024,128]{1,0:T(8,128)(2,1)S(1)}, bf16[1024,128]{1,0:T(8,128)(2,1)S(1)}, u32[]{:S(2)}, u32[]{:S(2)}) collective-permute-start(bf16[1024,128]{1,0:T(8,128)(2,1)S(1)} %get-tuple-element.16), channel_id=1, source_target_pairs={{0,240},{16,0},{32,16},{48,32},{64,48},{80,64},{96,80},{112,96},{1... | collective-permute-start | bytes 786440 | tf_op jit(solution)/shard_map/ppermute | solution.py:158
  85.8 14.7 %all-to-all-start.1 = ((bf16[16,192,128]{2,1,0:T(8,128)(2,1)}), bf16[16,192,128]{2,1,0:T(8,128)(2,1)S(1)}, u32[]{:S(2)}, u32[]{:S(2)}) async-start(bf16[16,192,128]{2,1,0:T(8,128)(2,1)} %bitcast.28), calls=%async_computation.1 | async-start | bytes 1572864 | tf_op jit(solution)/shard_map/all_to_all | solution.py:214
  100.5 0.9 copy-start.3
  108.3 2.4 %collective-permute-start.6 = (bf16[21,128,128]{2,1,0:T(8,128)(2,1)}, bf16[21,128,128]{2,1,0:T(8,128)(2,1)S(1)}, u32[]{:S(2)}, u32[]{:S(2)}) collective-permute-start(bf16[21,128,128]{2,1,0:T(8,128)(2,1)} %get-tuple-element.8), channel_id=1, source_target_pairs={{0,16},{16,0},{32,48},{48,32},{64,80},{80,64},{96,112},{112,96},{1... | collective-permute-start | bytes 2064392 | tf_op jit(solution)/shard_map/ppermute | solution.py:162
  127.9 3.0 %collective-permute-start.7 = (bf16[168,128]{1,0:T(8,128)(2,1)S(1)}, bf16[168,128]{1,0:T(8,128)(2,1)S(1)}, u32[]{:S(2)}, u32[]{:S(2)}) collective-permute-start(bf16[168,128]{1,0:T(8,128)(2,1)S(1)} %reduce_sum.92), channel_id=1, source_target_pairs={{0,32},{16,48},{32,0},{48,16},{64,96},{80,112},{96,64},{112,80},{1... | collective-permute-start | bytes 129032 | tf_op jit(solution)/shard_map/ppermute | solution.py:162
  130.9 7.7 %collective-permute-start.8 = (bf16[168,128]{1,0:T(8,128)(2,1)S(1)}, bf16[168,128]{1,0:T(8,128)(2,1)S(1)}, u32[]{:S(2)}, u32[]{:S(2)}) collective-permute-start(bf16[168,128]{1,0:T(8,128)(2,1)S(1)} %add_convert_fusion.3), channel_id=1, source_target_pairs={{0,64},{16,80},{32,96},{48,112},{64,0},{80,16},{96,32},{112,48},{1... | collective-permute-start | bytes 129032 | tf_op jit(solution)/shard_map/ppermute | solution.py:162
  138.6 6.9 %collective-permute-start.9 = (bf16[168,128]{1,0:T(8,128)(2,1)S(1)}, bf16[168,128]{1,0:T(8,128)(2,1)S(1)}, u32[]{:S(2)}, u32[]{:S(2)}) collective-permute-start(bf16[168,128]{1,0:T(8,128)(2,1)S(1)} %add_convert_fusion.2), channel_id=1, source_target_pairs={{0,128},{16,144},{32,160},{48,176},{64,192},{80,208},{96,224},{112... | collective-permute-start | bytes 129032 | tf_op jit(solution)/shard_map/ppermute | solution.py:162
  158.7 7.6 %copy-start.5 = (bf16[16,168,128]{2,1,0:T(8,128)(2,1)}, bf16[16,168,128]{2,1,0:T(8,128)(2,1)S(1)}, u32[]{:S(2)}) copy-start(bf16[16,168,128]{2,1,0:T(8,128)(2,1)S(1)} %all_to_all.35) | copy-start | bytes 2064388
  158.7 7.6 %collective-permute-start.10 = (bf16[21,128,128]{2,1,0:T(8,128)(2,1)S(1)}, bf16[21,128,128]{2,1,0:T(8,128)(2,1)S(1)}, u32[]{:S(2)}, u32[]{:S(2)}) collective-permute-start(bf16[21,128,128]{2,1,0:T(8,128)(2,1)S(1)} %bitcast.29), channel_id=1, source_target_pairs={{0,16},{16,0},{32,48},{48,32},{64,80},{80,64},{96,112},{112,96},{1... | collective-permute-start | bytes 2064392 | tf_op jit(solution)/shard_map/ppermute | solution.py:162
  166.2 0.8 copy-start.6

commit v2 on v0

v2 whole, which is shorter than its diff:
```python
import functools

import jax
import jax.numpy as jnp
from jax import lax
from jax.experimental import pallas as pl
from jax.experimental.pallas import tpu as pltpu
from jax.sharding import PartitionSpec as P

HB = 8
BS = 128
NINT = 8
TILE = 128
PAIRS = 42
HALF = PAIRS // 2
REACH = 4
VMEM = pltpu.VMEM
SMEM = pltpu.SMEM
F32 = jnp.float32
BF16 = jnp.bfloat16


def vmem(count):
    return [pl.BlockSpec(memory_space=VMEM)] * count


def smem(count):
    return [pl.BlockSpec(memory_space=SMEM)] * count


def call(kernel, outs, scalars, arrays, scratch=(), flops=0, limit=24 << 20):
    moved = sum(a.size * a.dtype.itemsize for a in (*arrays, *outs))
    return pl.pallas_call(
        kernel,
        out_shape=tuple(outs),
        in_specs=smem(len(scalars)) + vmem(len(arrays)),
        out_specs=tuple(vmem(len(outs))),
        scratch_shapes=list(scratch),
        compiler_params=pltpu.CompilerParams(vmem_limit_bytes=limit),
        cost_estimate=pl.CostEstimate(flops=flops, bytes_accessed=moved, transcendentals=0),
    )(*scalars, *arrays)


def shape(dims, dtype=BF16):
    return jax.ShapeDtypeStruct(dims, dtype)


def table_kernel(where_ref, turned_ref, width_ref, interval_ref, near_ref, far_ref, pair_ref):
    slots, blocks = turned_ref.shape
    first, total, cut = where_ref[0], where_ref[1], where_ref[2]
    edge = blocks // 3

    def one_row(b, _):
        line = jnp.where(b < edge, b, b - edge)
        outer = (b < edge) | (b >= 2 * edge)

        @pl.when(outer)
        def _():
            for k in range(edge):
                far_ref[line, k] = edge

        found = jnp.int32(0)
        for n in range(slots):
            away = turned_ref[n, b] - first
            away = jnp.where(away < -HB, away + total, away)
            away = jnp.where(away >= total - HB, away - total, away)
            local = (away >= 0) & (away < blocks)
            near_ref[n, b] = jnp.where(local, away, blocks)
            halo = jnp.where(away < 0, away + HB, away - blocks)

            @pl.when(jnp.logical_not(local))
            def _():
                far_ref[line, found] = n * 16 + halo

            found += jnp.where(local, 0, 1)
        return 0

    lax.fori_loop(0, blocks, one_row, 0)
    tiles = (pair_ref.shape[0] - 2) // REACH
    ends = []
    end = jnp.int32(0)
    for s in range(width_ref.shape[0]):
        end += width_ref[s] // TILE
        ends.append(end)

    def slice_of(t):
        index = jnp.int32(0)
        for end in ends:
            index += jnp.where(t >= end, 1, 0)
        return index

    lanes = [slice_of(t) for t in range(tiles)]
    slot = jnp.int32(0)
    for i in range(tiles):
        for d in range(REACH):
            if i + d < tiles:
                valid = lanes[i + d] - lanes[i] <= 1
                pair_ref[i * REACH + d] = jnp.where(valid, slot, PAIRS)
                slot += jnp.where(valid, 1, 0)
            else:
                pair_ref[i * REACH + d] = PAIRS
    pair_ref[tiles * REACH] = where_ref[3]
    pair_ref[tiles * REACH + 1] = interval_ref[slice_of(cut)]


def near_kernel(scale, near_ref, pair_ref, ham_ref, low_ref, mid_ref, high_ref, *rest):
    before = rest[:3] if scale != 1 else None
    mid_out, low_out, high_out, stack = rest[-4:]
    blocks, slots = ham_ref.shape[:2]
    third = blocks // 3
    span = third * BS
    for q, ref in enumerate((low_ref, mid_ref, high_ref)):
        stack[q * span : (q + 1) * span] = ref[...]
    stack[blocks * BS :] = jnp.zeros((BS, TILE), BF16)
    centre = -0.5 + pair_ref[pair_ref.shape[0] - 1].astype(F32) * F32(1 / (NINT - 1))

    def tile_at(n, b):
        return stack[pl.ds(pl.multiple_of(near_ref[n, b] * BS, BS), BS), :]

    for b in (*range(third), *range(2 * third, blocks), *range(third, 2 * third)):
        total = jnp.zeros((BS, TILE), F32)
        for n in range(0, slots, 2):
            if n + 1 < slots:
                left = jnp.concatenate([ham_ref[b, n], ham_ref[b, n + 1]], axis=1)
                right = jnp.concatenate([tile_at(n, b), tile_at(n + 1, b)], axis=0)
            else:
                left, right = ham_ref[b, n], tile_at(n, b)
            total += jnp.dot(left, right, preferred_element_type=F32)
        part = b // third
        here = slice((b - part * third) * BS, (b - part * third + 1) * BS)
        own = stack[b * BS : (b + 1) * BS].astype(F32)
        value = total - centre * own
        if scale != 1:
            value = scale * value - before[part][here, :].astype(F32)
        out = (low_out, mid_out, high_out)[part]
        out[here, :] = value.astype(out.dtype)


def far_kernel(scale, joined, far_ref, ham_ref, below_ref, above_ref, low_ref, high_ref, *rest):
    stack = rest[-1]
    span = below_ref.shape[0]
    edge = span // BS
    for q, ref in enumerate((below_ref, above_ref)):
        stack[q, :span] = ref[...]
        stack[q, span:] = jnp.zeros((BS, TILE), BF16)
    for line in range(2 * edge):
        side = line // edge
        index = line - side * edge
        b = index + side * 2 * edge
        most = edge - index if side == 0 else index + 1
        left, right = [], []
        for k in range(most):
            entry = far_ref[line, k]
            slot = entry // 16
            left.append(ham_ref[b, slot])
            start = pl.multiple_of((entry - slot * 16) * BS, BS)
            right.append(stack[side, pl.ds(start, BS), :])
        total = (low_ref, high_ref)[side][index * BS : (index + 1) * BS, :]
        for k in range(0, most, 2):
            lhs = jnp.concatenate(left[k : k + 2], axis=1)
            rhs = jnp.concatenate(right[k : k + 2], axis=0)
            total += scale * jnp.dot(lhs, rhs, preferred_element_type=F32)
        value = total.astype(BF16)
        if joined:
            rest[-2][b * BS : (b + 1) * BS, :] = value
        else:
            rest[side][index * BS : (index + 1) * BS, :] = value
    if joined:
        rest[-2][span : 2 * span, :] = rest[0][...]


def gram_kernel(pair_ref, field_ref, keep_ref, send_ref):
    tiles = field_ref.shape[0]
    core = pair_ref[tiles * REACH]
    mine = core * HALF
    theirs = HALF - mine
    for i in range(tiles):
        reach = min(REACH, tiles - i)
        right = jnp.concatenate([field_ref[i + d] for d in range(reach)], axis=1)
        block = lax.dot_general(
            field_ref[i], right, (((0,), (0,)), ((), ())), preferred_element_type=F32
        )
        for d in range(reach):
            slot = pair_ref[i * REACH + d]
            piece = block[:, d * TILE : (d + 1) * TILE]

            @pl.when((slot >= mine) & (slot < mine + HALF))
            def _():
                keep_ref[slot - mine] = piece

            @pl.when((slot >= theirs) & (slot < theirs + HALF))
            def _():
                send_ref[slot - theirs] = piece.astype(BF16)


def correct_kernel(rows_all, pair_ref, field_ref, mine_ref, other_ref, out_ref, gram, scaled, norm):
    tiles = field_ref.shape[0]
    core = pair_ref[tiles * REACH]
    gram[pl.ds(core * HALF, HALF)] = mine_ref[...]
    gram[pl.ds(HALF - core * HALF, HALF)] = other_ref[...]
    gram[PAIRS] = jnp.zeros((TILE, TILE), BF16)
    at_row = lax.broadcasted_iota(jnp.int32, (TILE, TILE), 0)
    at_col = lax.broadcasted_iota(jnp.int32, (TILE, TILE), 1)
    eye = at_row == at_col
    for t in range(tiles):
        block = gram[pair_ref[t * REACH]].astype(F32)
        squares = jnp.sum(jnp.where(eye, block, 0.0), axis=0, keepdims=True)
        inverse = lax.rsqrt(squares / rows_all + 1e-05)
        norm[t : t + 1, :] = inverse
        scaled[t] = (field_ref[t].astype(F32) * (inverse * inverse)).astype(BF16)
    for j in range(tiles):
        below = range(max(0, j - REACH + 1), j + 1)
        left = jnp.concatenate([scaled[i] for i in below], axis=1)
        right = jnp.concatenate([gram[pair_ref[i * REACH + j - i]] for i in below], axis=0)
        total = jnp.dot(left, right, preferred_element_type=F32)
        above = range(j + 1, min(tiles, j + REACH))
        if above:
            left = jnp.concatenate([scaled[i] for i in above], axis=1)
            right = jnp.concatenate([gram[pair_ref[j * REACH + i - j]] for i in above], axis=1)
            total += lax.dot_general(
                left, right, (((1,), (1,)), ((), ())), preferred_element_type=F32
            )
        value = norm[j : j + 1, :] * (1.5 * field_ref[j].astype(F32) - (0.5 / rows_all) * total)
        out_ref[:, j * TILE : (j + 1) * TILE] = value.astype(BF16)


def shift(array, distance):
    size = lax.axis_size("row")
    return lax.ppermute(array, "row", [(i, (i + distance) % size) for i in range(size)])


def exchange(array, bit):
    return lax.ppermute(array, "row", [(i, i ^ bit) for i in range(lax.axis_size("row"))])


def body(ham_blocks, neighbors, slice_widths, interval_index, start_vectors):
    rows_mine, columns = start_vectors.shape
    tiles = columns // TILE
    blocks, slots = ham_blocks.shape[:2]
    row_count = lax.axis_size("row")
    rows_all = blocks * BS * row_count
    panel_rows = blocks * BS
    span = panel_rows // 3
    panel = lax.all_to_all(start_vectors, "cuts", split_axis=1, concat_axis=0, tiled=True)

    row = lax.axis_index("row")
    place = jnp.stack(
        [row * blocks, jnp.int32(blocks * row_count), lax.axis_index("cuts"), row % 2]
    ).astype(jnp.int32)
    near, far, pair = pl.pallas_call(
        table_kernel,
        out_shape=(
            shape((slots, blocks), jnp.int32),
            shape((2 * blocks // 3, HB), jnp.int32),
            shape((tiles * REACH + 2,), jnp.int32),
        ),
        in_specs=smem(4),
        out_specs=tuple(smem(3)),
        cost_estimate=pl.CostEstimate(flops=1 << 20, bytes_accessed=1 << 12, transcendentals=0),
    )(place, neighbors.T, slice_widths, interval_index)
    ham = pltpu.with_memory_space_constraint(ham_blocks, VMEM)
    work = 2 * blocks * slots * BS * BS * TILE

    def apply_ham(scale, field, before, joined):
        low, mid, high = field
        below = shift(high, 1)
        above = shift(low, -1)
        mid, low, high = call(
            functools.partial(near_kernel, scale),
            [shape((span, TILE)), shape((span, TILE), F32), shape((span, TILE), F32)],
            [near, pair],
            [ham, low, mid, high, *before],
            [VMEM((panel_rows + BS, TILE), BF16)],
            work,
        )
        outs = [shape((panel_rows, TILE))] if joined else [shape((span, TILE))] * 2
        result = call(
            functools.partial(far_kernel, scale, joined),
            outs,
            [far],
            [ham, below, above, low, high] + [mid] * joined,
            [VMEM((2, span + BS, TILE), BF16)],
            work // 4,
        )
        return result[0] if joined else (result[0], mid, result[1])

    start = tuple(panel[q * span : (q + 1) * span] for q in range(3))
    first = apply_ham(1, start, (), False)
    second = apply_ham(2, first, start, False)
    filtered = apply_ham(2, second, first, True)

    field = lax.all_to_all(filtered.reshape(tiles, rows_mine, TILE), "cuts", 0, 0)
    kept, sent = call(
        gram_kernel,
        [shape((HALF, TILE, TILE), F32), shape((HALF, TILE, TILE))],
        [pair],
        [field],
        (),
        1 << 28,
    )
    partial = (kept + exchange(sent, 1).astype(F32)).astype(BF16)
    cut_count = lax.axis_size("cuts")
    share = HALF * TILE // cut_count
    pieces = lax.all_to_all(partial.reshape(cut_count, share, TILE), "cuts", 0, 0)
    total = jnp.sum(pieces.astype(F32), axis=0)
    bit = 2
    while bit < row_count:
        rounded = total.astype(BF16)
        total = rounded.astype(F32) + exchange(rounded, bit).astype(F32)
        bit *= 2
    spread = jnp.broadcast_to(total.astype(BF16)[None], (cut_count, share, TILE))
    mine = lax.all_to_all(spread, "cuts", 0, 0).reshape(HALF, TILE, TILE)
    other = exchange(mine, 1)
    (corrected,) = call(
        functools.partial(correct_kernel, rows_all),
        [shape((rows_mine, columns))],
        [pair],
        [field, mine, other],
        [
            VMEM((PAIRS + 1, TILE, TILE), BF16),
            VMEM((tiles, rows_mine, TILE), BF16),
            VMEM((tiles, TILE), F32),
        ],
        1 << 29,
    )
    return corrected


def solution(mesh):
    return jax.shard_map(
        body,
        mesh=mesh,
        in_specs=(P("row", None, None, None), P("row", None), P(), P(), P(("row", "cuts"), None)),
        out_specs=P(("row", "cuts"), None),
        check_vma=False,
    )
```

time: 283 us -> 136 us (0.48)
  waiting for transfers between devices: 125 us -> 16.2 us
  local copies, waits for them, and re-layouts: 37.9 us -> 6.41 us
  matrix products: 31.4 us -> 0 us
  Pallas kernels: 0 us -> 26.5 us
  blocking collectives: 40.3 us -> 64.6 us
  between operations: 13.7 us -> 0.17 us
  other arithmetic: 9.49 us -> 0.95 us
  starting transfers between devices: 23.1 us -> 20.1 us
    ppermute x12 -> x11, waiting for transfers between devices: 93.8 us -> 16.2 us  [the longest x5 10.6 us: exchange(): lax.ppermute(array, 'row', [(i, i ^ bit) for i in range(lax.axis_size('ro...]
    all_to_all x1 -> x4, blocking collectives: 19.6 us -> 64.6 us  [the longest x1 20 us: body(): lax.all_to_all(start_vectors, 'cuts', split_axis=1, concat_axis=0, tiled=...]
    dot_general x6 -> x0, matrix products: 31.4 us -> none  [the longest x3 25 us: apply_ham(): jnp.einsum('bnij,bnjw->biw', ham_blocks, picked, preferred_element_type=j...]
    gather x3 -> x0, local copies, waits for them, and re-layouts: 30.7 us -> none  [apply_ham(): picked = stacked[position]]
    pallas_call x0 -> x9, Pallas kernels: none -> 26.5 us  [the longest x8 22.4 us: call(): pl.pallas_call(kernel, out_shape=tuple(outs), in_specs=smem(len(scalars))...]
    all_gather x1 -> x0, blocking collectives: 20.6 us -> none  [total_of_pieces(): return lax.all_gather(array, axis).astype(jnp.float32).sum(0)]
    all_gather x1 -> x0, waiting for transfers between devices: 20.5 us -> none  [total_of_pieces(): return lax.all_gather(array, axis).astype(jnp.float32).sum(0)]
    all_to_all x1 -> x0, waiting for transfers between devices: 10.9 us -> none  [body(): lax.all_to_all(start_vectors, 'cuts', split_axis=1, concat_axis=0, tiled=...]
  transfers between devices with their start and end apart: 14 -> 11, of which waited for: 11 -> 7; matrix products, arithmetic and copies ran while one was open for 2% -> 0% of each run, Pallas kernels for 0% -> 10%
where the time goes in v2:
time: 136 us; the launch traced here: 135 us
  blocking collectives  64.6 us (47%)
  Pallas kernels  26.5 us (19%)
  starting transfers between devices  20.1 us (15%)
  waiting for transfers between devices  16.2 us (12%)
  local copies, waits for them, and re-layouts  6.41 us (5%)
    pallas_call x8, Pallas kernels, call(): pl.pallas_call(kernel, out_shape=tuple(outs), in_specs=smem(len(scalars))...  22.4 us
    all_to_all x1, blocking collectives, body(): lax.all_to_all(start_vectors, 'cuts', split_axis=1, concat_axis=0, tiled=...  20 us
    ppermute x5, starting transfers between devices, exchange(): lax.ppermute(array, 'row', [(i, i ^ bit) for i in range(lax.axis_size('ro...  15.9 us
    all_to_all x1, blocking collectives, body(): lax.all_to_all(filtered.reshape(tiles, rows_mine, TILE), 'cuts', 0, 0)  15.8 us
    all_to_all x1, blocking collectives, body(): lax.all_to_all(partial.reshape(cut_count, share, TILE), 'cuts', 0, 0)  15.7 us
    all_to_all x1, blocking collectives, body(): mine = lax.all_to_all(spread, 'cuts', 0, 0).reshape(HALF, TILE, TILE)  13.1 us
    ppermute x5, waiting for transfers between devices, exchange(): lax.ppermute(array, 'row', [(i, i ^ bit) for i in range(lax.axis_size('ro...  10.6 us
    unnamed x14, local copies, waits for them, and re-layouts  6.07 us
  transfers between devices with their start and end apart: 11, of which 7 were waited for; matrix products, arithmetic and copies ran while one was open for 0% of the time, Pallas kernels for 10%

profile of v2, /device:TPU:33, one launch (start us, length us, event | category | flops | bytes accessed | tf_op | source)
XLA Modules:
  0.0 134.9 jit_solution(13809942912142662238)
XLA Ops:
  0.0 0.0 copy-start
  0.0 1.1 copy-done
  1.1 0.2 copy_bitcast_fusion
  1.3 20.0 %all_to_all.34 = bf16[192,16,128]{2,0,1:T(8,128)(2,1)S(1)} all-to-all(bf16[192,16,128]{2,0,1:T(8,128)(2,1)S(1)} %copy_bitcast_fusion), channel_id=1, replica_groups=mesh['row'=16,'cuts'=16] {'cuts'}, dimensions={1} | all-to-all | bytes 1572864 | tf_op jit(solution)/shard_map/all_to_all | solution.py:244
  21.3 0.1 fusion
  21.4 1.7 %collective-permute-start.1 = (bf16[1024,128]{1,0:T(8,128)(2,1)S(1)}, bf16[1024,128]{1,0:T(8,128)(2,1)S(1)}, u32[]{:S(2)}, u32[]{:S(2)}) collective-permute-start(bf16[1024,128]{1,0:T(8,128)(2,1)S(1)} %get-tuple-element.42.low_ref.rest_0_), channel_id=1, source_target_pairs={{0,240},{16,0},{32,16},{48,32},{64,48},{80,64},{96,80},{112,96},{1... | collective-permute-start | bytes 786440 | tf_op jit(solution)/shard_map/ppermute | solution.py:229
  23.0 1.5 %collective-permute-start = (bf16[1024,128]{1,0:T(8,128)(2,1)S(1)}, bf16[1024,128]{1,0:T(8,128)(2,1)S(1)}, u32[]{:S(2)}, u32[]{:S(2)}) collective-permute-start(bf16[1024,128]{1,0:T(8,128)(2,1)S(1)} %get-tuple-element.43.high_ref.rest_2_), channel_id=1, source_target_pairs={{0,16},{16,32},{32,48},{48,64},{64,80},{80,96},{96,112},{112,128},... | collective-permute-start | bytes 786440 | tf_op jit(solution)/shard_map/ppermute | solution.py:229
  24.6 0.6 pad_add_fusion.where_ref
  25.2 4.1 %shard_map.55 = (s32[11,24]{1,0:T(8,128)}, s32[16,8]{1,0:T(8,128)}, s32[66]{0:T(128)}) custom-call(s32[4]{0:T(128)} %pad_add_fusion.where_ref, s32[11,24]{1,0:T(8,128)} %bitcast.20, s32[12]{0:T(128)} %width_ref.1, s32[12]{0:T(128)} %interval_ref.1), custom_call_target="tpu_custom_call" | custom-call | flops 1048576 | bytes 4096 | tf_op jit(solution)/shard_map/pallas_call | solution.py:250
  29.3 0.0 copy-start.1
  29.3 3.4 %copy-done.1 = bf16[24,11,128,128]{3,2,1,0:T(8,128)(2,1)S(1)} copy-done((bf16[24,11,128,128]{3,2,1,0:T(8,128)(2,1)S(1)}, bf16[24,11,128,128]{3,2,1,0:T(8,128)(2,1)}, u32[]{:S(2)}) %copy-start.1) | copy-done | bytes 8650776
  32.8 0.0 copy-start.4
  32.8 0.7 copy-done.4
  33.4 0.0 copy-start.5
  33.5 0.7 copy-done.5
  34.1 0.0 copy-start.2
  34.1 0.0 copy-start.3
  34.1 3.3 %shard_map.56 = (bf16[1024,128]{1,0:T(8,128)(2,1)S(1)}, f32[1024,128]{1,0:T(8,128)S(1)}, f32[1024,128]{1,0:T(8,128)S(1)}) custom-call(s32[11,24]{1,0:T(8,128)S(1)} %copy-done.4, s32[66]{0:T(128)S(1)} %copy-done.5, bf16[24,11,128,128]{3,2,1,0:T(8,128)(2,1)S(1)} %copy-done.1, bf16[1024,128]{1,0:T(8,128)(2,1)S(1)} %get-tuple-element.42.low_ref.rest_0_, ...), custom_call_target="tpu_custom_call" | custom-call | flops 1107296256 | bytes 10747904 | tf_op jit(solution)/shard_map/pallas_call | solution.py:33
  37.5 0.0 collective-permute-done.1.above_ref
  37.5 0.0 collective-permute-done.below_ref
  37.5 0.1 copy-done.2
  37.6 0.0 copy-done.3
  37.6 1.6 %shard_map.57 = (bf16[1024,128]{1,0:T(8,128)(2,1)S(1)}, bf16[1024,128]{1,0:T(8,128)(2,1)S(1)}) custom-call(s32[16,8]{1,0:T(8,128)S(1)} %copy-done.3, bf16[24,11,128,128]{3,2,1,0:T(8,128)(2,1)S(1)} %copy-done.2, bf16[1024,128]{1,0:T(8,128)(2,1)S(1)} %collective-permute-done.below_ref, bf16[1024,128]{1,0:T(8,128)(2,1)S(1)} %collective-permute-done.1.above_ref, ...), custom_call_target="tpu_custom_call" | custom-call | flops 276824064 | bytes 10747904 | tf_op jit(solution)/shard_map/pallas_call | solution.py:33
  39.2 0.5 collective-permute-start.2
  39.7 0.0 collective-permute-start.3
  39.7 3.3 %shard_map.58 = (bf16[1024,128]{1,0:T(8,128)(2,1)S(1)}, f32[1024,128]{1,0:T(8,128)S(1)}, f32[1024,128]{1,0:T(8,128)S(1)}) custom-call(s32[11,24]{1,0:T(8,128)S(1)} %copy-done.4, s32[66]{0:T(128)S(1)} %copy-done.5, bf16[24,11,128,128]{3,2,1,0:T(8,128)(2,1)S(1)} %copy-done.2, bf16[1024,128]{1,0:T(8,128)(2,1)S(1)} %get-tuple-element.29.low_ref.rest_0_, ...), custom_call_target="tpu_custom_call" | custom-call | flops 1107296256 | bytes 11534336 | tf_op jit(solution)/shard_map/pallas_call | solution.py:33
  43.0 0.0 collective-permute-done.2.below_ref
  43.1 2.4 %collective-permute-done.3.above_ref = bf16[1024,128]{1,0:T(8,128)(2,1)S(1)} collective-permute-done((bf16[1024,128]{1,0:T(8,128)(2,1)S(1)}, bf16[1024,128]{1,0:T(8,128)(2,1)S(1)}, u32[]{:S(2)}, u32[]{:S(2)}) %collective-permute-start.3) | collective-permute-done | bytes 262176 | tf_op jit(solution)/shard_map/ppermute | solution.py:229
  45.5 1.6 %shard_map.59 = (bf16[1024,128]{1,0:T(8,128)(2,1)S(1)}, bf16[1024,128]{1,0:T(8,128)(2,1)S(1)}) custom-call(s32[16,8]{1,0:T(8,128)S(1)} %copy-done.3, bf16[24,11,128,128]{3,2,1,0:T(8,128)(2,1)S(1)} %copy-done.2, bf16[1024,128]{1,0:T(8,128)(2,1)S(1)} %collective-permute-done.2.below_ref, bf16[1024,128]{1,0:T(8,128)(2,1)S(1)} %collective-permute-done.3.above_ref, ...), custom_call_target="tpu_custom_call" | custom-call | flops 276824064 | bytes 10747904 | tf_op jit(solution)/shard_map/pallas_call | solution.py:33
  47.1 0.0 collective-permute-start.4
  47.1 0.5 collective-permute-start.5
  47.6 3.4 %shard_map.60 = (bf16[1024,128]{1,0:T(8,128)(2,1)S(1)}, f32[1024,128]{1,0:T(8,128)S(1)}, f32[1024,128]{1,0:T(8,128)S(1)}) custom-call(s32[11,24]{1,0:T(8,128)S(1)} %copy-done.4, s32[66]{0:T(128)S(1)} %copy-done.5, bf16[24,11,128,128]{3,2,1,0:T(8,128)(2,1)S(1)} %copy-done.2, bf16[1024,128]{1,0:T(8,128)(2,1)S(1)} %get-tuple-element.34.low_ref, ...), custom_call_target="tpu_custom_call" | custom-call | flops 1107296256 | bytes 11534336 | tf_op jit(solution)/shard_map/pallas_call | solution.py:33
  50.9 0.0 collective-permute-done.4.below_ref
  51.0 3.2 %collective-permute-done.5.above_ref = bf16[1024,128]{1,0:T(8,128)(2,1)S(1)} collective-permute-done((bf16[1024,128]{1,0:T(8,128)(2,1)S(1)}, bf16[1024,128]{1,0:T(8,128)(2,1)S(1)}, u32[]{:S(2)}, u32[]{:S(2)}) %collective-permute-start.5) | collective-permute-done | bytes 262176 | tf_op jit(solution)/shard_map/ppermute | solution.py:229
  54.2 1.6 %shard_map.61 = bf16[3072,128]{1,0:T(8,128)(2,1)S(1)} custom-call(s32[16,8]{1,0:T(8,128)S(1)} %copy-done.3, bf16[24,11,128,128]{3,2,1,0:T(8,128)(2,1)S(1)} %copy-done.2, bf16[1024,128]{1,0:T(8,128)(2,1)S(1)} %collective-permute-done.4.below_ref, bf16[1024,128]{1,0:T(8,128)(2,1)S(1)} %collective-permute-done.5.above_ref, ...), custom_call_target="tpu_custom_call" | custom-call | flops 276824064 | bytes 11272192 | tf_op jit(solution)/shard_map/pallas_call | solution.py:33
  55.8 0.0 copy-start.6
  55.8 15.8 %all_to_all.35.field_ref = bf16[16,192,128]{2,1,0:T(8,128)(2,1)S(1)} all-to-all(bf16[16,192,128]{2,1,0:T(8,128)(2,1)S(1)} %bitcast.15), channel_id=1, replica_groups=mesh['row'=16,'cuts'=16] {'cuts'}, dimensions={0} | all-to-all | bytes 1572864 | tf_op jit(solution)/shard_map/all_to_all | solution.py:292
  71.6 0.0 copy-done.6
  71.6 4.6 %shard_map.62 = (f32[21,128,128]{2,1,0:T(8,128)S(1)}, bf16[21,128,128]{2,1,0:T(8,128)(2,1)S(1)}) custom-call(s32[66]{0:T(128)S(1)} %copy-done.6, bf16[16,192,128]{2,1,0:T(8,128)(2,1)S(1)} %all_to_all.35.field_ref), custom_call_target="tpu_custom_call" | custom-call | flops 268435456 | bytes 2850816 | tf_op jit(solution)/shard_map/pallas_call | solution.py:33
  76.2 0.1 collective-permute-start.6
  76.3 2.1 %collective-permute-done.6 = bf16[21,128,128]{2,1,0:T(8,128)(2,1)S(1)} collective-permute-done((bf16[21,128,128]{2,1,0:T(8,128)(2,1)S(1)}, bf16[21,128,128]{2,1,0:T(8,128)(2,1)S(1)}, u32[]{:S(2)}, u32[]{:S(2)}) %collective-permute-start.6) | collective-permute-done | bytes 688160 | tf_op jit(solution)/shard_map/ppermute | solution.py:233
  78.5 0.2 add_convert_fusion
  78.7 15.7 %all_to_all.36 = bf16[16,168,128]{2,1,0:T(8,128)(2,1)S(1)} all-to-all(bf16[16,168,128]{2,1,0:T(8,128)(2,1)S(1)} %bitcast.19), channel_id=1, replica_groups=mesh['row'=16,'cuts'=16] {'cuts'}, dimensions={0} | all-to-all | bytes 1376256 | tf_op jit(solution)/shard_map/all_to_all | solution.py:304
  94.4 0.1 reduce_sum.12
  94.5 1.5 %collective-permute-start.7 = (bf16[168,128]{1,0:T(8,128)(2,1)S(1)}, bf16[168,128]{1,0:T(8,128)(2,1)S(1)}, u32[]{:S(2)}, u32[]{:S(2)}) collective-permute-start(bf16[168,128]{1,0:T(8,128)(2,1)S(1)} %reduce_sum.12), channel_id=1, source_target_pairs={{0,32},{16,48},{32,0},{48,16},{64,96},{80,112},{96,64},{112,80},{1... | collective-permute-start | bytes 129032 | tf_op jit(solution)/shard_map/ppermute | solution.py:233
  96.0 1.4 %collective-permute-done.7 = bf16[168,128]{1,0:T(8,128)(2,1)S(1)} collective-permute-done((bf16[168,128]{1,0:T(8,128)(2,1)S(1)}, bf16[168,128]{1,0:T(8,128)(2,1)S(1)}, u32[]{:S(2)}, u32[]{:S(2)}) %collective-permute-start.7) | collective-permute-done | bytes 43040 | tf_op jit(solution)/shard_map/ppermute | solution.py:233
  97.4 5.3 %collective-permute-start.8 = (bf16[168,128]{1,0:T(8,128)(2,1)S(1)}, bf16[168,128]{1,0:T(8,128)(2,1)S(1)}, u32[]{:S(2)}, u32[]{:S(2)}) collective-permute-start(bf16[168,128]{1,0:T(8,128)(2,1)S(1)} %add_convert_fusion.3), channel_id=1, source_target_pairs={{0,64},{16,80},{32,96},{48,112},{64,0},{80,16},{96,32},{112,48},{1... | collective-permute-start | bytes 129032 | tf_op jit(solution)/shard_map/ppermute | solution.py:233
  102.7 1.4 %collective-permute-done.8 = bf16[168,128]{1,0:T(8,128)(2,1)S(1)} collective-permute-done((bf16[168,128]{1,0:T(8,128)(2,1)S(1)}, bf16[168,128]{1,0:T(8,128)(2,1)S(1)}, u32[]{:S(2)}, u32[]{:S(2)}) %collective-permute-start.8) | collective-permute-done | bytes 43040 | tf_op jit(solution)/shard_map/ppermute | solution.py:233
  104.1 3.1 %collective-permute-start.9 = (bf16[168,128]{1,0:T(8,128)(2,1)S(1)}, bf16[168,128]{1,0:T(8,128)(2,1)S(1)}, u32[]{:S(2)}, u32[]{:S(2)}) collective-permute-start(bf16[168,128]{1,0:T(8,128)(2,1)S(1)} %add_convert_fusion.2), channel_id=1, source_target_pairs={{0,128},{16,144},{32,160},{48,176},{64,192},{80,208},{96,224},{112... | collective-permute-start | bytes 129032 | tf_op jit(solution)/shard_map/ppermute | solution.py:233
  107.2 3.8 %collective-permute-done.9 = bf16[168,128]{1,0:T(8,128)(2,1)S(1)} collective-permute-done((bf16[168,128]{1,0:T(8,128)(2,1)S(1)}, bf16[168,128]{1,0:T(8,128)(2,1)S(1)}, u32[]{:S(2)}, u32[]{:S(2)}) %collective-permute-start.9) | collective-permute-done | bytes 43040 | tf_op jit(solution)/shard_map/ppermute | solution.py:233
  111.0 0.1 broadcast_in_dim.2
  111.1 13.1 %all_to_all.37 = bf16[16,168,128]{2,1,0:T(8,128)(2,1)S(1)} all-to-all(bf16[16,168,128]{2,1,0:T(8,128)(2,1)S(1)} %broadcast_in_dim.2), channel_id=1, replica_groups=mesh['row'=16,'cuts'=16] {'cuts'}, dimensions={0} | all-to-all | bytes 1376256 | tf_op jit(solution)/shard_map/all_to_all | solution.py:312
  124.3 5.9 %collective-permute-start.10 = (bf16[21,128,128]{2,1,0:T(8,128)(2,1)S(1)}, bf16[21,128,128]{2,1,0:T(8,128)(2,1)S(1)}, u32[]{:S(2)}, u32[]{:S(2)}) collective-permute-start(bf16[21,128,128]{2,1,0:T(8,128)(2,1)S(1)} %bitcast.16), channel_id=1, source_target_pairs={{0,16},{16,0},{32,48},{48,32},{64,80},{80,64},{96,112},{112,96},{1... | collective-permute-start | bytes 2064392 | tf_op jit(solution)/shard_map/ppermute | solution.py:233
  130.2 1.8 %collective-permute-done.10.other_ref = bf16[21,128,128]{2,1,0:T(8,128)(2,1)S(1)} collective-permute-done((bf16[21,128,128]{2,1,0:T(8,128)(2,1)S(1)}, bf16[21,128,128]{2,1,0:T(8,128)(2,1)S(1)}, u32[]{:S(2)}, u32[]{:S(2)}) %collective-permute-start.10) | collective-permute-done | bytes 688160 | tf_op jit(solution)/shard_map/ppermute | solution.py:233
  131.9 3.0 %shard_map.63 = bf16[192,2048]{1,0:T(8,128)(2,1)} custom-call(s32[66]{0:T(128)S(1)} %copy-done.6, bf16[16,192,128]{2,1,0:T(8,128)(2,1)S(1)} %all_to_all.35.field_ref, bf16[21,128,128]{2,1,0:T(8,128)(2,1)S(1)} %bitcast.17, bf16[21,128,128]{2,1,0:T(8,128)(2,1)S(1)} %collective-permute-done.10.other_ref), custom_call_target="tpu_custom_call" | custom-call | flops 536870912 | bytes 2949120 | tf_op jit(solution)/shard_map/pallas_call | solution.py:33
  (3 shorter events, 0.0 us)
Async XLA Ops:
  0.0 1.1 copy-start
  21.4 16.1 %collective-permute-start.1 = (bf16[1024,128]{1,0:T(8,128)(2,1)S(1)}, bf16[1024,128]{1,0:T(8,128)(2,1)S(1)}, u32[]{:S(2)}, u32[]{:S(2)}) collective-permute-start(bf16[1024,128]{1,0:T(8,128)(2,1)S(1)} %get-tuple-element.42.low_ref.rest_0_), channel_id=1, source_target_pairs={{0,240},{16,0},{32,16},{48,32},{64,48},{80,64},{96,80},{112,96},{1... | collective-permute-start | bytes 786440 | tf_op jit(solution)/shard_map/ppermute | solution.py:229
  23.0 14.4 %collective-permute-start = (bf16[1024,128]{1,0:T(8,128)(2,1)S(1)}, bf16[1024,128]{1,0:T(8,128)(2,1)S(1)}, u32[]{:S(2)}, u32[]{:S(2)}) collective-permute-start(bf16[1024,128]{1,0:T(8,128)(2,1)S(1)} %get-tuple-element.43.high_ref.rest_2_), channel_id=1, source_target_pairs={{0,16},{16,32},{32,48},{48,64},{64,80},{80,96},{96,112},{112,128},... | collective-permute-start | bytes 786440 | tf_op jit(solution)/shard_map/ppermute | solution.py:229
  29.3 3.5 %copy-start.1 = (bf16[24,11,128,128]{3,2,1,0:T(8,128)(2,1)S(1)}, bf16[24,11,128,128]{3,2,1,0:T(8,128)(2,1)}, u32[]{:S(2)}) copy-start(bf16[24,11,128,128]{3,2,1,0:T(8,128)(2,1)} %ham_ref.11) | copy-start | bytes 25952260
  32.8 0.7 copy-start.4
  33.4 0.7 copy-start.5
  34.1 3.5 %copy-start.2 = (bf16[24,11,128,128]{3,2,1,0:T(8,128)(2,1)S(1)}, bf16[24,11,128,128]{3,2,1,0:T(8,128)(2,1)}, u32[]{:S(2)}) copy-start(bf16[24,11,128,128]{3,2,1,0:T(8,128)(2,1)} %ham_ref.11) | copy-start | bytes 25952260
  34.1 3.5 %copy-start.3 = (s32[16,8]{1,0:T(8,128)S(1)}, s32[16,8]{1,0:T(8,128)}, u32[]{:S(2)}) copy-start(s32[16,8]{1,0:T(8,128)} %get-tuple-element.24.far_ref) | copy-start | bytes 1540
  39.2 3.9 %collective-permute-start.2 = (bf16[1024,128]{1,0:T(8,128)(2,1)S(1)}, bf16[1024,128]{1,0:T(8,128)(2,1)S(1)}, u32[]{:S(2)}, u32[]{:S(2)}) collective-permute-start(bf16[1024,128]{1,0:T(8,128)(2,1)S(1)} %get-tuple-element.28.high_ref.rest_2_), channel_id=1, source_target_pairs={{0,16},{16,32},{32,48},{48,64},{64,80},{80,96},{96,112},{112,128},... | collective-permute-start | bytes 786440 | tf_op jit(solution)/shard_map/ppermute | solution.py:229
  39.7 5.8 %collective-permute-start.3 = (bf16[1024,128]{1,0:T(8,128)(2,1)S(1)}, bf16[1024,128]{1,0:T(8,128)(2,1)S(1)}, u32[]{:S(2)}, u32[]{:S(2)}) collective-permute-start(bf16[1024,128]{1,0:T(8,128)(2,1)S(1)} %get-tuple-element.29.low_ref.rest_0_), channel_id=1, source_target_pairs={{0,240},{16,0},{32,16},{48,32},{64,48},{80,64},{96,80},{112,96},{1... | collective-permute-start | bytes 786440 | tf_op jit(solution)/shard_map/ppermute | solution.py:229
  47.1 3.9 %collective-permute-start.4 = (bf16[1024,128]{1,0:T(8,128)(2,1)S(1)}, bf16[1024,128]{1,0:T(8,128)(2,1)S(1)}, u32[]{:S(2)}, u32[]{:S(2)}) collective-permute-start(bf16[1024,128]{1,0:T(8,128)(2,1)S(1)} %get-tuple-element.33.high_ref), channel_id=1, source_target_pairs={{0,16},{16,32},{32,48},{48,64},{64,80},{80,96},{96,112},{112,128},... | collective-permute-start | bytes 786440 | tf_op jit(solution)/shard_map/ppermute | solution.py:229
  47.1 7.1 %collective-permute-start.5 = (bf16[1024,128]{1,0:T(8,128)(2,1)S(1)}, bf16[1024,128]{1,0:T(8,128)(2,1)S(1)}, u32[]{:S(2)}, u32[]{:S(2)}) collective-permute-start(bf16[1024,128]{1,0:T(8,128)(2,1)S(1)} %get-tuple-element.34.low_ref), channel_id=1, source_target_pairs={{0,240},{16,0},{32,16},{48,32},{64,48},{80,64},{96,80},{112,96},{1... | collective-permute-start | bytes 786440 | tf_op jit(solution)/shard_map/ppermute | solution.py:229
  55.8 15.8 %copy-start.6 = (s32[66]{0:T(128)S(1)}, s32[66]{0:T(128)}, u32[]{:S(2)}) copy-start(s32[66]{0:T(128)} %get-tuple-element.23.pair_ref) | copy-start | bytes 796
  76.2 2.2 %collective-permute-start.6 = (bf16[21,128,128]{2,1,0:T(8,128)(2,1)S(1)}, bf16[21,128,128]{2,1,0:T(8,128)(2,1)S(1)}, u32[]{:S(2)}, u32[]{:S(2)}) collective-permute-start(bf16[21,128,128]{2,1,0:T(8,128)(2,1)S(1)} %get-tuple-element.40), channel_id=1, source_target_pairs={{0,16},{16,0},{32,48},{48,32},{64,80},{80,64},{96,112},{112,96},{1... | collective-permute-start | bytes 2064392 | tf_op jit(solution)/shard_map/ppermute | solution.py:233
  94.5 3.0 %collective-permute-start.7 = (bf16[168,128]{1,0:T(8,128)(2,1)S(1)}, bf16[168,128]{1,0:T(8,128)(2,1)S(1)}, u32[]{:S(2)}, u32[]{:S(2)}) collective-permute-start(bf16[168,128]{1,0:T(8,128)(2,1)S(1)} %reduce_sum.12), channel_id=1, source_target_pairs={{0,32},{16,48},{32,0},{48,16},{64,96},{80,112},{96,64},{112,80},{1... | collective-permute-start | bytes 129032 | tf_op jit(solution)/shard_map/ppermute | solution.py:233
  97.4 6.7 %collective-permute-start.8 = (bf16[168,128]{1,0:T(8,128)(2,1)S(1)}, bf16[168,128]{1,0:T(8,128)(2,1)S(1)}, u32[]{:S(2)}, u32[]{:S(2)}) collective-permute-start(bf16[168,128]{1,0:T(8,128)(2,1)S(1)} %add_convert_fusion.3), channel_id=1, source_target_pairs={{0,64},{16,80},{32,96},{48,112},{64,0},{80,16},{96,32},{112,48},{1... | collective-permute-start | bytes 129032 | tf_op jit(solution)/shard_map/ppermute | solution.py:233
  104.1 6.9 %collective-permute-start.9 = (bf16[168,128]{1,0:T(8,128)(2,1)S(1)}, bf16[168,128]{1,0:T(8,128)(2,1)S(1)}, u32[]{:S(2)}, u32[]{:S(2)}) collective-permute-start(bf16[168,128]{1,0:T(8,128)(2,1)S(1)} %add_convert_fusion.2), channel_id=1, source_target_pairs={{0,128},{16,144},{32,160},{48,176},{64,192},{80,208},{96,224},{112... | collective-permute-start | bytes 129032 | tf_op jit(solution)/shard_map/ppermute | solution.py:233
  124.3 7.7 %collective-permute-start.10 = (bf16[21,128,128]{2,1,0:T(8,128)(2,1)S(1)}, bf16[21,128,128]{2,1,0:T(8,128)(2,1)S(1)}, u32[]{:S(2)}, u32[]{:S(2)}) collective-permute-start(bf16[21,128,128]{2,1,0:T(8,128)(2,1)S(1)} %bitcast.16), channel_id=1, source_target_pairs={{0,16},{16,0},{32,48},{48,32},{64,80},{80,64},{96,112},{112,96},{1... | collective-permute-start | bytes 2064392 | tf_op jit(solution)/shard_map/ppermute | solution.py:233

commit v3 on v2

v3 whole, which is shorter than its diff:
```python
import functools

import jax
import jax.numpy as jnp
from jax import lax
from jax.experimental import pallas as pl
from jax.experimental.pallas import tpu as pltpu
from jax.sharding import PartitionSpec as P

HB = 8
BS = 128
NINT = 8
TILE = 128
PAIRS = 42
HALF = PAIRS // 2
REACH = 4
VMEM = pltpu.VMEM
SMEM = pltpu.SMEM
F32 = jnp.float32
BF16 = jnp.bfloat16


def vmem(count):
    return [pl.BlockSpec(memory_space=VMEM)] * count


def smem(count):
    return [pl.BlockSpec(memory_space=SMEM)] * count


def call(kernel, outs, scalars, arrays, scratch=(), flops=0, limit=24 << 20):
    moved = sum(a.size * a.dtype.itemsize for a in (*arrays, *outs))
    return pl.pallas_call(
        kernel,
        out_shape=tuple(outs),
        in_specs=smem(len(scalars)) + vmem(len(arrays)),
        out_specs=tuple(vmem(len(outs))),
        scratch_shapes=list(scratch),
        compiler_params=pltpu.CompilerParams(vmem_limit_bytes=limit),
        cost_estimate=pl.CostEstimate(flops=flops, bytes_accessed=moved, transcendentals=0),
    )(*scalars, *arrays)


def shape(dims, dtype=BF16):
    return jax.ShapeDtypeStruct(dims, dtype)


def table_kernel(where_ref, turned_ref, width_ref, interval_ref, near_ref, far_ref, pair_ref, list_ref):
    slots, blocks = turned_ref.shape
    first, total, cut = where_ref[0], where_ref[1], where_ref[2]
    edge = blocks // 3

    def one_row(b, _):
        line = jnp.where(b < edge, b, b - edge)
        outer = (b < edge) | (b >= 2 * edge)

        @pl.when(outer)
        def _():
            for k in range(edge):
                far_ref[line, k] = edge

        found = jnp.int32(0)
        for n in range(slots):
            away = turned_ref[n, b] - first
            away = jnp.where(away < -HB, away + total, away)
            away = jnp.where(away >= total - HB, away - total, away)
            local = (away >= 0) & (away < blocks)
            near_ref[n, b] = jnp.where(local, away, blocks)
            halo = jnp.where(away < 0, away + HB, away - blocks)

            @pl.when(jnp.logical_not(local))
            def _():
                far_ref[line, found] = n * 16 + halo

            found += jnp.where(local, 0, 1)
        return 0

    lax.fori_loop(0, blocks, one_row, 0)
    tiles = (pair_ref.shape[0] - 2) // REACH
    ends = []
    end = jnp.int32(0)
    for s in range(width_ref.shape[0]):
        end += width_ref[s] // TILE
        ends.append(end)

    def slice_of(t):
        index = jnp.int32(0)
        for end in ends:
            index += jnp.where(t >= end, 1, 0)
        return index

    lanes = [slice_of(t) for t in range(tiles)]
    slot = jnp.int32(0)
    for m in range(PAIRS + 1):
        list_ref[m] = 0
    for i in range(tiles):
        for d in range(REACH):
            if i + d < tiles:
                valid = lanes[i + d] - lanes[i] <= 1
                pair_ref[i * REACH + d] = jnp.where(valid, slot, PAIRS)
                list_ref[jnp.where(valid, slot, PAIRS)] = i * REACH + d
                slot += jnp.where(valid, 1, 0)
            else:
                pair_ref[i * REACH + d] = PAIRS
    pair_ref[tiles * REACH] = where_ref[3]
    pair_ref[tiles * REACH + 1] = interval_ref[slice_of(cut)]


def turn_kernel(start_ref, out_ref, tiles_ref, read, written):
    tiles = out_ref.shape[0]

    def load(t):
        return pltpu.make_async_copy(
            start_ref.at[:, t * TILE : (t + 1) * TILE], tiles_ref.at[t], read.at[t]
        )

    def store(t):
        return pltpu.make_async_copy(tiles_ref.at[t], out_ref.at[t], written.at[t])

    for t in range(tiles):
        load(t).start()
    for t in range(tiles):
        load(t).wait()
        store(t).start()
    for t in range(tiles):
        store(t).wait()


def near_kernel(scale, near_ref, pair_ref, ham_ref, inner_ref, mid_ref, outer_ref, *rest):
    first = scale == 1
    blocks, slots = ham_ref.shape[:2]
    if first:
        mid_out, edge_out, ham_out, stack, loaded = rest
        chunk = blocks // loaded.shape[0]

        def load(c):
            rows = slice(c * chunk, (c + 1) * chunk)
            return pltpu.make_async_copy(ham_ref.at[rows], ham_out.at[rows], loaded.at[c])

        for c in range(blocks // chunk):
            load(c).start()
        ham = ham_out
    else:
        mid_out, edge_out, before, stack = rest[-4:]
        ham = ham_ref
    third = blocks // 3
    span = third * BS
    core = pair_ref[pair_ref.shape[0] - 2]
    inner_at, outer_at = (1 - core) * 2 * span, core * 2 * span

    def spread(inner, mid, outer, into):
        into[pl.ds(pl.multiple_of(inner_at, span), span)] = inner[...]
        into[pl.ds(pl.multiple_of(outer_at, span), span)] = outer[...]
        into[span : 2 * span] = mid[...]

    spread(inner_ref, mid_ref, outer_ref, stack)
    stack[blocks * BS :] = jnp.zeros((BS, TILE), BF16)
    if not first:
        spread(*rest[:3], before)
    centre = -0.5 + pair_ref[pair_ref.shape[0] - 1].astype(F32) * F32(1 / (NINT - 1))

    def tile_at(n, b):
        return stack[pl.ds(pl.multiple_of(near_ref[n, b] * BS, BS), BS), :]

    for b in range(blocks):
        if first and b % chunk == 0:
            load(b // chunk).wait()
        total = jnp.zeros((BS, TILE), F32)
        for n in range(0, slots, 2):
            if n + 1 < slots:
                left = jnp.concatenate([ham[b, n], ham[b, n + 1]], axis=1)
                right = jnp.concatenate([tile_at(n, b), tile_at(n + 1, b)], axis=0)
            else:
                left, right = ham[b, n], tile_at(n, b)
            total += jnp.dot(left, right, preferred_element_type=F32)
        part = b // third
        here = slice((b - part * third) * BS, (b - part * third + 1) * BS)
        own = stack[b * BS : (b + 1) * BS].astype(F32)
        value = total - centre * own
        if not first:
            value = scale * value - before[b * BS : (b + 1) * BS].astype(F32)
        if part == 1:
            mid_out[here, :] = value.astype(BF16)
        else:
            edge_out[part // 2, here, :] = value


def add_halo(scale, far_ref, ham_ref, stack, edge_ref, side, k, edge):
    index = k + side * (edge - 1 - 2 * k)
    b = k + side * (3 * edge - 1 - 2 * k)
    left, right = [], []
    for slot_at in range(edge - k):
        entry = far_ref[side * edge + index, slot_at]
        slot = entry // 16
        left.append(ham_ref[b, slot])
        start = pl.multiple_of((entry - slot * 16) * BS, BS)
        right.append(stack[pl.ds(start, BS), :])
    here = pl.ds(pl.multiple_of(index * BS, BS), BS)
    total = edge_ref[side, here, :]
    for slot_at in range(0, edge - k, 2):
        lhs = jnp.concatenate(left[slot_at : slot_at + 2], axis=1)
        rhs = jnp.concatenate(right[slot_at : slot_at + 2], axis=0)
        total += scale * jnp.dot(lhs, rhs, preferred_element_type=F32)
    return index, total.astype(BF16)


def edge_kernel(scale, outer, far_ref, pair_ref, ham_ref, halo_ref, edge_ref, out_ref, stack):
    span = halo_ref.shape[0]
    edge = span // BS
    core = pair_ref[pair_ref.shape[0] - 2]
    side = core if outer else 1 - core
    stack[:span] = halo_ref[...]
    stack[span:] = jnp.zeros((BS, TILE), BF16)
    for k in range(edge):
        index, value = add_halo(scale, far_ref, ham_ref, stack, edge_ref, side, k, edge)
        out_ref[pl.ds(pl.multiple_of(index * BS, BS), BS), :] = value


def joined_kernel(scale, far_ref, pair_ref, ham_ref, inner_ref, outer_ref, edge_ref, mid_ref, out_ref, stack):
    span = inner_ref.shape[0]
    edge = span // BS
    core = pair_ref[pair_ref.shape[0] - 2]
    for side, ref in ((1 - core, inner_ref), (core, outer_ref)):
        stack[side, :span] = ref[...]
        stack[side, span:] = jnp.zeros((BS, TILE), BF16)
    out_ref[span : 2 * span, :] = mid_ref[...]
    for side in range(2):
        for k in range(edge):
            index, value = add_halo(
                scale, far_ref, ham_ref, stack.at[side], edge_ref, side, k, edge
            )
            at = side * 2 * span + index * BS
            out_ref[at : at + BS, :] = value


def gram_kernel(keep, pair_ref, list_ref, field_ref, out_ref, turned):
    tiles = field_ref.shape[0]
    core = pair_ref[tiles * REACH]
    first = (core if keep else 1 - core) * HALF
    for t in range(tiles):
        turned[t] = field_ref[t].T
    for m in range(HALF):
        code = list_ref[first + m]
        low = code // REACH
        high = low + code - low * REACH
        block = jnp.dot(turned[low], field_ref[high], preferred_element_type=F32)
        out_ref[m] = block.astype(out_ref.dtype)


def correct_kernel(rows_all, pair_ref, field_ref, mine_ref, other_ref, out_ref, gram, scaled, norm):
    tiles = field_ref.shape[0]
    core = pair_ref[tiles * REACH]
    gram[pl.ds(core * HALF, HALF)] = mine_ref[...]
    gram[pl.ds(HALF - core * HALF, HALF)] = other_ref[...]
    gram[PAIRS] = jnp.zeros((TILE, TILE), BF16)
    at_row = lax.broadcasted_iota(jnp.int32, (TILE, TILE), 0)
    at_col = lax.broadcasted_iota(jnp.int32, (TILE, TILE), 1)
    eye = at_row == at_col
    for t in range(tiles):
        block = gram[pair_ref[t * REACH]].astype(F32)
        squares = jnp.sum(jnp.where(eye, block, 0.0), axis=0, keepdims=True)
        inverse = lax.rsqrt(squares / rows_all + 1e-05)
        norm[t : t + 1, :] = inverse
        scaled[t] = (field_ref[t].astype(F32) * (inverse * inverse)).astype(BF16)
    for j in range(tiles):
        below = range(max(0, j - REACH + 1), j + 1)
        left = jnp.concatenate([scaled[i] for i in below], axis=1)
        right = jnp.concatenate([gram[pair_ref[i * REACH + j - i]] for i in below], axis=0)
        total = jnp.dot(left, right, preferred_element_type=F32)
        above = range(j + 1, min(tiles, j + REACH))
        if above:
            left = jnp.concatenate([scaled[i] for i in above], axis=1)
            right = jnp.concatenate([gram[pair_ref[j * REACH + i - j]] for i in above], axis=1)
            total += lax.dot_general(
                left, right, (((1,), (1,)), ((), ())), preferred_element_type=F32
            )
        value = norm[j : j + 1, :] * (1.5 * field_ref[j].astype(F32) - (0.5 / rows_all) * total)
        out_ref[:, j * TILE : (j + 1) * TILE] = value.astype(BF16)


def shift(array, distance):
    size = lax.axis_size("row")
    return lax.ppermute(array, "row", [(i, (i + distance) % size) for i in range(size)])


def exchange(array):
    return lax.ppermute(array, "row", [(i, i ^ 1) for i in range(lax.axis_size("row"))])


def swap_outer(array):
    size = lax.axis_size("row")
    return lax.ppermute(array, "row", [(i, (i - 1 + 2 * (i % 2)) % size) for i in range(size)])


def ring_total(piece):
    own = piece.astype(F32)
    pair = own + shift(piece, -2).astype(F32)
    three = pair + shift(piece, 2).astype(F32)
    after = shift(three.astype(BF16), -6).astype(F32)
    before = shift(pair.astype(BF16), 6).astype(F32)
    return three + after + before


def body(ham_blocks, neighbors, slice_widths, interval_index, start_vectors):
    rows_mine, columns = start_vectors.shape
    tiles = columns // TILE
    blocks, slots = ham_blocks.shape[:2]
    row_count = lax.axis_size("row")
    rows_all = blocks * BS * row_count
    panel_rows = blocks * BS
    span = panel_rows // 3
    turned = pl.pallas_call(
        turn_kernel,
        out_shape=shape((tiles, rows_mine, TILE)),
        in_specs=[pl.BlockSpec(memory_space=pltpu.HBM)],
        out_specs=pl.BlockSpec(memory_space=pltpu.HBM),
        scratch_shapes=[
            VMEM((tiles, rows_mine, TILE), BF16),
            pltpu.SemaphoreType.DMA((tiles,)),
            pltpu.SemaphoreType.DMA((tiles,)),
        ],
        compiler_params=pltpu.CompilerParams(vmem_limit_bytes=62 << 20),
    )(start_vectors)
    panel = lax.all_to_all(turned, "cuts", 0, 0).reshape(panel_rows, TILE)

    row = lax.axis_index("row")
    place = jnp.stack(
        [row * blocks, jnp.int32(blocks * row_count), lax.axis_index("cuts"), row % 2]
    ).astype(jnp.int32)
    near, far, pair, listed = pl.pallas_call(
        table_kernel,
        out_shape=(
            shape((slots, blocks), jnp.int32),
            shape((2 * blocks // 3, HB), jnp.int32),
            shape((tiles * REACH + 2,), jnp.int32),
            shape((PAIRS + 1,), jnp.int32),
        ),
        in_specs=smem(4),
        out_specs=tuple(smem(4)),
        compiler_params=pltpu.CompilerParams(vmem_limit_bytes=1 << 20),
        cost_estimate=pl.CostEstimate(flops=1 << 20, bytes_accessed=1 << 12, transcendentals=0),
    )(place, neighbors.T, slice_widths, interval_index)
    panel, near, far, pair, listed = lax.optimization_barrier((panel, near, far, pair, listed))
    work = 2 * blocks * slots * BS * BS * TILE
    outs = [shape((span, TILE)), shape((2, span, TILE), F32)]
    stacks = [VMEM((panel_rows, TILE), BF16), VMEM((panel_rows + BS, TILE), BF16)]

    def halos(inner, outer):
        from_outer = swap_outer(outer)
        return exchange(inner), from_outer

    def apply_first(field):
        inner, mid, outer = field
        from_inner, from_outer = halos(inner, outer)
        mid, edges, ham = pl.pallas_call(
            functools.partial(near_kernel, 1),
            out_shape=(*outs, shape(ham_blocks.shape)),
            in_specs=smem(2) + [pl.BlockSpec(memory_space=pltpu.HBM)] + vmem(3),
            out_specs=tuple(vmem(3)),
            scratch_shapes=[stacks[1], pltpu.SemaphoreType.DMA((blocks // 3,))],
            compiler_params=pltpu.CompilerParams(vmem_limit_bytes=40 << 20),
            cost_estimate=pl.CostEstimate(
                flops=work, bytes_accessed=ham_blocks.size * 2, transcendentals=0
            ),
        )(near, pair, ham_blocks, inner, mid, outer)
        ham = pltpu.with_memory_space_constraint(ham, VMEM)
        return ham, (from_inner, from_outer, edges, mid)

    def apply_next(ham, field, before):
        inner, mid, outer = field
        from_inner, from_outer = halos(inner, outer)
        mid, edges = call(
            functools.partial(near_kernel, 2),
            outs,
            [near, pair],
            [ham, inner, mid, outer, *before],
            stacks,
            work,
        )
        return from_inner, from_outer, edges, mid

    def edges_of(scale, ham, from_inner, from_outer, edges, mid):
        def side(outer, halo):
            (out,) = call(
                functools.partial(edge_kernel, scale, outer),
                [shape((span, TILE))],
                [far, pair],
                [ham, halo, edges],
                [VMEM((span + BS, TILE), BF16)],
                work // 8,
            )
            return out

        outer = side(True, from_outer)
        return side(False, from_inner), mid, outer

    low, mid, high = (panel[q * span : (q + 1) * span] for q in range(3))
    even = row % 2 == 0
    start = (jnp.where(even, high, low), mid, jnp.where(even, low, high))
    ham, parts = apply_first(start)
    first = edges_of(1, ham, *parts)
    second = edges_of(2, ham, *apply_next(ham, first, start))
    from_inner, from_outer, edges, mid = apply_next(ham, second, first)
    (filtered,) = call(
        functools.partial(joined_kernel, 2),
        [shape((panel_rows, TILE))],
        [far, pair],
        [ham, from_inner, from_outer, edges, mid],
        [VMEM((2, span + BS, TILE), BF16)],
        work // 4,
    )

    field = lax.all_to_all(filtered.reshape(tiles, rows_mine, TILE), "cuts", 0, 0)

    def gram(keep):
        (out,) = call(
            functools.partial(gram_kernel, keep),
            [shape((HALF, TILE, TILE), F32 if keep else BF16)],
            [pair, listed],
            [field],
            [VMEM((tiles, TILE, rows_mine), BF16)],
            1 << 28,
        )
        return out

    partial = (gram(True) + exchange(gram(False)).astype(F32)).astype(BF16)
    cut_count = lax.axis_size("cuts")
    share = HALF * TILE // cut_count
    pieces = lax.all_to_all(partial.reshape(cut_count, share, TILE), "cuts", 0, 0)
    total = ring_total(jnp.sum(pieces.astype(F32), axis=0).astype(BF16))
    spread = jnp.broadcast_to(total.astype(BF16)[None], (cut_count, share, TILE))
    mine = lax.all_to_all(spread, "cuts", 0, 0).reshape(HALF, TILE, TILE)
    other = exchange(mine)
    (corrected,) = call(
        functools.partial(correct_kernel, rows_all),
        [shape((rows_mine, columns))],
        [pair],
        [field, mine, other],
        [
            VMEM((PAIRS + 1, TILE, TILE), BF16),
            VMEM((tiles, rows_mine, TILE), BF16),
            VMEM((tiles, TILE), F32),
        ],
        1 << 29,
    )
    return corrected


def solution(mesh):
    return jax.shard_map(
        body,
        mesh=mesh,
        in_specs=(P("row", None, None, None), P("row", None), P(), P(), P(("row", "cuts"), None)),
        out_specs=P(("row", "cuts"), None),
        check_vma=False,
    )
```

time: 136 us -> 128 us (0.941)
  blocking collectives: 64.6 us -> 44.7 us
  starting transfers between devices: 20.1 us -> 31.1 us
  local copies, waits for them, and re-layouts: 6.41 us -> 0.1 us
  Pallas kernels: 26.5 us -> 30.6 us
  waiting for transfers between devices: 16.2 us -> 20.3 us
    all_to_all x1 -> x0, blocking collectives: 20 us -> none  [body(): lax.all_to_all(start_vectors, 'cuts', split_axis=1, concat_axis=0, tiled=...]
    all_to_all x0 -> x1, waiting for transfers between devices: none -> 8.54 us  [body(): panel = lax.all_to_all(turned, 'cuts', 0, 0).reshape(panel_rows, TILE)]
    ppermute x5 -> x8, waiting for transfers between devices: 10.6 us -> 2.16 us  [the longest x5 2.15 us: exchange(): lax.ppermute(array, 'row', [(i, i ^ 1) for i in range(lax.axis_size('row'...]
    pallas_call x0 -> x2, Pallas kernels: none -> 7.66 us  [the longest x1 5.59 us: apply_first(): pl.pallas_call(functools.partial(near_kernel, 1), out_shape=(*outs, shape...]
    all_to_all x0 -> x1, starting transfers between devices: none -> 6.77 us  [body(): panel = lax.all_to_all(turned, 'cuts', 0, 0).reshape(panel_rows, TILE)]
    unnamed x14 -> x6, local copies, waits for them, and re-layouts: 6.07 us -> 0.01 us
    ppermute x6 -> x4, waiting for transfers between devices: 5.65 us -> 9.58 us  [shift(): lax.ppermute(array, 'row', [(i, (i + distance) % size) for i in range(siz...]
    pallas_call x8 -> x10, Pallas kernels: 22.4 us -> 18.8 us  [call(): pl.pallas_call(kernel, out_shape=tuple(outs), in_specs=smem(len(scalars))...]
  transfers between devices with their start and end apart: 11 -> 13, of which waited for: 7 -> 7; matrix products, arithmetic and copies ran while one was open for 0% -> 0% of each run, Pallas kernels for 10% -> 18%
where the time goes in v3:
time: 128 us; the launch traced here: 127 us
  blocking collectives  44.7 us (35%)
  starting transfers between devices  31.1 us (24%)
  Pallas kernels  30.6 us (24%)
  waiting for transfers between devices  20.3 us (16%)
    pallas_call x10, Pallas kernels, call(): pl.pallas_call(kernel, out_shape=tuple(outs), in_specs=smem(len(scalars))...  18.8 us
    all_to_all x1, blocking collectives, body(): lax.all_to_all(filtered.reshape(tiles, rows_mine, TILE), 'cuts', 0, 0)  16.1 us
    all_to_all x1, blocking collectives, body(): lax.all_to_all(partial.reshape(cut_count, share, TILE), 'cuts', 0, 0)  15.4 us
    all_to_all x1, blocking collectives, body(): mine = lax.all_to_all(spread, 'cuts', 0, 0).reshape(HALF, TILE, TILE)  13.2 us
    ppermute x3, starting transfers between devices, swap_outer(): lax.ppermute(array, 'row', [(i, (i - 1 + 2 * (i % 2)) % size) for i in ra...  9.74 us
    ppermute x4, waiting for transfers between devices, shift(): lax.ppermute(array, 'row', [(i, (i + distance) % size) for i in range(siz...  9.58 us
    all_to_all x1, waiting for transfers between devices, body(): panel = lax.all_to_all(turned, 'cuts', 0, 0).reshape(panel_rows, TILE)  8.54 us
    ppermute x5, starting transfers between devices, exchange(): lax.ppermute(array, 'row', [(i, i ^ 1) for i in range(lax.axis_size('row'...  7.88 us
  transfers between devices with their start and end apart: 13, of which 7 were waited for; matrix products, arithmetic and copies ran while one was open for 0% of the time, Pallas kernels for 18%

profile of v3, /device:TPU:33, one launch (start us, length us, event | category | flops | bytes accessed | tf_op | source)
XLA Modules:
  0.0 127.5 jit_solution(1175369328003798415)
XLA Ops:
  0.0 0.0 copy-start
  0.0 0.0 copy-start.1
  0.0 0.0 copy-start.2
  0.0 2.1 %shard_map.55 = bf16[16,192,128]{2,1,0:T(8,128)(2,1)} custom-call(bf16[192,2048]{1,0:T(8,128)(2,1)} %start_ref.1), custom_call_target="tpu_custom_call" | custom-call | tf_op jit(solution)/shard_map/pallas_call | solution.py:312
  2.1 6.8 %all-to-all-start = ((bf16[16,192,128]{2,1,0:T(8,128)(2,1)}), bf16[16,192,128]{2,1,0:T(8,128)(2,1)S(1)}, u32[]{:S(2)}, u32[]{:S(2)}) async-start(bf16[16,192,128]{2,1,0:T(8,128)(2,1)} %shard_map.55), calls=%async_computation | async-start | bytes 1572864 | tf_op jit(solution)/shard_map/all_to_all | solution.py:324
  8.9 0.1 pad_add_fusion.where_ref
  9.0 0.0 copy-done
  9.0 0.0 copy-done.1
  9.0 0.0 copy-done.2
  9.0 4.1 %shard_map.56 = (s32[11,24]{1,0:T(8,128)S(1)}, s32[16,8]{1,0:T(8,128)S(1)}, s32[66]{0:T(128)S(1)}, s32[43]{0:T(128)S(1)}) custom-call(s32[4]{0:T(128)S(1)} %pad_add_fusion.where_ref, s32[11,24]{1,0:T(8,128)S(1)} %bitcast.11, s32[12]{0:T(128)S(1)} %copy-done.1, s32[12]{0:T(128)S(1)} %copy-done.2), custom_call_target="tpu_custom_call" | custom-call | flops 1048576 | bytes 4096 | tf_op jit(solution)/shard_map/pallas_call | solution.py:330
  13.1 8.5 %all-to-all-done = bf16[16,192,128]{2,1,0:T(8,128)(2,1)S(1)} async-done(((bf16[16,192,128]{2,1,0:T(8,128)(2,1)}), bf16[16,192,128]{2,1,0:T(8,128)(2,1)S(1)}, u32[]{:S(2)}, u32[]{:S(2)}) %all-to-all-start) | async-done | bytes 786464 | tf_op jit(solution)/shard_map/all_to_all | solution.py:324
  21.7 0.1 broadcast_select_fusion
  21.7 4.2 %collective-permute-start.2 = (bf16[1024,128]{1,0:T(8,128)(2,1)S(1)}, bf16[1024,128]{1,0:T(8,128)(2,1)S(1)}, u32[]{:S(2)}, u32[]{:S(2)}) collective-permute-start(bf16[1024,128]{1,0:T(8,128)(2,1)S(1)} %get-tuple-element.37.outer_ref.rest_2_), channel_id=1, source_target_pairs={{0,240},{16,32},{32,16},{48,64},{64,48},{80,96},{96,80},{112,128},... | collective-permute-start | bytes 786440 | tf_op jit(solution)/shard_map/ppermute | solution.py:292
  25.9 0.0 collective-permute-start
  25.9 5.6 %shard_map.57 = (bf16[1024,128]{1,0:T(8,128)(2,1)S(1)}, f32[2,1024,128]{2,1,0:T(8,128)S(1)}, bf16[24,11,128,128]{3,2,1,0:T(8,128)(2,1)S(1)}) custom-call(s32[11,24]{1,0:T(8,128)S(1)} %get-tuple-element.27.near_ref, s32[66]{0:T(128)S(1)} %get-tuple-element.25.pair_ref, bf16[24,11,128,128]{3,2,1,0:T(8,128)(2,1)} %ham_ref.1, ...), custom_call_target="tpu_custom_call" | custom-call | flops 1107296256 | bytes 8650752 | tf_op jit(solution)/shard_map/pallas_call | solution.py:355
  31.5 0.0 collective-permute-done.2.halo_ref
  31.5 1.2 shard_map.59.outer_ref.rest_2_
  32.7 2.1 %collective-permute-start.4 = (bf16[1024,128]{1,0:T(8,128)(2,1)S(1)}, bf16[1024,128]{1,0:T(8,128)(2,1)S(1)}, u32[]{:S(2)}, u32[]{:S(2)}) collective-permute-start(bf16[1024,128]{1,0:T(8,128)(2,1)S(1)} %shard_map.59.outer_ref.rest_2_), channel_id=1, source_target_pairs={{0,240},{16,32},{32,16},{48,64},{64,48},{80,96},{96,80},{112,128},... | collective-permute-start | bytes 786440 | tf_op jit(solution)/shard_map/ppermute | solution.py:292
  34.8 0.0 collective-permute-done.halo_ref
  34.8 1.2 shard_map.58.inner_ref.rest_0_
  36.0 0.2 collective-permute-start.1
  36.2 3.3 %shard_map.60 = (bf16[1024,128]{1,0:T(8,128)(2,1)S(1)}, f32[2,1024,128]{2,1,0:T(8,128)S(1)}) custom-call(s32[11,24]{1,0:T(8,128)S(1)} %get-tuple-element.27.near_ref, s32[66]{0:T(128)S(1)} %get-tuple-element.25.pair_ref, bf16[24,11,128,128]{3,2,1,0:T(8,128)(2,1)S(1)} %get-tuple-element.29.ham_ref, bf16[1024,128]{1,0:T(8,128)(2,1)S(1)} %shard_map.58.inner_ref.rest_0_, ...), custom_call_target="tpu_custom_call" | custom-call | flops 1107296256 | bytes 11534336 | tf_op jit(solution)/shard_map/pallas_call | solution.py:33
  39.5 0.0 collective-permute-done.4.halo_ref
  39.5 1.2 shard_map.62.outer_ref
  40.7 3.4 %collective-permute-start.5 = (bf16[1024,128]{1,0:T(8,128)(2,1)S(1)}, bf16[1024,128]{1,0:T(8,128)(2,1)S(1)}, u32[]{:S(2)}, u32[]{:S(2)}) collective-permute-start(bf16[1024,128]{1,0:T(8,128)(2,1)S(1)} %shard_map.62.outer_ref), channel_id=1, source_target_pairs={{0,240},{16,32},{32,16},{48,64},{64,48},{80,96},{96,80},{112,128},... | collective-permute-start | bytes 786440 | tf_op jit(solution)/shard_map/ppermute | solution.py:292
  44.2 0.0 collective-permute-done.1.halo_ref
  44.2 1.2 shard_map.61.inner_ref
  45.4 0.1 collective-permute-start.3
  45.5 3.3 %shard_map.63 = (bf16[1024,128]{1,0:T(8,128)(2,1)S(1)}, f32[2,1024,128]{2,1,0:T(8,128)S(1)}) custom-call(s32[11,24]{1,0:T(8,128)S(1)} %get-tuple-element.27.near_ref, s32[66]{0:T(128)S(1)} %get-tuple-element.25.pair_ref, bf16[24,11,128,128]{3,2,1,0:T(8,128)(2,1)S(1)} %get-tuple-element.29.ham_ref, bf16[1024,128]{1,0:T(8,128)(2,1)S(1)} %shard_map.61.inner_ref, ...), custom_call_target="tpu_custom_call" | custom-call | flops 1107296256 | bytes 11534336 | tf_op jit(solution)/shard_map/pallas_call | solution.py:33
  48.8 0.0 collective-permute-done.5.outer_ref
  48.8 0.0 collective-permute-done.3.inner_ref
  48.8 1.6 %shard_map.64 = bf16[3072,128]{1,0:T(8,128)(2,1)S(1)} custom-call(s32[16,8]{1,0:T(8,128)S(1)} %get-tuple-element.26.far_ref, s32[66]{0:T(128)S(1)} %get-tuple-element.25.pair_ref, bf16[24,11,128,128]{3,2,1,0:T(8,128)(2,1)S(1)} %get-tuple-element.29.ham_ref, bf16[1024,128]{1,0:T(8,128)(2,1)S(1)} %collective-permute-done.3.inner_ref, ...), custom_call_target="tpu_custom_call" | custom-call | flops 276824064 | bytes 11272192 | tf_op jit(solution)/shard_map/pallas_call | solution.py:33
  50.4 16.1 %all_to_all.20.field_ref = bf16[16,192,128]{2,1,0:T(8,128)(2,1)S(1)} all-to-all(bf16[16,192,128]{2,1,0:T(8,128)(2,1)S(1)} %bitcast.8), channel_id=1, replica_groups=mesh['row'=16,'cuts'=16] {'cuts'}, dimensions={0} | all-to-all | bytes 1572864 | tf_op jit(solution)/shard_map/all_to_all | solution.py:413
  66.5 1.4 %shard_map.66 = bf16[21,128,128]{2,1,0:T(8,128)(2,1)S(1)} custom-call(s32[66]{0:T(128)S(1)} %get-tuple-element.25.pair_ref, s32[43]{0:T(128)S(1)} %get-tuple-element.36.list_ref, bf16[16,192,128]{2,1,0:T(8,128)(2,1)S(1)} %all_to_all.20.field_ref), custom_call_target="tpu_custom_call" | custom-call | flops 268435456 | bytes 1474560 | tf_op jit(solution)/shard_map/pallas_call | solution.py:33
  67.9 1.9 %collective-permute-start.6 = (bf16[21,128,128]{2,1,0:T(8,128)(2,1)S(1)}, bf16[21,128,128]{2,1,0:T(8,128)(2,1)S(1)}, u32[]{:S(2)}, u32[]{:S(2)}) collective-permute-start(bf16[21,128,128]{2,1,0:T(8,128)(2,1)S(1)} %shard_map.66), channel_id=1, source_target_pairs={{0,16},{16,0},{32,48},{48,32},{64,80},{80,64},{96,112},{112,96},{1... | collective-permute-start | bytes 2064392 | tf_op jit(solution)/shard_map/ppermute | solution.py:287
  69.8 1.4 %shard_map.65 = f32[21,128,128]{2,1,0:T(8,128)S(1)} custom-call(s32[66]{0:T(128)S(1)} %get-tuple-element.25.pair_ref, s32[43]{0:T(128)S(1)} %get-tuple-element.36.list_ref, bf16[16,192,128]{2,1,0:T(8,128)(2,1)S(1)} %all_to_all.20.field_ref), custom_call_target="tpu_custom_call" | custom-call | flops 268435456 | bytes 2162688 | tf_op jit(solution)/shard_map/pallas_call | solution.py:33
  71.2 0.4 collective-permute-done.6
  71.6 0.2 add_convert_fusion
  71.8 15.4 %all_to_all.21 = bf16[16,168,128]{2,1,0:T(8,128)(2,1)S(1)} all-to-all(bf16[16,168,128]{2,1,0:T(8,128)(2,1)S(1)} %bitcast.13), channel_id=1, replica_groups=mesh['row'=16,'cuts'=16] {'cuts'}, dimensions={0} | all-to-all | bytes 1376256 | tf_op jit(solution)/shard_map/all_to_all | solution.py:429
  87.2 0.1 reduce_sum.12
  87.3 1.6 %collective-permute-start.7 = (bf16[168,128]{1,0:T(8,128)(2,1)S(1)}, bf16[168,128]{1,0:T(8,128)(2,1)S(1)}, u32[]{:S(2)}, u32[]{:S(2)}) collective-permute-start(bf16[168,128]{1,0:T(8,128)(2,1)S(1)} %reduce_sum.12), channel_id=1, source_target_pairs={{0,224},{16,240},{32,0},{48,16},{64,32},{80,48},{96,64},{112,80},{... | collective-permute-start | bytes 129032 | tf_op jit(solution)/shard_map/ppermute | solution.py:283
  88.9 0.0 collective-permute-start.8
  88.9 1.3 %collective-permute-done.7 = bf16[168,128]{1,0:T(8,128)(2,1)S(1)} collective-permute-done((bf16[168,128]{1,0:T(8,128)(2,1)S(1)}, bf16[168,128]{1,0:T(8,128)(2,1)S(1)}, u32[]{:S(2)}, u32[]{:S(2)}) %collective-permute-start.7) | collective-permute-done | bytes 43040 | tf_op jit(solution)/shard_map/ppermute | solution.py:283
  90.2 2.3 %collective-permute-done.8 = bf16[168,128]{1,0:T(8,128)(2,1)S(1)} collective-permute-done((bf16[168,128]{1,0:T(8,128)(2,1)S(1)}, bf16[168,128]{1,0:T(8,128)(2,1)S(1)}, u32[]{:S(2)}, u32[]{:S(2)}) %collective-permute-start.8) | collective-permute-done | bytes 43040 | tf_op jit(solution)/shard_map/ppermute | solution.py:283
  92.6 5.1 %collective-permute-start.10 = (bf16[168,128]{1,0:T(8,128)(2,1)S(1)}, bf16[168,128]{1,0:T(8,128)(2,1)S(1)}, u32[]{:S(2)}, u32[]{:S(2)}) collective-permute-start(bf16[168,128]{1,0:T(8,128)(2,1)S(1)} %get-tuple-element.41), channel_id=1, source_target_pairs={{0,96},{16,112},{32,128},{48,144},{64,160},{80,176},{96,192},{112,... | collective-permute-start | bytes 129032 | tf_op jit(solution)/shard_map/ppermute | solution.py:283
  97.7 0.0 collective-permute-start.9
  97.7 1.1 collective-permute-done.10
  98.8 4.8 %collective-permute-done.9 = bf16[168,128]{1,0:T(8,128)(2,1)S(1)} collective-permute-done((bf16[168,128]{1,0:T(8,128)(2,1)S(1)}, bf16[168,128]{1,0:T(8,128)(2,1)S(1)}, u32[]{:S(2)}, u32[]{:S(2)}) %collective-permute-start.9) | collective-permute-done | bytes 43040 | tf_op jit(solution)/shard_map/ppermute | solution.py:283
  103.7 0.1 broadcast_in_dim.2
  103.8 13.2 %all_to_all.22 = bf16[16,168,128]{2,1,0:T(8,128)(2,1)S(1)} all-to-all(bf16[16,168,128]{2,1,0:T(8,128)(2,1)S(1)} %broadcast_in_dim.2), channel_id=1, replica_groups=mesh['row'=16,'cuts'=16] {'cuts'}, dimensions={0} | all-to-all | bytes 1376256 | tf_op jit(solution)/shard_map/all_to_all | solution.py:432
  116.9 5.7 %collective-permute-start.11 = (bf16[21,128,128]{2,1,0:T(8,128)(2,1)S(1)}, bf16[21,128,128]{2,1,0:T(8,128)(2,1)S(1)}, u32[]{:S(2)}, u32[]{:S(2)}) collective-permute-start(bf16[21,128,128]{2,1,0:T(8,128)(2,1)S(1)} %bitcast.9), channel_id=1, source_target_pairs={{0,16},{16,0},{32,48},{48,32},{64,80},{80,64},{96,112},{112,96},{1... | collective-permute-start | bytes 2064392 | tf_op jit(solution)/shard_map/ppermute | solution.py:287
  122.7 1.8 %collective-permute-done.11.other_ref = bf16[21,128,128]{2,1,0:T(8,128)(2,1)S(1)} collective-permute-done((bf16[21,128,128]{2,1,0:T(8,128)(2,1)S(1)}, bf16[21,128,128]{2,1,0:T(8,128)(2,1)S(1)}, u32[]{:S(2)}, u32[]{:S(2)}) %collective-permute-start.11) | collective-permute-done | bytes 688160 | tf_op jit(solution)/shard_map/ppermute | solution.py:287
  124.4 3.0 %shard_map.67 = bf16[192,2048]{1,0:T(8,128)(2,1)} custom-call(s32[66]{0:T(128)S(1)} %get-tuple-element.25.pair_ref, bf16[16,192,128]{2,1,0:T(8,128)(2,1)S(1)} %all_to_all.20.field_ref, bf16[21,128,128]{2,1,0:T(8,128)(2,1)S(1)} %bitcast.10, bf16[21,128,128]{2,1,0:T(8,128)(2,1)S(1)} %collective-permute-done.11.other_ref), custom_call_target="tpu_custom_call" | custom-call | flops 536870912 | bytes 2949120 | tf_op jit(solution)/shard_map/pallas_call | solution.py:33
  (2 shorter events, 0.1 us)
Async XLA Ops:
  0.0 9.0 %copy-start = (s32[24,11]{0,1:T(8,128)S(1)}, s32[24,11]{0,1:T(8,128)}, u32[]{:S(2)}) copy-start(s32[24,11]{0,1:T(8,128)} %param.6) | copy-start | bytes 3172
  0.0 9.0 %copy-start.1 = (s32[12]{0:T(128)S(1)}, s32[12]{0:T(128)}, u32[]{:S(2)}) copy-start(s32[12]{0:T(128)} %width_ref.1) | copy-start | bytes 148
  0.0 9.0 %copy-start.2 = (s32[12]{0:T(128)S(1)}, s32[12]{0:T(128)}, u32[]{:S(2)}) copy-start(s32[12]{0:T(128)} %interval_ref.1) | copy-start | bytes 148
  2.1 19.6 %all-to-all-start = ((bf16[16,192,128]{2,1,0:T(8,128)(2,1)}), bf16[16,192,128]{2,1,0:T(8,128)(2,1)S(1)}, u32[]{:S(2)}, u32[]{:S(2)}) async-start(bf16[16,192,128]{2,1,0:T(8,128)(2,1)} %shard_map.55), calls=%async_computation | async-start | bytes 1572864 | tf_op jit(solution)/shard_map/all_to_all | solution.py:324
  21.7 9.8 %collective-permute-start.2 = (bf16[1024,128]{1,0:T(8,128)(2,1)S(1)}, bf16[1024,128]{1,0:T(8,128)(2,1)S(1)}, u32[]{:S(2)}, u32[]{:S(2)}) collective-permute-start(bf16[1024,128]{1,0:T(8,128)(2,1)S(1)} %get-tuple-element.37.outer_ref.rest_2_), channel_id=1, source_target_pairs={{0,240},{16,32},{32,16},{48,64},{64,48},{80,96},{96,80},{112,128},... | collective-permute-start | bytes 786440 | tf_op jit(solution)/shard_map/ppermute | solution.py:292
  25.9 8.9 %collective-permute-start = (bf16[1024,128]{1,0:T(8,128)(2,1)S(1)}, bf16[1024,128]{1,0:T(8,128)(2,1)S(1)}, u32[]{:S(2)}, u32[]{:S(2)}) collective-permute-start(bf16[1024,128]{1,0:T(8,128)(2,1)S(1)} %get-tuple-element.39.inner_ref.rest_0_), channel_id=1, source_target_pairs={{0,16},{16,0},{32,48},{48,32},{64,80},{80,64},{96,112},{112,96},{1... | collective-permute-start | bytes 786440 | tf_op jit(solution)/shard_map/ppermute | solution.py:287
  32.7 6.8 %collective-permute-start.4 = (bf16[1024,128]{1,0:T(8,128)(2,1)S(1)}, bf16[1024,128]{1,0:T(8,128)(2,1)S(1)}, u32[]{:S(2)}, u32[]{:S(2)}) collective-permute-start(bf16[1024,128]{1,0:T(8,128)(2,1)S(1)} %shard_map.59.outer_ref.rest_2_), channel_id=1, source_target_pairs={{0,240},{16,32},{32,16},{48,64},{64,48},{80,96},{96,80},{112,128},... | collective-permute-start | bytes 786440 | tf_op jit(solution)/shard_map/ppermute | solution.py:292
  36.0 8.1 %collective-permute-start.1 = (bf16[1024,128]{1,0:T(8,128)(2,1)S(1)}, bf16[1024,128]{1,0:T(8,128)(2,1)S(1)}, u32[]{:S(2)}, u32[]{:S(2)}) collective-permute-start(bf16[1024,128]{1,0:T(8,128)(2,1)S(1)} %shard_map.58.inner_ref.rest_0_), channel_id=1, source_target_pairs={{0,16},{16,0},{32,48},{48,32},{64,80},{80,64},{96,112},{112,96},{1... | collective-permute-start | bytes 786440 | tf_op jit(solution)/shard_map/ppermute | solution.py:287
  40.7 8.1 %collective-permute-start.5 = (bf16[1024,128]{1,0:T(8,128)(2,1)S(1)}, bf16[1024,128]{1,0:T(8,128)(2,1)S(1)}, u32[]{:S(2)}, u32[]{:S(2)}) collective-permute-start(bf16[1024,128]{1,0:T(8,128)(2,1)S(1)} %shard_map.62.outer_ref), channel_id=1, source_target_pairs={{0,240},{16,32},{32,16},{48,64},{64,48},{80,96},{96,80},{112,128},... | collective-permute-start | bytes 786440 | tf_op jit(solution)/shard_map/ppermute | solution.py:292
  45.4 3.4 %collective-permute-start.3 = (bf16[1024,128]{1,0:T(8,128)(2,1)S(1)}, bf16[1024,128]{1,0:T(8,128)(2,1)S(1)}, u32[]{:S(2)}, u32[]{:S(2)}) collective-permute-start(bf16[1024,128]{1,0:T(8,128)(2,1)S(1)} %shard_map.61.inner_ref), channel_id=1, source_target_pairs={{0,16},{16,0},{32,48},{48,32},{64,80},{80,64},{96,112},{112,96},{1... | collective-permute-start | bytes 786440 | tf_op jit(solution)/shard_map/ppermute | solution.py:287
  67.9 3.7 %collective-permute-start.6 = (bf16[21,128,128]{2,1,0:T(8,128)(2,1)S(1)}, bf16[21,128,128]{2,1,0:T(8,128)(2,1)S(1)}, u32[]{:S(2)}, u32[]{:S(2)}) collective-permute-start(bf16[21,128,128]{2,1,0:T(8,128)(2,1)S(1)} %shard_map.66), channel_id=1, source_target_pairs={{0,16},{16,0},{32,48},{48,32},{64,80},{80,64},{96,112},{112,96},{1... | collective-permute-start | bytes 2064392 | tf_op jit(solution)/shard_map/ppermute | solution.py:287
  87.3 3.0 %collective-permute-start.7 = (bf16[168,128]{1,0:T(8,128)(2,1)S(1)}, bf16[168,128]{1,0:T(8,128)(2,1)S(1)}, u32[]{:S(2)}, u32[]{:S(2)}) collective-permute-start(bf16[168,128]{1,0:T(8,128)(2,1)S(1)} %reduce_sum.12), channel_id=1, source_target_pairs={{0,224},{16,240},{32,0},{48,16},{64,32},{80,48},{96,64},{112,80},{... | collective-permute-start | bytes 129032 | tf_op jit(solution)/shard_map/ppermute | solution.py:283
  88.9 3.7 %collective-permute-start.8 = (bf16[168,128]{1,0:T(8,128)(2,1)S(1)}, bf16[168,128]{1,0:T(8,128)(2,1)S(1)}, u32[]{:S(2)}, u32[]{:S(2)}) collective-permute-start(bf16[168,128]{1,0:T(8,128)(2,1)S(1)} %reduce_sum.12), channel_id=1, source_target_pairs={{0,32},{16,48},{32,64},{48,80},{64,96},{80,112},{96,128},{112,144}... | collective-permute-start | bytes 129032 | tf_op jit(solution)/shard_map/ppermute | solution.py:283
  92.6 6.2 %collective-permute-start.10 = (bf16[168,128]{1,0:T(8,128)(2,1)S(1)}, bf16[168,128]{1,0:T(8,128)(2,1)S(1)}, u32[]{:S(2)}, u32[]{:S(2)}) collective-permute-start(bf16[168,128]{1,0:T(8,128)(2,1)S(1)} %get-tuple-element.41), channel_id=1, source_target_pairs={{0,96},{16,112},{32,128},{48,144},{64,160},{80,176},{96,192},{112,... | collective-permute-start | bytes 129032 | tf_op jit(solution)/shard_map/ppermute | solution.py:283
  97.7 5.9 %collective-permute-start.9 = (bf16[168,128]{1,0:T(8,128)(2,1)S(1)}, bf16[168,128]{1,0:T(8,128)(2,1)S(1)}, u32[]{:S(2)}, u32[]{:S(2)}) collective-permute-start(bf16[168,128]{1,0:T(8,128)(2,1)S(1)} %get-tuple-element.40), channel_id=1, source_target_pairs={{0,160},{16,176},{32,192},{48,208},{64,224},{80,240},{96,0},{112,1... | collective-permute-start | bytes 129032 | tf_op jit(solution)/shard_map/ppermute | solution.py:283
  116.9 7.5 %collective-permute-start.11 = (bf16[21,128,128]{2,1,0:T(8,128)(2,1)S(1)}, bf16[21,128,128]{2,1,0:T(8,128)(2,1)S(1)}, u32[]{:S(2)}, u32[]{:S(2)}) collective-permute-start(bf16[21,128,128]{2,1,0:T(8,128)(2,1)S(1)} %bitcast.9), channel_id=1, source_target_pairs={{0,16},{16,0},{32,48},{48,32},{64,80},{80,64},{96,112},{112,96},{1... | collective-permute-start | bytes 2064392 | tf_op jit(solution)/shard_map/ppermute | solution.py:287

commit v4 on v3

--- a/solution.py
+++ b/solution.py
@@ -13,6 +13,7 @@
 TILE = 128
 PAIRS = 42
 HALF = PAIRS // 2
+FLIGHT = 4
 REACH = 4
 VMEM = pltpu.VMEM
 SMEM = pltpu.SMEM
@@ -76,7 +77,7 @@
         return 0
 
     lax.fori_loop(0, blocks, one_row, 0)
-    tiles = (pair_ref.shape[0] - 2) // REACH
+    tiles = pair_ref.shape[0] // REACH
     ends = []
     end = jnp.int32(0)
     for s in range(width_ref.shape[0]):
@@ -102,8 +103,11 @@
                 slot += jnp.where(valid, 1, 0)
             else:
                 pair_ref[i * REACH + d] = PAIRS
-    pair_ref[tiles * REACH] = where_ref[3]
-    pair_ref[tiles * REACH + 1] = interval_ref[slice_of(cut)]
+    core = where_ref[3]
+    pair_ref[tiles * REACH] = core
+    near_ref[slots, 0] = core
+    near_ref[slots, 1] = interval_ref[slice_of(cut)]
+    far_ref[2 * edge, 0] = core
 
 
 def turn_kernel(start_ref, out_ref, tiles_ref, read, written):
@@ -126,7 +130,7 @@
         store(t).wait()
 
 
-def near_kernel(scale, near_ref, pair_ref, ham_ref, inner_ref, mid_ref, outer_ref, *rest):
+def near_kernel(scale, near_ref, ham_ref, inner_ref, mid_ref, outer_ref, *rest):
     first = scale == 1
     blocks, slots = ham_ref.shape[:2]
     if first:
@@ -137,7 +141,7 @@
             rows = slice(c * chunk, (c + 1) * chunk)
             return pltpu.make_async_copy(ham_ref.at[rows], ham_out.at[rows], loaded.at[c])
 
-        for c in range(blocks // chunk):
+        for c in range(FLIGHT):
             load(c).start()
         ham = ham_out
     else:
@@ -145,7 +149,7 @@
         ham = ham_ref
     third = blocks // 3
     span = third * BS
-    core = pair_ref[pair_ref.shape[0] - 2]
+    core = near_ref[slots, 0]
     inner_at, outer_at = (1 - core) * 2 * span, core * 2 * span
 
     def spread(inner, mid, outer, into):
@@ -157,14 +161,17 @@
     stack[blocks * BS :] = jnp.zeros((BS, TILE), BF16)
     if not first:
         spread(*rest[:3], before)
-    centre = -0.5 + pair_ref[pair_ref.shape[0] - 1].astype(F32) * F32(1 / (NINT - 1))
+    centre = -0.5 + near_ref[slots, 1].astype(F32) * F32(1 / (NINT - 1))
 
     def tile_at(n, b):
         return stack[pl.ds(pl.multiple_of(near_ref[n, b] * BS, BS), BS), :]
 
     for b in range(blocks):
         if first and b % chunk == 0:
-            load(b // chunk).wait()
+            c = b // chunk
+            load(c).wait()
+            if c + FLIGHT < blocks // chunk:
+                load(c + FLIGHT).start()
         total = jnp.zeros((BS, TILE), F32)
         for n in range(0, slots, 2):
             if n + 1 < slots:
@@ -204,10 +211,10 @@
     return index, total.astype(BF16)
 
 
-def edge_kernel(scale, outer, far_ref, pair_ref, ham_ref, halo_ref, edge_ref, out_ref, stack):
+def edge_kernel(scale, outer, far_ref, ham_ref, halo_ref, edge_ref, out_ref, stack):
     span = halo_ref.shape[0]
     edge = span // BS
-    core = pair_ref[pair_ref.shape[0] - 2]
+    core = far_ref[2 * edge, 0]
     side = core if outer else 1 - core
     stack[:span] = halo_ref[...]
     stack[span:] = jnp.zeros((BS, TILE), BF16)
@@ -216,10 +223,10 @@
         out_ref[pl.ds(pl.multiple_of(index * BS, BS), BS), :] = value
 
 
-def joined_kernel(scale, far_ref, pair_ref, ham_ref, inner_ref, outer_ref, edge_ref, mid_ref, out_ref, stack):
+def joined_kernel(scale, far_ref, ham_ref, inner_ref, outer_ref, edge_ref, mid_ref, out_ref, stack):
     span = inner_ref.shape[0]
     edge = span // BS
-    core = pair_ref[pair_ref.shape[0] - 2]
+    core = far_ref[2 * edge, 0]
     for side, ref in ((1 - core, inner_ref), (core, outer_ref)):
         stack[side, :span] = ref[...]
         stack[side, span:] = jnp.zeros((BS, TILE), BF16)
@@ -278,9 +285,11 @@
         out_ref[:, j * TILE : (j + 1) * TILE] = value.astype(BF16)
 
 
-def shift(array, distance):
+def shift(array, chips):
     size = lax.axis_size("row")
-    return lax.ppermute(array, "row", [(i, (i + distance) % size) for i in range(size)])
+    return lax.ppermute(
+        array, "row", [(i, (i + 2 * chips * (1 - 2 * (i % 2))) % size) for i in range(size)]
+    )
 
 
 def exchange(array):
@@ -294,10 +303,10 @@
 
 def ring_total(piece):
     own = piece.astype(F32)
-    pair = own + shift(piece, -2).astype(F32)
-    three = pair + shift(piece, 2).astype(F32)
-    after = shift(three.astype(BF16), -6).astype(F32)
-    before = shift(pair.astype(BF16), 6).astype(F32)
+    pair = own + shift(piece, -1).astype(F32)
+    three = pair + shift(piece, 1).astype(F32)
+    after = shift(three.astype(BF16), -3).astype(F32)
+    before = shift(pair.astype(BF16), 3).astype(F32)
     return three + after + before
 
 
@@ -330,9 +339,9 @@
     near, far, pair, listed = pl.pallas_call(
         table_kernel,
         out_shape=(
-            shape((slots, blocks), jnp.int32),
-            shape((2 * blocks // 3, HB), jnp.int32),
-            shape((tiles * REACH + 2,), jnp.int32),
+            shape((slots + 1, blocks), jnp.int32),
+            shape((2 * blocks // 3 + 1, HB), jnp.int32),
+            shape((tiles * REACH + 1,), jnp.int32),
             shape((PAIRS + 1,), jnp.int32),
         ),
         in_specs=smem(4),
@@ -355,14 +364,14 @@
         mid, edges, ham = pl.pallas_call(
             functools.partial(near_kernel, 1),
             out_shape=(*outs, shape(ham_blocks.shape)),
-            in_specs=smem(2) + [pl.BlockSpec(memory_space=pltpu.HBM)] + vmem(3),
+            in_specs=smem(1) + [pl.BlockSpec(memory_space=pltpu.HBM)] + vmem(3),
             out_specs=tuple(vmem(3)),
-            scratch_shapes=[stacks[1], pltpu.SemaphoreType.DMA((blocks // 3,))],
+            scratch_shapes=[stacks[1], pltpu.SemaphoreType.DMA((FLIGHT,))],
             compiler_params=pltpu.CompilerParams(vmem_limit_bytes=40 << 20),
             cost_estimate=pl.CostEstimate(
                 flops=work, bytes_accessed=ham_blocks.size * 2, transcendentals=0
             ),
-        )(near, pair, ham_blocks, inner, mid, outer)
+        )(near, ham_blocks, inner, mid, outer)
         ham = pltpu.with_memory_space_constraint(ham, VMEM)
         return ham, (from_inner, from_outer, edges, mid)
 
@@ -372,7 +381,7 @@
         mid, edges = call(
             functools.partial(near_kernel, 2),
             outs,
-            [near, pair],
+            [near],
             [ham, inner, mid, outer, *before],
             stacks,
             work,
@@ -384,7 +393,7 @@
             (out,) = call(
                 functools.partial(edge_kernel, scale, outer),
                 [shape((span, TILE))],
-                [far, pair],
+                [far],
                 [ham, halo, edges],
                 [VMEM((span + BS, TILE), BF16)],
                 work // 8,
@@ -404,7 +413,7 @@
     (filtered,) = call(
         functools.partial(joined_kernel, 2),
         [shape((panel_rows, TILE))],
-        [far, pair],
+        [far],
         [ham, from_inner, from_outer, edges, mid],
         [VMEM((2, span + BS, TILE), BF16)],
         work // 4,

time: 128 us -> 127 us (level)
  waiting for transfers between devices: 20.3 us -> 17.8 us
    ppermute x4, waiting for transfers between devices: 9.58 us -> 7.21 us  [shift(): lax.ppermute(array, 'row', [(i, (i + 2 * chips * (1 - 2 * (i % 2))) % siz...]
    ppermute x5, starting transfers between devices: 7.88 us -> 9.5 us  [exchange(): lax.ppermute(array, 'row', [(i, i ^ 1) for i in range(lax.axis_size('row'...]
where the time goes in v4:
time: 127 us
  blocking collectives  45.8 us (36%)
  starting transfers between devices  31.9 us (25%)
  Pallas kernels  30.7 us (24%)
  waiting for transfers between devices  17.8 us (14%)
    pallas_call x10, Pallas kernels, call(): pl.pallas_call(kernel, out_shape=tuple(outs), in_specs=smem(len(scalars))...  19.1 us
    all_to_all x1, blocking collectives, body(): lax.all_to_all(filtered.reshape(tiles, rows_mine, TILE), 'cuts', 0, 0)  16.1 us
    all_to_all x1, blocking collectives, body(): lax.all_to_all(partial.reshape(cut_count, share, TILE), 'cuts', 0, 0)  15.4 us
    all_to_all x1, blocking collectives, body(): mine = lax.all_to_all(spread, 'cuts', 0, 0).reshape(HALF, TILE, TILE)  14.2 us
    ppermute x3, starting transfers between devices, swap_outer(): lax.ppermute(array, 'row', [(i, (i - 1 + 2 * (i % 2)) % size) for i in ra...  9.55 us
    ppermute x5, starting transfers between devices, exchange(): lax.ppermute(array, 'row', [(i, i ^ 1) for i in range(lax.axis_size('row'...  9.5 us
    all_to_all x1, waiting for transfers between devices, body(): panel = lax.all_to_all(turned, 'cuts', 0, 0).reshape(panel_rows, TILE)  8.42 us
    ppermute x4, waiting for transfers between devices, shift(): lax.ppermute(array, 'row', [(i, (i + 2 * chips * (1 - 2 * (i % 2))) % siz...  7.21 us
  transfers between devices with their start and end apart: 13, of which 7 were waited for; matrix products, arithmetic and copies ran while one was open for 0% of the time, Pallas kernels for 18%

profile of v4, /device:TPU:33, one launch (start us, length us, event | category | flops | bytes accessed | tf_op | source)
XLA Modules:
  0.0 127.0 jit_solution(14606963238899442370)
XLA Ops:
  0.0 0.0 copy-start
  0.0 0.0 copy-start.1
  0.0 0.0 copy-start.2
  0.0 2.1 %shard_map.55 = bf16[16,192,128]{2,1,0:T(8,128)(2,1)} custom-call(bf16[192,2048]{1,0:T(8,128)(2,1)} %start_ref.1), custom_call_target="tpu_custom_call" | custom-call | tf_op jit(solution)/shard_map/pallas_call | solution.py:321
  2.1 6.8 %all-to-all-start = ((bf16[16,192,128]{2,1,0:T(8,128)(2,1)}), bf16[16,192,128]{2,1,0:T(8,128)(2,1)S(1)}, u32[]{:S(2)}, u32[]{:S(2)}) async-start(bf16[16,192,128]{2,1,0:T(8,128)(2,1)} %shard_map.55), calls=%async_computation | async-start | bytes 1572864 | tf_op jit(solution)/shard_map/all_to_all | solution.py:333
  8.9 0.1 pad_add_fusion.where_ref
  9.0 0.0 copy-done
  9.0 0.0 copy-done.1
  9.0 0.0 copy-done.2
  9.0 4.3 %shard_map.56 = (s32[12,24]{1,0:T(8,128)S(1)}, s32[17,8]{1,0:T(8,128)S(1)}, s32[65]{0:T(128)S(1)}, s32[43]{0:T(128)S(1)}) custom-call(s32[4]{0:T(128)S(1)} %pad_add_fusion.where_ref, s32[11,24]{1,0:T(8,128)S(1)} %bitcast.11, s32[12]{0:T(128)S(1)} %copy-done.1, s32[12]{0:T(128)S(1)} %copy-done.2), custom_call_target="tpu_custom_call" | custom-call | flops 1048576 | bytes 4096 | tf_op jit(solution)/shard_map/pallas_call | solution.py:339
  13.3 8.4 %all-to-all-done = bf16[16,192,128]{2,1,0:T(8,128)(2,1)S(1)} async-done(((bf16[16,192,128]{2,1,0:T(8,128)(2,1)}), bf16[16,192,128]{2,1,0:T(8,128)(2,1)S(1)}, u32[]{:S(2)}, u32[]{:S(2)}) %all-to-all-start) | async-done | bytes 786464 | tf_op jit(solution)/shard_map/all_to_all | solution.py:333
  21.7 0.1 broadcast_select_fusion
  21.7 4.2 %collective-permute-start.2 = (bf16[1024,128]{1,0:T(8,128)(2,1)S(1)}, bf16[1024,128]{1,0:T(8,128)(2,1)S(1)}, u32[]{:S(2)}, u32[]{:S(2)}) collective-permute-start(bf16[1024,128]{1,0:T(8,128)(2,1)S(1)} %get-tuple-element.37.outer_ref.rest_2_), channel_id=1, source_target_pairs={{0,240},{16,32},{32,16},{48,64},{64,48},{80,96},{96,80},{112,128},... | collective-permute-start | bytes 786440 | tf_op jit(solution)/shard_map/ppermute | solution.py:301
  25.9 0.0 collective-permute-start
  25.9 5.2 %shard_map.57 = (bf16[1024,128]{1,0:T(8,128)(2,1)S(1)}, f32[2,1024,128]{2,1,0:T(8,128)S(1)}, bf16[24,11,128,128]{3,2,1,0:T(8,128)(2,1)S(1)}) custom-call(s32[12,24]{1,0:T(8,128)S(1)} %get-tuple-element.27.near_ref, bf16[24,11,128,128]{3,2,1,0:T(8,128)(2,1)} %ham_ref.1, bf16[1024,128]{1,0:T(8,128)(2,1)S(1)} %get-tuple-element.39.inner_ref.rest_0_, ...), custom_call_target="tpu_custom_call" | custom-call | flops 1107296256 | bytes 8650752 | tf_op jit(solution)/shard_map/pallas_call | solution.py:364
  31.2 0.0 collective-permute-done.2.halo_ref
  31.2 1.3 shard_map.59.outer_ref.rest_2_
  32.4 2.1 %collective-permute-start.4 = (bf16[1024,128]{1,0:T(8,128)(2,1)S(1)}, bf16[1024,128]{1,0:T(8,128)(2,1)S(1)}, u32[]{:S(2)}, u32[]{:S(2)}) collective-permute-start(bf16[1024,128]{1,0:T(8,128)(2,1)S(1)} %shard_map.59.outer_ref.rest_2_), channel_id=1, source_target_pairs={{0,240},{16,32},{32,16},{48,64},{64,48},{80,96},{96,80},{112,128},... | collective-permute-start | bytes 786440 | tf_op jit(solution)/shard_map/ppermute | solution.py:301
  34.6 0.0 collective-permute-done.halo_ref
  34.6 1.3 shard_map.58.inner_ref.rest_0_
  35.8 0.2 collective-permute-start.1
  36.0 3.3 %shard_map.60 = (bf16[1024,128]{1,0:T(8,128)(2,1)S(1)}, f32[2,1024,128]{2,1,0:T(8,128)S(1)}) custom-call(s32[12,24]{1,0:T(8,128)S(1)} %get-tuple-element.27.near_ref, bf16[24,11,128,128]{3,2,1,0:T(8,128)(2,1)S(1)} %get-tuple-element.29.ham_ref, bf16[1024,128]{1,0:T(8,128)(2,1)S(1)} %shard_map.58.inner_ref.rest_0_, ...), custom_call_target="tpu_custom_call" | custom-call | flops 1107296256 | bytes 11534336 | tf_op jit(solution)/shard_map/pallas_call | solution.py:34
  39.3 0.0 collective-permute-done.4.halo_ref
  39.3 1.3 shard_map.62.outer_ref
  40.6 3.3 %collective-permute-start.5 = (bf16[1024,128]{1,0:T(8,128)(2,1)S(1)}, bf16[1024,128]{1,0:T(8,128)(2,1)S(1)}, u32[]{:S(2)}, u32[]{:S(2)}) collective-permute-start(bf16[1024,128]{1,0:T(8,128)(2,1)S(1)} %shard_map.62.outer_ref), channel_id=1, source_target_pairs={{0,240},{16,32},{32,16},{48,64},{64,48},{80,96},{96,80},{112,128},... | collective-permute-start | bytes 786440 | tf_op jit(solution)/shard_map/ppermute | solution.py:301
  43.8 0.0 collective-permute-done.1.halo_ref
  43.8 1.3 shard_map.61.inner_ref
  45.1 0.3 collective-permute-start.3
  45.4 3.3 %shard_map.63 = (bf16[1024,128]{1,0:T(8,128)(2,1)S(1)}, f32[2,1024,128]{2,1,0:T(8,128)S(1)}) custom-call(s32[12,24]{1,0:T(8,128)S(1)} %get-tuple-element.27.near_ref, bf16[24,11,128,128]{3,2,1,0:T(8,128)(2,1)S(1)} %get-tuple-element.29.ham_ref, bf16[1024,128]{1,0:T(8,128)(2,1)S(1)} %shard_map.61.inner_ref, bf16[1024,128]{1,0:T(8,128)(2,1)S(1)} %get-tuple-element.33.mid_ref, ...), custom_call_target="tpu_custom_call" | custom-call | flops 1107296256 | bytes 11534336 | tf_op jit(solution)/shard_map/pallas_call | solution.py:34
  48.7 0.0 collective-permute-done.5.outer_ref
  48.7 0.0 collective-permute-done.3.inner_ref
  48.7 1.6 %shard_map.64 = bf16[3072,128]{1,0:T(8,128)(2,1)S(1)} custom-call(s32[17,8]{1,0:T(8,128)S(1)} %get-tuple-element.26.far_ref, bf16[24,11,128,128]{3,2,1,0:T(8,128)(2,1)S(1)} %get-tuple-element.29.ham_ref, bf16[1024,128]{1,0:T(8,128)(2,1)S(1)} %collective-permute-done.3.inner_ref, bf16[1024,128]{1,0:T(8,128)(2,1)S(1)} %collective-permute-done.5.outer_ref, ...), custom_call_target="tpu_custom_call" | custom-call | flops 276824064 | bytes 11272192 | tf_op jit(solution)/shard_map/pallas_call | solution.py:34
  50.4 16.1 %all_to_all.20.field_ref = bf16[16,192,128]{2,1,0:T(8,128)(2,1)S(1)} all-to-all(bf16[16,192,128]{2,1,0:T(8,128)(2,1)S(1)} %bitcast.8), channel_id=1, replica_groups=mesh['row'=16,'cuts'=16] {'cuts'}, dimensions={0} | all-to-all | bytes 1572864 | tf_op jit(solution)/shard_map/all_to_all | solution.py:422
  66.5 1.4 %shard_map.66 = bf16[21,128,128]{2,1,0:T(8,128)(2,1)S(1)} custom-call(s32[65]{0:T(128)S(1)} %get-tuple-element.25.pair_ref, s32[43]{0:T(128)S(1)} %get-tuple-element.36.list_ref, bf16[16,192,128]{2,1,0:T(8,128)(2,1)S(1)} %all_to_all.20.field_ref), custom_call_target="tpu_custom_call" | custom-call | flops 268435456 | bytes 1474560 | tf_op jit(solution)/shard_map/pallas_call | solution.py:34
  67.9 1.9 %collective-permute-start.6 = (bf16[21,128,128]{2,1,0:T(8,128)(2,1)S(1)}, bf16[21,128,128]{2,1,0:T(8,128)(2,1)S(1)}, u32[]{:S(2)}, u32[]{:S(2)}) collective-permute-start(bf16[21,128,128]{2,1,0:T(8,128)(2,1)S(1)} %shard_map.66), channel_id=1, source_target_pairs={{0,16},{16,0},{32,48},{48,32},{64,80},{80,64},{96,112},{112,96},{1... | collective-permute-start | bytes 2064392 | tf_op jit(solution)/shard_map/ppermute | solution.py:296
  69.8 1.4 %shard_map.65 = f32[21,128,128]{2,1,0:T(8,128)S(1)} custom-call(s32[65]{0:T(128)S(1)} %get-tuple-element.25.pair_ref, s32[43]{0:T(128)S(1)} %get-tuple-element.36.list_ref, bf16[16,192,128]{2,1,0:T(8,128)(2,1)S(1)} %all_to_all.20.field_ref), custom_call_target="tpu_custom_call" | custom-call | flops 268435456 | bytes 2162688 | tf_op jit(solution)/shard_map/pallas_call | solution.py:34
  71.2 0.4 collective-permute-done.6
  71.6 0.2 add_convert_fusion
  71.8 15.4 %all_to_all.21 = bf16[16,168,128]{2,1,0:T(8,128)(2,1)S(1)} all-to-all(bf16[16,168,128]{2,1,0:T(8,128)(2,1)S(1)} %bitcast.13), channel_id=1, replica_groups=mesh['row'=16,'cuts'=16] {'cuts'}, dimensions={0} | all-to-all | bytes 1376256 | tf_op jit(solution)/shard_map/all_to_all | solution.py:438
  87.2 0.1 reduce_sum.12
  87.3 1.4 %collective-permute-start.7 = (bf16[168,128]{1,0:T(8,128)(2,1)S(1)}, bf16[168,128]{1,0:T(8,128)(2,1)S(1)}, u32[]{:S(2)}, u32[]{:S(2)}) collective-permute-start(bf16[168,128]{1,0:T(8,128)(2,1)S(1)} %reduce_sum.12), channel_id=1, source_target_pairs={{0,224},{16,48},{32,0},{48,80},{64,32},{80,112},{96,64},{112,144},... | collective-permute-start | bytes 129032 | tf_op jit(solution)/shard_map/ppermute | solution.py:290
  88.7 0.1 collective-permute-start.8
  88.9 1.4 %collective-permute-done.7 = bf16[168,128]{1,0:T(8,128)(2,1)S(1)} collective-permute-done((bf16[168,128]{1,0:T(8,128)(2,1)S(1)}, bf16[168,128]{1,0:T(8,128)(2,1)S(1)}, u32[]{:S(2)}, u32[]{:S(2)}) %collective-permute-start.7) | collective-permute-done | bytes 43040 | tf_op jit(solution)/shard_map/ppermute | solution.py:290
  90.2 2.9 %collective-permute-done.8 = bf16[168,128]{1,0:T(8,128)(2,1)S(1)} collective-permute-done((bf16[168,128]{1,0:T(8,128)(2,1)S(1)}, bf16[168,128]{1,0:T(8,128)(2,1)S(1)}, u32[]{:S(2)}, u32[]{:S(2)}) %collective-permute-start.8) | collective-permute-done | bytes 43040 | tf_op jit(solution)/shard_map/ppermute | solution.py:290
  93.2 1.3 %collective-permute-start.10 = (bf16[168,128]{1,0:T(8,128)(2,1)S(1)}, bf16[168,128]{1,0:T(8,128)(2,1)S(1)}, u32[]{:S(2)}, u32[]{:S(2)}) collective-permute-start(bf16[168,128]{1,0:T(8,128)(2,1)S(1)} %get-tuple-element.41), channel_id=1, source_target_pairs={{0,96},{16,176},{32,128},{48,208},{64,160},{80,240},{96,192},{112,... | collective-permute-start | bytes 129032 | tf_op jit(solution)/shard_map/ppermute | solution.py:290
  94.5 3.2 %collective-permute-start.9 = (bf16[168,128]{1,0:T(8,128)(2,1)S(1)}, bf16[168,128]{1,0:T(8,128)(2,1)S(1)}, u32[]{:S(2)}, u32[]{:S(2)}) collective-permute-start(bf16[168,128]{1,0:T(8,128)(2,1)S(1)} %get-tuple-element.40), channel_id=1, source_target_pairs={{0,160},{16,112},{32,192},{48,144},{64,224},{80,176},{96,0},{112,2... | collective-permute-start | bytes 129032 | tf_op jit(solution)/shard_map/ppermute | solution.py:290
  97.7 1.4 %collective-permute-done.10 = bf16[168,128]{1,0:T(8,128)(2,1)S(1)} collective-permute-done((bf16[168,128]{1,0:T(8,128)(2,1)S(1)}, bf16[168,128]{1,0:T(8,128)(2,1)S(1)}, u32[]{:S(2)}, u32[]{:S(2)}) %collective-permute-start.10) | collective-permute-done | bytes 43040 | tf_op jit(solution)/shard_map/ppermute | solution.py:290
  99.1 1.5 %collective-permute-done.9 = bf16[168,128]{1,0:T(8,128)(2,1)S(1)} collective-permute-done((bf16[168,128]{1,0:T(8,128)(2,1)S(1)}, bf16[168,128]{1,0:T(8,128)(2,1)S(1)}, u32[]{:S(2)}, u32[]{:S(2)}) %collective-permute-start.9) | collective-permute-done | bytes 43040 | tf_op jit(solution)/shard_map/ppermute | solution.py:290
  100.7 0.1 broadcast_in_dim.2
  100.8 14.2 %all_to_all.22 = bf16[16,168,128]{2,1,0:T(8,128)(2,1)S(1)} all-to-all(bf16[16,168,128]{2,1,0:T(8,128)(2,1)S(1)} %broadcast_in_dim.2), channel_id=1, replica_groups=mesh['row'=16,'cuts'=16] {'cuts'}, dimensions={0} | all-to-all | bytes 1376256 | tf_op jit(solution)/shard_map/all_to_all | solution.py:441
  115.0 7.2 %collective-permute-start.11 = (bf16[21,128,128]{2,1,0:T(8,128)(2,1)S(1)}, bf16[21,128,128]{2,1,0:T(8,128)(2,1)S(1)}, u32[]{:S(2)}, u32[]{:S(2)}) collective-permute-start(bf16[21,128,128]{2,1,0:T(8,128)(2,1)S(1)} %bitcast.9), channel_id=1, source_target_pairs={{0,16},{16,0},{32,48},{48,32},{64,80},{80,64},{96,112},{112,96},{1... | collective-permute-start | bytes 2064392 | tf_op jit(solution)/shard_map/ppermute | solution.py:296
  122.2 1.8 %collective-permute-done.11.other_ref = bf16[21,128,128]{2,1,0:T(8,128)(2,1)S(1)} collective-permute-done((bf16[21,128,128]{2,1,0:T(8,128)(2,1)S(1)}, bf16[21,128,128]{2,1,0:T(8,128)(2,1)S(1)}, u32[]{:S(2)}, u32[]{:S(2)}) %collective-permute-start.11) | collective-permute-done | bytes 688160 | tf_op jit(solution)/shard_map/ppermute | solution.py:296
  124.0 3.0 %shard_map.67 = bf16[192,2048]{1,0:T(8,128)(2,1)} custom-call(s32[65]{0:T(128)S(1)} %get-tuple-element.25.pair_ref, bf16[16,192,128]{2,1,0:T(8,128)(2,1)S(1)} %all_to_all.20.field_ref, bf16[21,128,128]{2,1,0:T(8,128)(2,1)S(1)} %bitcast.10, bf16[21,128,128]{2,1,0:T(8,128)(2,1)S(1)} %collective-permute-done.11.other_ref), custom_call_target="tpu_custom_call" | custom-call | flops 536870912 | bytes 2949120 | tf_op jit(solution)/shard_map/pallas_call | solution.py:34
  (2 shorter events, 0.1 us)
Async XLA Ops:
  0.0 9.0 %copy-start = (s32[24,11]{0,1:T(8,128)S(1)}, s32[24,11]{0,1:T(8,128)}, u32[]{:S(2)}) copy-start(s32[24,11]{0,1:T(8,128)} %param.6) | copy-start | bytes 3172
  0.0 9.0 %copy-start.1 = (s32[12]{0:T(128)S(1)}, s32[12]{0:T(128)}, u32[]{:S(2)}) copy-start(s32[12]{0:T(128)} %width_ref.1) | copy-start | bytes 148
  0.0 9.0 %copy-start.2 = (s32[12]{0:T(128)S(1)}, s32[12]{0:T(128)}, u32[]{:S(2)}) copy-start(s32[12]{0:T(128)} %interval_ref.1) | copy-start | bytes 148
  2.1 19.6 %all-to-all-start = ((bf16[16,192,128]{2,1,0:T(8,128)(2,1)}), bf16[16,192,128]{2,1,0:T(8,128)(2,1)S(1)}, u32[]{:S(2)}, u32[]{:S(2)}) async-start(bf16[16,192,128]{2,1,0:T(8,128)(2,1)} %shard_map.55), calls=%async_computation | async-start | bytes 1572864 | tf_op jit(solution)/shard_map/all_to_all | solution.py:333
  21.7 9.4 %collective-permute-start.2 = (bf16[1024,128]{1,0:T(8,128)(2,1)S(1)}, bf16[1024,128]{1,0:T(8,128)(2,1)S(1)}, u32[]{:S(2)}, u32[]{:S(2)}) collective-permute-start(bf16[1024,128]{1,0:T(8,128)(2,1)S(1)} %get-tuple-element.37.outer_ref.rest_2_), channel_id=1, source_target_pairs={{0,240},{16,32},{32,16},{48,64},{64,48},{80,96},{96,80},{112,128},... | collective-permute-start | bytes 786440 | tf_op jit(solution)/shard_map/ppermute | solution.py:301
  25.9 8.6 %collective-permute-start = (bf16[1024,128]{1,0:T(8,128)(2,1)S(1)}, bf16[1024,128]{1,0:T(8,128)(2,1)S(1)}, u32[]{:S(2)}, u32[]{:S(2)}) collective-permute-start(bf16[1024,128]{1,0:T(8,128)(2,1)S(1)} %get-tuple-element.39.inner_ref.rest_0_), channel_id=1, source_target_pairs={{0,16},{16,0},{32,48},{48,32},{64,80},{80,64},{96,112},{112,96},{1... | collective-permute-start | bytes 786440 | tf_op jit(solution)/shard_map/ppermute | solution.py:296
  32.4 6.8 %collective-permute-start.4 = (bf16[1024,128]{1,0:T(8,128)(2,1)S(1)}, bf16[1024,128]{1,0:T(8,128)(2,1)S(1)}, u32[]{:S(2)}, u32[]{:S(2)}) collective-permute-start(bf16[1024,128]{1,0:T(8,128)(2,1)S(1)} %shard_map.59.outer_ref.rest_2_), channel_id=1, source_target_pairs={{0,240},{16,32},{32,16},{48,64},{64,48},{80,96},{96,80},{112,128},... | collective-permute-start | bytes 786440 | tf_op jit(solution)/shard_map/ppermute | solution.py:301
  35.8 8.0 %collective-permute-start.1 = (bf16[1024,128]{1,0:T(8,128)(2,1)S(1)}, bf16[1024,128]{1,0:T(8,128)(2,1)S(1)}, u32[]{:S(2)}, u32[]{:S(2)}) collective-permute-start(bf16[1024,128]{1,0:T(8,128)(2,1)S(1)} %shard_map.58.inner_ref.rest_0_), channel_id=1, source_target_pairs={{0,16},{16,0},{32,48},{48,32},{64,80},{80,64},{96,112},{112,96},{1... | collective-permute-start | bytes 786440 | tf_op jit(solution)/shard_map/ppermute | solution.py:296
  40.6 8.1 %collective-permute-start.5 = (bf16[1024,128]{1,0:T(8,128)(2,1)S(1)}, bf16[1024,128]{1,0:T(8,128)(2,1)S(1)}, u32[]{:S(2)}, u32[]{:S(2)}) collective-permute-start(bf16[1024,128]{1,0:T(8,128)(2,1)S(1)} %shard_map.62.outer_ref), channel_id=1, source_target_pairs={{0,240},{16,32},{32,16},{48,64},{64,48},{80,96},{96,80},{112,128},... | collective-permute-start | bytes 786440 | tf_op jit(solution)/shard_map/ppermute | solution.py:301
  45.1 3.6 %collective-permute-start.3 = (bf16[1024,128]{1,0:T(8,128)(2,1)S(1)}, bf16[1024,128]{1,0:T(8,128)(2,1)S(1)}, u32[]{:S(2)}, u32[]{:S(2)}) collective-permute-start(bf16[1024,128]{1,0:T(8,128)(2,1)S(1)} %shard_map.61.inner_ref), channel_id=1, source_target_pairs={{0,16},{16,0},{32,48},{48,32},{64,80},{80,64},{96,112},{112,96},{1... | collective-permute-start | bytes 786440 | tf_op jit(solution)/shard_map/ppermute | solution.py:296
  67.9 3.7 %collective-permute-start.6 = (bf16[21,128,128]{2,1,0:T(8,128)(2,1)S(1)}, bf16[21,128,128]{2,1,0:T(8,128)(2,1)S(1)}, u32[]{:S(2)}, u32[]{:S(2)}) collective-permute-start(bf16[21,128,128]{2,1,0:T(8,128)(2,1)S(1)} %shard_map.66), channel_id=1, source_target_pairs={{0,16},{16,0},{32,48},{48,32},{64,80},{80,64},{96,112},{112,96},{1... | collective-permute-start | bytes 2064392 | tf_op jit(solution)/shard_map/ppermute | solution.py:296
  87.3 3.0 %collective-permute-start.7 = (bf16[168,128]{1,0:T(8,128)(2,1)S(1)}, bf16[168,128]{1,0:T(8,128)(2,1)S(1)}, u32[]{:S(2)}, u32[]{:S(2)}) collective-permute-start(bf16[168,128]{1,0:T(8,128)(2,1)S(1)} %reduce_sum.12), channel_id=1, source_target_pairs={{0,224},{16,48},{32,0},{48,80},{64,32},{80,112},{96,64},{112,144},... | collective-permute-start | bytes 129032 | tf_op jit(solution)/shard_map/ppermute | solution.py:290
  88.7 4.4 %collective-permute-start.8 = (bf16[168,128]{1,0:T(8,128)(2,1)S(1)}, bf16[168,128]{1,0:T(8,128)(2,1)S(1)}, u32[]{:S(2)}, u32[]{:S(2)}) collective-permute-start(bf16[168,128]{1,0:T(8,128)(2,1)S(1)} %reduce_sum.12), channel_id=1, source_target_pairs={{0,32},{16,240},{32,64},{48,16},{64,96},{80,48},{96,128},{112,80},... | collective-permute-start | bytes 129032 | tf_op jit(solution)/shard_map/ppermute | solution.py:290
  93.2 6.0 %collective-permute-start.10 = (bf16[168,128]{1,0:T(8,128)(2,1)S(1)}, bf16[168,128]{1,0:T(8,128)(2,1)S(1)}, u32[]{:S(2)}, u32[]{:S(2)}) collective-permute-start(bf16[168,128]{1,0:T(8,128)(2,1)S(1)} %get-tuple-element.41), channel_id=1, source_target_pairs={{0,96},{16,176},{32,128},{48,208},{64,160},{80,240},{96,192},{112,... | collective-permute-start | bytes 129032 | tf_op jit(solution)/shard_map/ppermute | solution.py:290
  94.5 6.2 %collective-permute-start.9 = (bf16[168,128]{1,0:T(8,128)(2,1)S(1)}, bf16[168,128]{1,0:T(8,128)(2,1)S(1)}, u32[]{:S(2)}, u32[]{:S(2)}) collective-permute-start(bf16[168,128]{1,0:T(8,128)(2,1)S(1)} %get-tuple-element.40), channel_id=1, source_target_pairs={{0,160},{16,112},{32,192},{48,144},{64,224},{80,176},{96,0},{112,2... | collective-permute-start | bytes 129032 | tf_op jit(solution)/shard_map/ppermute | solution.py:290
  115.0 8.9 %collective-permute-start.11 = (bf16[21,128,128]{2,1,0:T(8,128)(2,1)S(1)}, bf16[21,128,128]{2,1,0:T(8,128)(2,1)S(1)}, u32[]{:S(2)}, u32[]{:S(2)}) collective-permute-start(bf16[21,128,128]{2,1,0:T(8,128)(2,1)S(1)} %bitcast.9), channel_id=1, source_target_pairs={{0,16},{16,0},{32,48},{48,32},{64,80},{80,64},{96,112},{112,96},{1... | collective-permute-start | bytes 2064392 | tf_op jit(solution)/shard_map/ppermute | solution.py:296

commit v5 on v4

--- a/solution.py
+++ b/solution.py
@@ -11,8 +11,10 @@
 BS = 128
 NINT = 8
 TILE = 128
-PAIRS = 42
-HALF = PAIRS // 2
+SIDE = 13
+DIAG = 4
+HALF = DIAG + 1 + SIDE
+ZERO = 2 * HALF
 FLIGHT = 4
 REACH = 4
 VMEM = pltpu.VMEM
@@ -91,18 +93,17 @@
         return index
 
     lanes = [slice_of(t) for t in range(tiles)]
-    slot = jnp.int32(0)
-    for m in range(PAIRS + 1):
-        list_ref[m] = 0
+    found = jnp.int32(0)
+    for m in range(2 * SIDE + 1):
+        list_ref[m] = 1
     for i in range(tiles):
-        for d in range(REACH):
+        for d in range(1, REACH):
             if i + d < tiles:
                 valid = lanes[i + d] - lanes[i] <= 1
-                pair_ref[i * REACH + d] = jnp.where(valid, slot, PAIRS)
-                list_ref[jnp.where(valid, slot, PAIRS)] = i * REACH + d
-                slot += jnp.where(valid, 1, 0)
-            else:
-                pair_ref[i * REACH + d] = PAIRS
+                slot = found + DIAG + 1 + jnp.where(found >= SIDE, DIAG + 1, 0)
+                pair_ref[i * REACH + d] = jnp.where(valid, slot, ZERO)
+                list_ref[jnp.where(valid, found, 2 * SIDE)] = i * REACH + d
+                found += jnp.where(valid, 1, 0)
     core = where_ref[3]
     pair_ref[tiles * REACH] = core
     near_ref[slots, 0] = core
@@ -240,39 +241,69 @@
             out_ref[at : at + BS, :] = value
 
 
+def places():
+    at_row = lax.broadcasted_iota(jnp.int32, (TILE, TILE), 0)
+    at_col = lax.broadcasted_iota(jnp.int32, (TILE, TILE), 1)
+    return at_row, at_col
+
+
 def gram_kernel(keep, pair_ref, list_ref, field_ref, out_ref, turned):
     tiles = field_ref.shape[0]
     core = pair_ref[tiles * REACH]
-    first = (core if keep else 1 - core) * HALF
+    half = core if keep else 1 - core
+    at_row, at_col = places()
     for t in range(tiles):
         turned[t] = field_ref[t].T
-    for m in range(HALF):
-        code = list_ref[first + m]
+
+    def block(low, high):
+        return jnp.dot(turned[low], field_ref[high], preferred_element_type=F32)
+
+    extra = jnp.zeros((TILE, TILE), F32)
+    for k in range(DIAG):
+        tile = (half * DIAG + k) * 2
+        upper = block(tile, tile)
+        lower = block(tile + 1, tile + 1)
+        squares = jnp.sum(jnp.where(at_row == at_col, lower, 0.0), axis=0, keepdims=True)
+        extra = jnp.where(at_row == k, squares, extra)
+        out_ref[k] = jnp.where(at_row <= at_col, upper, lower).astype(out_ref.dtype)
+    out_ref[DIAG] = extra.astype(out_ref.dtype)
+    for m in range(SIDE):
+        code = list_ref[half * SIDE + m]
         low = code // REACH
         high = low + code - low * REACH
-        block = jnp.dot(turned[low], field_ref[high], preferred_element_type=F32)
-        out_ref[m] = block.astype(out_ref.dtype)
-
-
-def correct_kernel(rows_all, pair_ref, field_ref, mine_ref, other_ref, out_ref, gram, scaled, norm):
+        out_ref[DIAG + 1 + m] = block(low, high).astype(out_ref.dtype)
+
+
+def correct_kernel(rows_all, pair_ref, field_ref, mine_ref, other_ref, out_ref, gram, own, scaled, norm):
     tiles = field_ref.shape[0]
     core = pair_ref[tiles * REACH]
     gram[pl.ds(core * HALF, HALF)] = mine_ref[...]
     gram[pl.ds(HALF - core * HALF, HALF)] = other_ref[...]
-    gram[PAIRS] = jnp.zeros((TILE, TILE), BF16)
-    at_row = lax.broadcasted_iota(jnp.int32, (TILE, TILE), 0)
-    at_col = lax.broadcasted_iota(jnp.int32, (TILE, TILE), 1)
-    eye = at_row == at_col
-    for t in range(tiles):
-        block = gram[pair_ref[t * REACH]].astype(F32)
-        squares = jnp.sum(jnp.where(eye, block, 0.0), axis=0, keepdims=True)
+    gram[ZERO] = jnp.zeros((TILE, TILE), BF16)
+    at_row, at_col = places()
+
+    def prepare(t, block, squares):
+        own[t] = block.astype(BF16)
         inverse = lax.rsqrt(squares / rows_all + 1e-05)
         norm[t : t + 1, :] = inverse
         scaled[t] = (field_ref[t].astype(F32) * (inverse * inverse)).astype(BF16)
+
+    for q in range(tiles // 2):
+        half, k = q // DIAG, q % DIAG
+        packed = gram[half * HALF + k].astype(F32)
+        flipped = packed.T
+        upper = jnp.where(at_row <= at_col, packed, flipped)
+        squares = jnp.sum(jnp.where(at_row == at_col, packed, 0.0), axis=0, keepdims=True)
+        prepare(2 * q, upper, squares)
+        squares = gram[half * HALF + DIAG].astype(F32)[k : k + 1, :]
+        lower = jnp.where(at_row > at_col, packed, flipped)
+        prepare(2 * q + 1, jnp.where(at_row == at_col, squares, lower), squares)
     for j in range(tiles):
-        below = range(max(0, j - REACH + 1), j + 1)
-        left = jnp.concatenate([scaled[i] for i in below], axis=1)
-        right = jnp.concatenate([gram[pair_ref[i * REACH + j - i]] for i in below], axis=0)
+        below = range(max(0, j - REACH + 1), j)
+        left = jnp.concatenate([scaled[i] for i in below] + [scaled[j]], axis=1)
+        right = jnp.concatenate(
+            [gram[pair_ref[i * REACH + j - i]] for i in below] + [own[j]], axis=0
+        )
         total = jnp.dot(left, right, preferred_element_type=F32)
         above = range(j + 1, min(tiles, j + REACH))
         if above:
@@ -342,7 +373,7 @@
             shape((slots + 1, blocks), jnp.int32),
             shape((2 * blocks // 3 + 1, HB), jnp.int32),
             shape((tiles * REACH + 1,), jnp.int32),
-            shape((PAIRS + 1,), jnp.int32),
+            shape((2 * SIDE + 1,), jnp.int32),
         ),
         in_specs=smem(4),
         out_specs=tuple(smem(4)),
@@ -446,7 +477,8 @@
         [pair],
         [field, mine, other],
         [
-            VMEM((PAIRS + 1, TILE, TILE), BF16),
+            VMEM((2 * HALF + 1, TILE, TILE), BF16),
+            VMEM((tiles, TILE, TILE), BF16),
             VMEM((tiles, rows_mine, TILE), BF16),
             VMEM((tiles, TILE), F32),
         ],

time: 127 us -> 126 us (level)
  blocking collectives: 45.8 us -> 44.1 us
where the time goes in v5:
time: 126 us; the launch traced here: 125 us
  blocking collectives  44.1 us (35%)
  starting transfers between devices  32.4 us (26%)
  Pallas kernels  30.9 us (25%)
  waiting for transfers between devices  17.3 us (14%)
    pallas_call x10, Pallas kernels, call(): pl.pallas_call(kernel, out_shape=tuple(outs), in_specs=smem(len(scalars))...  19.2 us
    all_to_all x1, blocking collectives, body(): lax.all_to_all(filtered.reshape(tiles, rows_mine, TILE), 'cuts', 0, 0)  16.2 us
    all_to_all x1, blocking collectives, body(): lax.all_to_all(partial.reshape(cut_count, share, TILE), 'cuts', 0, 0)  14.7 us
    all_to_all x1, blocking collectives, body(): mine = lax.all_to_all(spread, 'cuts', 0, 0).reshape(HALF, TILE, TILE)  13.3 us
    ppermute x5, starting transfers between devices, exchange(): lax.ppermute(array, 'row', [(i, i ^ 1) for i in range(lax.axis_size('row'...  9.79 us
    ppermute x3, starting transfers between devices, swap_outer(): lax.ppermute(array, 'row', [(i, (i - 1 + 2 * (i % 2)) % size) for i in ra...  9.55 us
    all_to_all x1, waiting for transfers between devices, body(): panel = lax.all_to_all(turned, 'cuts', 0, 0).reshape(panel_rows, TILE)  8.31 us
    ppermute x4, waiting for transfers between devices, shift(): lax.ppermute(array, 'row', [(i, (i + 2 * chips * (1 - 2 * (i % 2))) % siz...  7.12 us
  transfers between devices with their start and end apart: 13, of which 7 were waited for; matrix products, arithmetic and copies ran while one was open for 0% of the time, Pallas kernels for 18%

profile of v5, /device:TPU:33, one launch (start us, length us, event | category | flops | bytes accessed | tf_op | source)
XLA Modules:
  0.0 125.3 jit_solution(7413993055223499768)
XLA Ops:
  0.0 2.0 %shard_map.55 = bf16[16,192,128]{2,1,0:T(8,128)(2,1)} custom-call(bf16[192,2048]{1,0:T(8,128)(2,1)} %start_ref.1), custom_call_target="tpu_custom_call" | custom-call | tf_op jit(solution)/shard_map/pallas_call | solution.py:352
  2.1 0.0 copy-start
  2.1 0.0 copy-start.1
  2.1 0.0 copy-start.2
  2.1 6.9 %all-to-all-start = ((bf16[16,192,128]{2,1,0:T(8,128)(2,1)}), bf16[16,192,128]{2,1,0:T(8,128)(2,1)S(1)}, u32[]{:S(2)}, u32[]{:S(2)}) async-start(bf16[16,192,128]{2,1,0:T(8,128)(2,1)} %shard_map.55), calls=%async_computation | async-start | bytes 1572864 | tf_op jit(solution)/shard_map/all_to_all | solution.py:364
  9.0 0.1 pad_add_fusion.where_ref
  9.1 0.0 copy-done
  9.1 0.0 copy-done.1
  9.1 0.0 copy-done.2
  9.1 4.4 %shard_map.56 = (s32[12,24]{1,0:T(8,128)S(1)}, s32[17,8]{1,0:T(8,128)S(1)}, s32[65]{0:T(128)S(1)}, s32[27]{0:T(128)S(1)}) custom-call(s32[4]{0:T(128)S(1)} %pad_add_fusion.where_ref, s32[11,24]{1,0:T(8,128)S(1)} %bitcast.11, s32[12]{0:T(128)S(1)} %copy-done.1, s32[12]{0:T(128)S(1)} %copy-done.2), custom_call_target="tpu_custom_call" | custom-call | flops 1048576 | bytes 4096 | tf_op jit(solution)/shard_map/pallas_call | solution.py:370
  13.5 8.3 %all-to-all-done = bf16[16,192,128]{2,1,0:T(8,128)(2,1)S(1)} async-done(((bf16[16,192,128]{2,1,0:T(8,128)(2,1)}), bf16[16,192,128]{2,1,0:T(8,128)(2,1)S(1)}, u32[]{:S(2)}, u32[]{:S(2)}) %all-to-all-start) | async-done | bytes 786464 | tf_op jit(solution)/shard_map/all_to_all | solution.py:364
  21.8 0.1 broadcast_select_fusion
  21.8 4.2 %collective-permute-start.2 = (bf16[1024,128]{1,0:T(8,128)(2,1)S(1)}, bf16[1024,128]{1,0:T(8,128)(2,1)S(1)}, u32[]{:S(2)}, u32[]{:S(2)}) collective-permute-start(bf16[1024,128]{1,0:T(8,128)(2,1)S(1)} %get-tuple-element.37.outer_ref.rest_2_), channel_id=1, source_target_pairs={{0,240},{16,32},{32,16},{48,64},{64,48},{80,96},{96,80},{112,128},... | collective-permute-start | bytes 786440 | tf_op jit(solution)/shard_map/ppermute | solution.py:332
  26.0 0.0 collective-permute-start
  26.0 5.2 %shard_map.57 = (bf16[1024,128]{1,0:T(8,128)(2,1)S(1)}, f32[2,1024,128]{2,1,0:T(8,128)S(1)}, bf16[24,11,128,128]{3,2,1,0:T(8,128)(2,1)S(1)}) custom-call(s32[12,24]{1,0:T(8,128)S(1)} %get-tuple-element.27.near_ref, bf16[24,11,128,128]{3,2,1,0:T(8,128)(2,1)} %ham_ref.1, bf16[1024,128]{1,0:T(8,128)(2,1)S(1)} %get-tuple-element.39.inner_ref.rest_0_, ...), custom_call_target="tpu_custom_call" | custom-call | flops 1107296256 | bytes 8650752 | tf_op jit(solution)/shard_map/pallas_call | solution.py:395
  31.3 0.0 collective-permute-done.2.halo_ref
  31.3 1.3 %shard_map.59.outer_ref.rest_2_ = bf16[1024,128]{1,0:T(8,128)(2,1)S(1)} custom-call(s32[17,8]{1,0:T(8,128)S(1)} %get-tuple-element.26.far_ref, bf16[24,11,128,128]{3,2,1,0:T(8,128)(2,1)S(1)} %get-tuple-element.29.ham_ref, bf16[1024,128]{1,0:T(8,128)(2,1)S(1)} %collective-permute-done.2.halo_ref, f32[2,1024,128]{2,1,0:T(8,128)S(1)} %get-tuple-element.30.edge_ref), custom_call_target="tpu_custom_call" | custom-call | flops 138412032 | bytes 10223616 | tf_op jit(solution)/shard_map/pallas_call | solution.py:36
  32.6 2.1 %collective-permute-start.4 = (bf16[1024,128]{1,0:T(8,128)(2,1)S(1)}, bf16[1024,128]{1,0:T(8,128)(2,1)S(1)}, u32[]{:S(2)}, u32[]{:S(2)}) collective-permute-start(bf16[1024,128]{1,0:T(8,128)(2,1)S(1)} %shard_map.59.outer_ref.rest_2_), channel_id=1, source_target_pairs={{0,240},{16,32},{32,16},{48,64},{64,48},{80,96},{96,80},{112,128},... | collective-permute-start | bytes 786440 | tf_op jit(solution)/shard_map/ppermute | solution.py:332
  34.7 0.0 collective-permute-done.halo_ref
  34.7 1.3 %shard_map.58.inner_ref.rest_0_ = bf16[1024,128]{1,0:T(8,128)(2,1)S(1)} custom-call(s32[17,8]{1,0:T(8,128)S(1)} %get-tuple-element.26.far_ref, bf16[24,11,128,128]{3,2,1,0:T(8,128)(2,1)S(1)} %get-tuple-element.29.ham_ref, bf16[1024,128]{1,0:T(8,128)(2,1)S(1)} %collective-permute-done.halo_ref, f32[2,1024,128]{2,1,0:T(8,128)S(1)} %get-tuple-element.30.edge_ref), custom_call_target="tpu_custom_call" | custom-call | flops 138412032 | bytes 10223616 | tf_op jit(solution)/shard_map/pallas_call | solution.py:36
  35.9 0.1 collective-permute-start.1
  36.1 3.3 %shard_map.60 = (bf16[1024,128]{1,0:T(8,128)(2,1)S(1)}, f32[2,1024,128]{2,1,0:T(8,128)S(1)}) custom-call(s32[12,24]{1,0:T(8,128)S(1)} %get-tuple-element.27.near_ref, bf16[24,11,128,128]{3,2,1,0:T(8,128)(2,1)S(1)} %get-tuple-element.29.ham_ref, bf16[1024,128]{1,0:T(8,128)(2,1)S(1)} %shard_map.58.inner_ref.rest_0_, ...), custom_call_target="tpu_custom_call" | custom-call | flops 1107296256 | bytes 11534336 | tf_op jit(solution)/shard_map/pallas_call | solution.py:36
  39.4 0.0 collective-permute-done.4.halo_ref
  39.4 1.3 %shard_map.62.outer_ref = bf16[1024,128]{1,0:T(8,128)(2,1)S(1)} custom-call(s32[17,8]{1,0:T(8,128)S(1)} %get-tuple-element.26.far_ref, bf16[24,11,128,128]{3,2,1,0:T(8,128)(2,1)S(1)} %get-tuple-element.29.ham_ref, bf16[1024,128]{1,0:T(8,128)(2,1)S(1)} %collective-permute-done.4.halo_ref, f32[2,1024,128]{2,1,0:T(8,128)S(1)} %get-tuple-element.32.edge_ref), custom_call_target="tpu_custom_call" | custom-call | flops 138412032 | bytes 10223616 | tf_op jit(solution)/shard_map/pallas_call | solution.py:36
  40.7 3.2 %collective-permute-start.5 = (bf16[1024,128]{1,0:T(8,128)(2,1)S(1)}, bf16[1024,128]{1,0:T(8,128)(2,1)S(1)}, u32[]{:S(2)}, u32[]{:S(2)}) collective-permute-start(bf16[1024,128]{1,0:T(8,128)(2,1)S(1)} %shard_map.62.outer_ref), channel_id=1, source_target_pairs={{0,240},{16,32},{32,16},{48,64},{64,48},{80,96},{96,80},{112,128},... | collective-permute-start | bytes 786440 | tf_op jit(solution)/shard_map/ppermute | solution.py:332
  43.9 0.0 collective-permute-done.1.halo_ref
  43.9 1.3 %shard_map.61.inner_ref = bf16[1024,128]{1,0:T(8,128)(2,1)S(1)} custom-call(s32[17,8]{1,0:T(8,128)S(1)} %get-tuple-element.26.far_ref, bf16[24,11,128,128]{3,2,1,0:T(8,128)(2,1)S(1)} %get-tuple-element.29.ham_ref, bf16[1024,128]{1,0:T(8,128)(2,1)S(1)} %collective-permute-done.1.halo_ref, f32[2,1024,128]{2,1,0:T(8,128)S(1)} %get-tuple-element.32.edge_ref), custom_call_target="tpu_custom_call" | custom-call | flops 138412032 | bytes 10223616 | tf_op jit(solution)/shard_map/pallas_call | solution.py:36
  45.2 0.3 collective-permute-start.3
  45.5 3.3 %shard_map.63 = (bf16[1024,128]{1,0:T(8,128)(2,1)S(1)}, f32[2,1024,128]{2,1,0:T(8,128)S(1)}) custom-call(s32[12,24]{1,0:T(8,128)S(1)} %get-tuple-element.27.near_ref, bf16[24,11,128,128]{3,2,1,0:T(8,128)(2,1)S(1)} %get-tuple-element.29.ham_ref, bf16[1024,128]{1,0:T(8,128)(2,1)S(1)} %shard_map.61.inner_ref, bf16[1024,128]{1,0:T(8,128)(2,1)S(1)} %get-tuple-element.33.mid_ref, ...), custom_call_target="tpu_custom_call" | custom-call | flops 1107296256 | bytes 11534336 | tf_op jit(solution)/shard_map/pallas_call | solution.py:36
  48.8 0.0 collective-permute-done.5.outer_ref
  48.8 0.0 collective-permute-done.3.inner_ref
  48.8 1.6 %shard_map.64 = bf16[3072,128]{1,0:T(8,128)(2,1)S(1)} custom-call(s32[17,8]{1,0:T(8,128)S(1)} %get-tuple-element.26.far_ref, bf16[24,11,128,128]{3,2,1,0:T(8,128)(2,1)S(1)} %get-tuple-element.29.ham_ref, bf16[1024,128]{1,0:T(8,128)(2,1)S(1)} %collective-permute-done.3.inner_ref, bf16[1024,128]{1,0:T(8,128)(2,1)S(1)} %collective-permute-done.5.outer_ref, ...), custom_call_target="tpu_custom_call" | custom-call | flops 276824064 | bytes 11272192 | tf_op jit(solution)/shard_map/pallas_call | solution.py:36
  50.5 16.2 %all_to_all.20.field_ref = bf16[16,192,128]{2,1,0:T(8,128)(2,1)S(1)} all-to-all(bf16[16,192,128]{2,1,0:T(8,128)(2,1)S(1)} %bitcast.8), channel_id=1, replica_groups=mesh['row'=16,'cuts'=16] {'cuts'}, dimensions={0} | all-to-all | bytes 1572864 | tf_op jit(solution)/shard_map/all_to_all | solution.py:453
  66.6 1.4 %shard_map.66 = bf16[18,128,128]{2,1,0:T(8,128)(2,1)S(1)} custom-call(s32[65]{0:T(128)S(1)} %get-tuple-element.25.pair_ref, s32[27]{0:T(128)S(1)} %get-tuple-element.36.list_ref, bf16[16,192,128]{2,1,0:T(8,128)(2,1)S(1)} %all_to_all.20.field_ref), custom_call_target="tpu_custom_call" | custom-call | flops 268435456 | bytes 1376256 | tf_op jit(solution)/shard_map/pallas_call | solution.py:36
  68.0 1.9 %collective-permute-start.6 = (bf16[18,128,128]{2,1,0:T(8,128)(2,1)S(1)}, bf16[18,128,128]{2,1,0:T(8,128)(2,1)S(1)}, u32[]{:S(2)}, u32[]{:S(2)}) collective-permute-start(bf16[18,128,128]{2,1,0:T(8,128)(2,1)S(1)} %shard_map.66), channel_id=1, source_target_pairs={{0,16},{16,0},{32,48},{48,32},{64,80},{80,64},{96,112},{112,96},{1... | collective-permute-start | bytes 1769480 | tf_op jit(solution)/shard_map/ppermute | solution.py:327
  70.0 1.4 %shard_map.65 = f32[18,128,128]{2,1,0:T(8,128)S(1)} custom-call(s32[65]{0:T(128)S(1)} %get-tuple-element.25.pair_ref, s32[27]{0:T(128)S(1)} %get-tuple-element.36.list_ref, bf16[16,192,128]{2,1,0:T(8,128)(2,1)S(1)} %all_to_all.20.field_ref), custom_call_target="tpu_custom_call" | custom-call | flops 268435456 | bytes 1966080 | tf_op jit(solution)/shard_map/pallas_call | solution.py:36
  71.4 0.2 collective-permute-done.6
  71.6 0.1 add_convert_fusion
  71.8 14.7 %all_to_all.21 = bf16[16,144,128]{2,1,0:T(8,128)(2,1)S(1)} all-to-all(bf16[16,144,128]{2,1,0:T(8,128)(2,1)S(1)} %bitcast.13), channel_id=1, replica_groups=mesh['row'=16,'cuts'=16] {'cuts'}, dimensions={0} | all-to-all | bytes 1179648 | tf_op jit(solution)/shard_map/all_to_all | solution.py:469
  86.4 0.1 reduce_sum.12
  86.5 1.4 %collective-permute-start.7 = (bf16[144,128]{1,0:T(8,128)(2,1)S(1)}, bf16[144,128]{1,0:T(8,128)(2,1)S(1)}, u32[]{:S(2)}, u32[]{:S(2)}) collective-permute-start(bf16[144,128]{1,0:T(8,128)(2,1)S(1)} %reduce_sum.12), channel_id=1, source_target_pairs={{0,224},{16,48},{32,0},{48,80},{64,32},{80,112},{96,64},{112,144},... | collective-permute-start | bytes 110600 | tf_op jit(solution)/shard_map/ppermute | solution.py:321
  87.9 0.1 collective-permute-start.8
  88.1 1.3 %collective-permute-done.7 = bf16[144,128]{1,0:T(8,128)(2,1)S(1)} collective-permute-done((bf16[144,128]{1,0:T(8,128)(2,1)S(1)}, bf16[144,128]{1,0:T(8,128)(2,1)S(1)}, u32[]{:S(2)}, u32[]{:S(2)}) %collective-permute-start.7) | collective-permute-done | bytes 36896 | tf_op jit(solution)/shard_map/ppermute | solution.py:321
  89.4 2.8 %collective-permute-done.8 = bf16[144,128]{1,0:T(8,128)(2,1)S(1)} collective-permute-done((bf16[144,128]{1,0:T(8,128)(2,1)S(1)}, bf16[144,128]{1,0:T(8,128)(2,1)S(1)}, u32[]{:S(2)}, u32[]{:S(2)}) %collective-permute-start.8) | collective-permute-done | bytes 36896 | tf_op jit(solution)/shard_map/ppermute | solution.py:321
  92.2 1.7 %collective-permute-start.10 = (bf16[144,128]{1,0:T(8,128)(2,1)S(1)}, bf16[144,128]{1,0:T(8,128)(2,1)S(1)}, u32[]{:S(2)}, u32[]{:S(2)}) collective-permute-start(bf16[144,128]{1,0:T(8,128)(2,1)S(1)} %get-tuple-element.41), channel_id=1, source_target_pairs={{0,96},{16,176},{32,128},{48,208},{64,160},{80,240},{96,192},{112,... | collective-permute-start | bytes 110600 | tf_op jit(solution)/shard_map/ppermute | solution.py:321
  93.9 2.8 %collective-permute-start.9 = (bf16[144,128]{1,0:T(8,128)(2,1)S(1)}, bf16[144,128]{1,0:T(8,128)(2,1)S(1)}, u32[]{:S(2)}, u32[]{:S(2)}) collective-permute-start(bf16[144,128]{1,0:T(8,128)(2,1)S(1)} %get-tuple-element.40), channel_id=1, source_target_pairs={{0,160},{16,112},{32,192},{48,144},{64,224},{80,176},{96,0},{112,2... | collective-permute-start | bytes 110600 | tf_op jit(solution)/shard_map/ppermute | solution.py:321
  96.7 1.3 %collective-permute-done.10 = bf16[144,128]{1,0:T(8,128)(2,1)S(1)} collective-permute-done((bf16[144,128]{1,0:T(8,128)(2,1)S(1)}, bf16[144,128]{1,0:T(8,128)(2,1)S(1)}, u32[]{:S(2)}, u32[]{:S(2)}) %collective-permute-start.10) | collective-permute-done | bytes 36896 | tf_op jit(solution)/shard_map/ppermute | solution.py:321
  98.1 1.7 %collective-permute-done.9 = bf16[144,128]{1,0:T(8,128)(2,1)S(1)} collective-permute-done((bf16[144,128]{1,0:T(8,128)(2,1)S(1)}, bf16[144,128]{1,0:T(8,128)(2,1)S(1)}, u32[]{:S(2)}, u32[]{:S(2)}) %collective-permute-start.9) | collective-permute-done | bytes 36896 | tf_op jit(solution)/shard_map/ppermute | solution.py:321
  99.8 0.1 broadcast_in_dim.2
  99.9 13.3 %all_to_all.22 = bf16[16,144,128]{2,1,0:T(8,128)(2,1)S(1)} all-to-all(bf16[16,144,128]{2,1,0:T(8,128)(2,1)S(1)} %broadcast_in_dim.2), channel_id=1, replica_groups=mesh['row'=16,'cuts'=16] {'cuts'}, dimensions={0} | all-to-all | bytes 1179648 | tf_op jit(solution)/shard_map/all_to_all | solution.py:472
  113.2 7.4 %collective-permute-start.11 = (bf16[18,128,128]{2,1,0:T(8,128)(2,1)S(1)}, bf16[18,128,128]{2,1,0:T(8,128)(2,1)S(1)}, u32[]{:S(2)}, u32[]{:S(2)}) collective-permute-start(bf16[18,128,128]{2,1,0:T(8,128)(2,1)S(1)} %bitcast.9), channel_id=1, source_target_pairs={{0,16},{16,0},{32,48},{48,32},{64,80},{80,64},{96,112},{112,96},{1... | collective-permute-start | bytes 1769480 | tf_op jit(solution)/shard_map/ppermute | solution.py:327
  120.6 1.6 %collective-permute-done.11.other_ref = bf16[18,128,128]{2,1,0:T(8,128)(2,1)S(1)} collective-permute-done((bf16[18,128,128]{2,1,0:T(8,128)(2,1)S(1)}, bf16[18,128,128]{2,1,0:T(8,128)(2,1)S(1)}, u32[]{:S(2)}, u32[]{:S(2)}) %collective-permute-start.11) | collective-permute-done | bytes 589856 | tf_op jit(solution)/shard_map/ppermute | solution.py:327
  122.2 3.1 %shard_map.67 = bf16[192,2048]{1,0:T(8,128)(2,1)} custom-call(s32[65]{0:T(128)S(1)} %get-tuple-element.25.pair_ref, bf16[16,192,128]{2,1,0:T(8,128)(2,1)S(1)} %all_to_all.20.field_ref, bf16[18,128,128]{2,1,0:T(8,128)(2,1)S(1)} %bitcast.10, bf16[18,128,128]{2,1,0:T(8,128)(2,1)S(1)} %collective-permute-done.11.other_ref), custom_call_target="tpu_custom_call" | custom-call | flops 536870912 | bytes 2752512 | tf_op jit(solution)/shard_map/pallas_call | solution.py:36
  (2 shorter events, 0.1 us)
Async XLA Ops:
  2.1 7.0 %copy-start = (s32[24,11]{0,1:T(8,128)S(1)}, s32[24,11]{0,1:T(8,128)}, u32[]{:S(2)}) copy-start(s32[24,11]{0,1:T(8,128)} %param.6) | copy-start | bytes 3172
  2.1 7.0 %copy-start.1 = (s32[12]{0:T(128)S(1)}, s32[12]{0:T(128)}, u32[]{:S(2)}) copy-start(s32[12]{0:T(128)} %width_ref.1) | copy-start | bytes 148
  2.1 7.0 %copy-start.2 = (s32[12]{0:T(128)S(1)}, s32[12]{0:T(128)}, u32[]{:S(2)}) copy-start(s32[12]{0:T(128)} %interval_ref.1) | copy-start | bytes 148
  2.1 19.7 %all-to-all-start = ((bf16[16,192,128]{2,1,0:T(8,128)(2,1)}), bf16[16,192,128]{2,1,0:T(8,128)(2,1)S(1)}, u32[]{:S(2)}, u32[]{:S(2)}) async-start(bf16[16,192,128]{2,1,0:T(8,128)(2,1)} %shard_map.55), calls=%async_computation | async-start | bytes 1572864 | tf_op jit(solution)/shard_map/all_to_all | solution.py:364
  21.8 9.4 %collective-permute-start.2 = (bf16[1024,128]{1,0:T(8,128)(2,1)S(1)}, bf16[1024,128]{1,0:T(8,128)(2,1)S(1)}, u32[]{:S(2)}, u32[]{:S(2)}) collective-permute-start(bf16[1024,128]{1,0:T(8,128)(2,1)S(1)} %get-tuple-element.37.outer_ref.rest_2_), channel_id=1, source_target_pairs={{0,240},{16,32},{32,16},{48,64},{64,48},{80,96},{96,80},{112,128},... | collective-permute-start | bytes 786440 | tf_op jit(solution)/shard_map/ppermute | solution.py:332
  26.0 8.7 %collective-permute-start = (bf16[1024,128]{1,0:T(8,128)(2,1)S(1)}, bf16[1024,128]{1,0:T(8,128)(2,1)S(1)}, u32[]{:S(2)}, u32[]{:S(2)}) collective-permute-start(bf16[1024,128]{1,0:T(8,128)(2,1)S(1)} %get-tuple-element.39.inner_ref.rest_0_), channel_id=1, source_target_pairs={{0,16},{16,0},{32,48},{48,32},{64,80},{80,64},{96,112},{112,96},{1... | collective-permute-start | bytes 786440 | tf_op jit(solution)/shard_map/ppermute | solution.py:327
  32.6 6.9 %collective-permute-start.4 = (bf16[1024,128]{1,0:T(8,128)(2,1)S(1)}, bf16[1024,128]{1,0:T(8,128)(2,1)S(1)}, u32[]{:S(2)}, u32[]{:S(2)}) collective-permute-start(bf16[1024,128]{1,0:T(8,128)(2,1)S(1)} %shard_map.59.outer_ref.rest_2_), channel_id=1, source_target_pairs={{0,240},{16,32},{32,16},{48,64},{64,48},{80,96},{96,80},{112,128},... | collective-permute-start | bytes 786440 | tf_op jit(solution)/shard_map/ppermute | solution.py:332
  35.9 8.0 %collective-permute-start.1 = (bf16[1024,128]{1,0:T(8,128)(2,1)S(1)}, bf16[1024,128]{1,0:T(8,128)(2,1)S(1)}, u32[]{:S(2)}, u32[]{:S(2)}) collective-permute-start(bf16[1024,128]{1,0:T(8,128)(2,1)S(1)} %shard_map.58.inner_ref.rest_0_), channel_id=1, source_target_pairs={{0,16},{16,0},{32,48},{48,32},{64,80},{80,64},{96,112},{112,96},{1... | collective-permute-start | bytes 786440 | tf_op jit(solution)/shard_map/ppermute | solution.py:327
  40.7 8.1 %collective-permute-start.5 = (bf16[1024,128]{1,0:T(8,128)(2,1)S(1)}, bf16[1024,128]{1,0:T(8,128)(2,1)S(1)}, u32[]{:S(2)}, u32[]{:S(2)}) collective-permute-start(bf16[1024,128]{1,0:T(8,128)(2,1)S(1)} %shard_map.62.outer_ref), channel_id=1, source_target_pairs={{0,240},{16,32},{32,16},{48,64},{64,48},{80,96},{96,80},{112,128},... | collective-permute-start | bytes 786440 | tf_op jit(solution)/shard_map/ppermute | solution.py:332
  45.2 3.6 %collective-permute-start.3 = (bf16[1024,128]{1,0:T(8,128)(2,1)S(1)}, bf16[1024,128]{1,0:T(8,128)(2,1)S(1)}, u32[]{:S(2)}, u32[]{:S(2)}) collective-permute-start(bf16[1024,128]{1,0:T(8,128)(2,1)S(1)} %shard_map.61.inner_ref), channel_id=1, source_target_pairs={{0,16},{16,0},{32,48},{48,32},{64,80},{80,64},{96,112},{112,96},{1... | collective-permute-start | bytes 786440 | tf_op jit(solution)/shard_map/ppermute | solution.py:327
  68.0 3.6 %collective-permute-start.6 = (bf16[18,128,128]{2,1,0:T(8,128)(2,1)S(1)}, bf16[18,128,128]{2,1,0:T(8,128)(2,1)S(1)}, u32[]{:S(2)}, u32[]{:S(2)}) collective-permute-start(bf16[18,128,128]{2,1,0:T(8,128)(2,1)S(1)} %shard_map.66), channel_id=1, source_target_pairs={{0,16},{16,0},{32,48},{48,32},{64,80},{80,64},{96,112},{112,96},{1... | collective-permute-start | bytes 1769480 | tf_op jit(solution)/shard_map/ppermute | solution.py:327
  86.5 2.9 %collective-permute-start.7 = (bf16[144,128]{1,0:T(8,128)(2,1)S(1)}, bf16[144,128]{1,0:T(8,128)(2,1)S(1)}, u32[]{:S(2)}, u32[]{:S(2)}) collective-permute-start(bf16[144,128]{1,0:T(8,128)(2,1)S(1)} %reduce_sum.12), channel_id=1, source_target_pairs={{0,224},{16,48},{32,0},{48,80},{64,32},{80,112},{96,64},{112,144},... | collective-permute-start | bytes 110600 | tf_op jit(solution)/shard_map/ppermute | solution.py:321
  87.9 4.2 %collective-permute-start.8 = (bf16[144,128]{1,0:T(8,128)(2,1)S(1)}, bf16[144,128]{1,0:T(8,128)(2,1)S(1)}, u32[]{:S(2)}, u32[]{:S(2)}) collective-permute-start(bf16[144,128]{1,0:T(8,128)(2,1)S(1)} %reduce_sum.12), channel_id=1, source_target_pairs={{0,32},{16,240},{32,64},{48,16},{64,96},{80,48},{96,128},{112,80},... | collective-permute-start | bytes 110600 | tf_op jit(solution)/shard_map/ppermute | solution.py:321
  92.2 5.9 %collective-permute-start.10 = (bf16[144,128]{1,0:T(8,128)(2,1)S(1)}, bf16[144,128]{1,0:T(8,128)(2,1)S(1)}, u32[]{:S(2)}, u32[]{:S(2)}) collective-permute-start(bf16[144,128]{1,0:T(8,128)(2,1)S(1)} %get-tuple-element.41), channel_id=1, source_target_pairs={{0,96},{16,176},{32,128},{48,208},{64,160},{80,240},{96,192},{112,... | collective-permute-start | bytes 110600 | tf_op jit(solution)/shard_map/ppermute | solution.py:321
  93.9 5.8 %collective-permute-start.9 = (bf16[144,128]{1,0:T(8,128)(2,1)S(1)}, bf16[144,128]{1,0:T(8,128)(2,1)S(1)}, u32[]{:S(2)}, u32[]{:S(2)}) collective-permute-start(bf16[144,128]{1,0:T(8,128)(2,1)S(1)} %get-tuple-element.40), channel_id=1, source_target_pairs={{0,160},{16,112},{32,192},{48,144},{64,224},{80,176},{96,0},{112,2... | collective-permute-start | bytes 110600 | tf_op jit(solution)/shard_map/ppermute | solution.py:321
  113.2 9.1 %collective-permute-start.11 = (bf16[18,128,128]{2,1,0:T(8,128)(2,1)S(1)}, bf16[18,128,128]{2,1,0:T(8,128)(2,1)S(1)}, u32[]{:S(2)}, u32[]{:S(2)}) collective-permute-start(bf16[18,128,128]{2,1,0:T(8,128)(2,1)S(1)} %bitcast.9), channel_id=1, source_target_pairs={{0,16},{16,0},{32,48},{48,32},{64,80},{80,64},{96,112},{112,96},{1... | collective-permute-start | bytes 1769480 | tf_op jit(solution)/shard_map/ppermute | solution.py:327

commit v6 on v5

--- a/solution.py
+++ b/solution.py
@@ -15,6 +15,7 @@
 DIAG = 4
 HALF = DIAG + 1 + SIDE
 ZERO = 2 * HALF
+LISTED = 63
 FLIGHT = 4
 REACH = 4
 VMEM = pltpu.VMEM
@@ -48,7 +49,7 @@
     return jax.ShapeDtypeStruct(dims, dtype)
 
 
-def table_kernel(where_ref, turned_ref, width_ref, interval_ref, near_ref, far_ref, pair_ref, list_ref):
+def table_kernel(where_ref, turned_ref, width_ref, interval_ref, near_ref, far_ref, pair_ref):
     slots, blocks = turned_ref.shape
     first, total, cut = where_ref[0], where_ref[1], where_ref[2]
     edge = blocks // 3
@@ -60,7 +61,7 @@
         @pl.when(outer)
         def _():
             for k in range(edge):
-                far_ref[line, k] = edge
+                far_ref[line * HB + k] = edge
 
         found = jnp.int32(0)
         for n in range(slots):
@@ -68,18 +69,19 @@
             away = jnp.where(away < -HB, away + total, away)
             away = jnp.where(away >= total - HB, away - total, away)
             local = (away >= 0) & (away < blocks)
-            near_ref[n, b] = jnp.where(local, away, blocks)
+            near_ref[n * blocks + b] = jnp.where(local, away, blocks)
             halo = jnp.where(away < 0, away + HB, away - blocks)
 
             @pl.when(jnp.logical_not(local))
             def _():
-                far_ref[line, found] = n * 16 + halo
+                far_ref[line * HB + found] = n * 16 + halo
 
             found += jnp.where(local, 0, 1)
         return 0
 
     lax.fori_loop(0, blocks, one_row, 0)
-    tiles = pair_ref.shape[0] // REACH
+    tiles = (pair_ref.shape[0] - LISTED) // REACH
+    listed = tiles * REACH + 1
     ends = []
     end = jnp.int32(0)
     for s in range(width_ref.shape[0]):
@@ -95,20 +97,20 @@
     lanes = [slice_of(t) for t in range(tiles)]
     found = jnp.int32(0)
     for m in range(2 * SIDE + 1):
-        list_ref[m] = 1
+        pair_ref[listed + m] = 1
     for i in range(tiles):
         for d in range(1, REACH):
             if i + d < tiles:
                 valid = lanes[i + d] - lanes[i] <= 1
                 slot = found + DIAG + 1 + jnp.where(found >= SIDE, DIAG + 1, 0)
                 pair_ref[i * REACH + d] = jnp.where(valid, slot, ZERO)
-                list_ref[jnp.where(valid, found, 2 * SIDE)] = i * REACH + d
+                pair_ref[listed + jnp.where(valid, found, 2 * SIDE)] = i * REACH + d
                 found += jnp.where(valid, 1, 0)
     core = where_ref[3]
     pair_ref[tiles * REACH] = core
-    near_ref[slots, 0] = core
-    near_ref[slots, 1] = interval_ref[slice_of(cut)]
-    far_ref[2 * edge, 0] = core
+    near_ref[slots * blocks] = core
+    near_ref[slots * blocks + 1] = interval_ref[slice_of(cut)]
+    far_ref[2 * edge * HB] = core
 
 
 def turn_kernel(start_ref, out_ref, tiles_ref, read, written):
@@ -150,7 +152,7 @@
         ham = ham_ref
     third = blocks // 3
     span = third * BS
-    core = near_ref[slots, 0]
+    core = near_ref[slots * blocks]
     inner_at, outer_at = (1 - core) * 2 * span, core * 2 * span
 
     def spread(inner, mid, outer, into):
@@ -162,10 +164,10 @@
     stack[blocks * BS :] = jnp.zeros((BS, TILE), BF16)
     if not first:
         spread(*rest[:3], before)
-    centre = -0.5 + near_ref[slots, 1].astype(F32) * F32(1 / (NINT - 1))
+    centre = -0.5 + near_ref[slots * blocks + 1].astype(F32) * F32(1 / (NINT - 1))
 
     def tile_at(n, b):
-        return stack[pl.ds(pl.multiple_of(near_ref[n, b] * BS, BS), BS), :]
+        return stack[pl.ds(pl.multiple_of(near_ref[n * blocks + b] * BS, BS), BS), :]
 
     for b in range(blocks):
         if first and b % chunk == 0:
@@ -198,7 +200,7 @@
     b = k + side * (3 * edge - 1 - 2 * k)
     left, right = [], []
     for slot_at in range(edge - k):
-        entry = far_ref[side * edge + index, slot_at]
+        entry = far_ref[(side * edge + index) * HB + slot_at]
         slot = entry // 16
         left.append(ham_ref[b, slot])
         start = pl.multiple_of((entry - slot * 16) * BS, BS)
@@ -215,7 +217,7 @@
 def edge_kernel(scale, outer, far_ref, ham_ref, halo_ref, edge_ref, out_ref, stack):
     span = halo_ref.shape[0]
     edge = span // BS
-    core = far_ref[2 * edge, 0]
+    core = far_ref[2 * edge * HB]
     side = core if outer else 1 - core
     stack[:span] = halo_ref[...]
     stack[span:] = jnp.zeros((BS, TILE), BF16)
@@ -227,7 +229,7 @@
 def joined_kernel(scale, far_ref, ham_ref, inner_ref, outer_ref, edge_ref, mid_ref, out_ref, stack):
     span = inner_ref.shape[0]
     edge = span // BS
-    core = far_ref[2 * edge, 0]
+    core = far_ref[2 * edge * HB]
     for side, ref in ((1 - core, inner_ref), (core, outer_ref)):
         stack[side, :span] = ref[...]
         stack[side, span:] = jnp.zeros((BS, TILE), BF16)
@@ -247,13 +249,16 @@
     return at_row, at_col
 
 
-def gram_kernel(keep, pair_ref, list_ref, field_ref, out_ref, turned):
+def gram_kernel(keep, table_ref, field_ref, out_ref, turned, pair_ref, fetched):
     tiles = field_ref.shape[0]
-    core = pair_ref[tiles * REACH]
-    half = core if keep else 1 - core
+    fetch = pltpu.make_async_copy(table_ref, pair_ref, fetched.at[0])
+    fetch.start()
     at_row, at_col = places()
     for t in range(tiles):
         turned[t] = field_ref[t].T
+    fetch.wait()
+    core = pair_ref[tiles * REACH]
+    half = core if keep else 1 - core
 
     def block(low, high):
         return jnp.dot(turned[low], field_ref[high], preferred_element_type=F32)
@@ -268,7 +273,7 @@
         out_ref[k] = jnp.where(at_row <= at_col, upper, lower).astype(out_ref.dtype)
     out_ref[DIAG] = extra.astype(out_ref.dtype)
     for m in range(SIDE):
-        code = list_ref[half * SIDE + m]
+        code = pair_ref[tiles * REACH + 1 + half * SIDE + m]
         low = code // REACH
         high = low + code - low * REACH
         out_ref[DIAG + 1 + m] = block(low, high).astype(out_ref.dtype)
@@ -367,20 +372,19 @@
     place = jnp.stack(
         [row * blocks, jnp.int32(blocks * row_count), lax.axis_index("cuts"), row % 2]
     ).astype(jnp.int32)
-    near, far, pair, listed = pl.pallas_call(
+    near, far, pair = pl.pallas_call(
         table_kernel,
         out_shape=(
-            shape((slots + 1, blocks), jnp.int32),
-            shape((2 * blocks // 3 + 1, HB), jnp.int32),
-            shape((tiles * REACH + 1,), jnp.int32),
-            shape((2 * SIDE + 1,), jnp.int32),
+            shape((slots * blocks + 2,), jnp.int32),
+            shape((2 * blocks // 3 * HB + 1,), jnp.int32),
+            shape((tiles * REACH + LISTED,), jnp.int32),
         ),
         in_specs=smem(4),
-        out_specs=tuple(smem(4)),
+        out_specs=tuple(smem(3)),
         compiler_params=pltpu.CompilerParams(vmem_limit_bytes=1 << 20),
         cost_estimate=pl.CostEstimate(flops=1 << 20, bytes_accessed=1 << 12, transcendentals=0),
     )(place, neighbors.T, slice_widths, interval_index)
-    panel, near, far, pair, listed = lax.optimization_barrier((panel, near, far, pair, listed))
+    panel, near, far, pair = lax.optimization_barrier((panel, near, far, pair))
     work = 2 * blocks * slots * BS * BS * TILE
     outs = [shape((span, TILE)), shape((2, span, TILE), F32)]
     stacks = [VMEM((panel_rows, TILE), BF16), VMEM((panel_rows + BS, TILE), BF16)]
@@ -453,15 +457,21 @@
     field = lax.all_to_all(filtered.reshape(tiles, rows_mine, TILE), "cuts", 0, 0)
 
     def gram(keep):
-        (out,) = call(
+        return pl.pallas_call(
             functools.partial(gram_kernel, keep),
-            [shape((HALF, TILE, TILE), F32 if keep else BF16)],
-            [pair, listed],
-            [field],
-            [VMEM((tiles, TILE, rows_mine), BF16)],
-            1 << 28,
-        )
-        return out
+            out_shape=shape((HALF, TILE, TILE), F32 if keep else BF16),
+            in_specs=[pl.BlockSpec(memory_space=pl.ANY)] + vmem(1),
+            out_specs=pl.BlockSpec(memory_space=VMEM),
+            scratch_shapes=[
+                VMEM((tiles, TILE, rows_mine), BF16),
+                SMEM(pair.shape, jnp.int32),
+                pltpu.SemaphoreType.DMA((1,)),
+            ],
+            compiler_params=pltpu.CompilerParams(vmem_limit_bytes=24 << 20),
+            cost_estimate=pl.CostEstimate(
+                flops=1 << 28, bytes_accessed=1 << 21, transcendentals=0
+            ),
+        )(pair, field)
 
     partial = (gram(True) + exchange(gram(False)).astype(F32)).astype(BF16)
     cut_count = lax.axis_size("cuts")

time: 126 us -> 125 us (level)
  Pallas kernels: 30.9 us -> 28.7 us
    pallas_call x10 -> x8, Pallas kernels: 19.2 us -> 15.3 us  [call(): pl.pallas_call(kernel, out_shape=tuple(outs), in_specs=smem(len(scalars))...]
    pallas_call x1 -> x3, Pallas kernels: 4.38 us -> 6.14 us  [the longest x1 4 us: body(): pl.pallas_call(table_kernel, out_shape=(shape((slots * blocks + 2,), jnp....]
  transfers between devices with their start and end apart: 13 -> 13, of which waited for: 7 -> 7; matrix products, arithmetic and copies ran while one was open for 0% -> 0% of each run, Pallas kernels for 18% -> 17%
where the time goes in v6:
time: 125 us; the launch traced here: 124 us
  blocking collectives  44.1 us (35%)
  starting transfers between devices  32.8 us (26%)
  Pallas kernels  28.7 us (23%)
  waiting for transfers between devices  18.1 us (14%)
    all_to_all x1, blocking collectives, body(): lax.all_to_all(filtered.reshape(tiles, rows_mine, TILE), 'cuts', 0, 0)  16.1 us
    pallas_call x8, Pallas kernels, call(): pl.pallas_call(kernel, out_shape=tuple(outs), in_specs=smem(len(scalars))...  15.3 us
    all_to_all x1, blocking collectives, body(): lax.all_to_all(partial.reshape(cut_count, share, TILE), 'cuts', 0, 0)  14.7 us
    all_to_all x1, blocking collectives, body(): mine = lax.all_to_all(spread, 'cuts', 0, 0).reshape(HALF, TILE, TILE)  13.3 us
    ppermute x5, starting transfers between devices, exchange(): lax.ppermute(array, 'row', [(i, i ^ 1) for i in range(lax.axis_size('row'...  9.87 us
    ppermute x3, starting transfers between devices, swap_outer(): lax.ppermute(array, 'row', [(i, (i - 1 + 2 * (i % 2)) % size) for i in ra...  9.57 us
    all_to_all x1, waiting for transfers between devices, body(): panel = lax.all_to_all(turned, 'cuts', 0, 0).reshape(panel_rows, TILE)  8.68 us
    ppermute x4, waiting for transfers between devices, shift(): lax.ppermute(array, 'row', [(i, (i + 2 * chips * (1 - 2 * (i % 2))) % siz...  7.21 us
  transfers between devices with their start and end apart: 13, of which 7 were waited for; matrix products, arithmetic and copies ran while one was open for 0% of the time, Pallas kernels for 17%

profile of v6, /device:TPU:33, one launch (start us, length us, event | category | flops | bytes accessed | tf_op | source)
XLA Modules:
  0.0 124.4 jit_solution(16824014525788439469)
XLA Ops:
  0.0 2.0 %shard_map.55 = bf16[16,192,128]{2,1,0:T(8,128)(2,1)} custom-call(bf16[192,2048]{1,0:T(8,128)(2,1)} %start_ref.1), custom_call_target="tpu_custom_call" | custom-call | tf_op jit(solution)/shard_map/pallas_call | solution.py:357
  2.1 0.0 copy-start
  2.1 0.0 copy-start.1
  2.1 0.0 copy-start.2
  2.1 6.9 %all-to-all-start = ((bf16[16,192,128]{2,1,0:T(8,128)(2,1)}), bf16[16,192,128]{2,1,0:T(8,128)(2,1)S(1)}, u32[]{:S(2)}, u32[]{:S(2)}) async-start(bf16[16,192,128]{2,1,0:T(8,128)(2,1)} %shard_map.55), calls=%async_computation | async-start | bytes 1572864 | tf_op jit(solution)/shard_map/all_to_all | solution.py:369
  9.0 0.1 pad_add_fusion.where_ref
  9.1 0.0 copy-done
  9.1 0.0 copy-done.1
  9.1 0.0 copy-done.2
  9.1 4.0 %shard_map.56 = (s32[266]{0:T(512)S(1)}, s32[129]{0:T(256)S(1)}, s32[127]{0:T(128)S(1)}) custom-call(s32[4]{0:T(128)S(1)} %pad_add_fusion.where_ref, s32[11,24]{1,0:T(8,128)S(1)} %bitcast.11, s32[12]{0:T(128)S(1)} %copy-done.1, s32[12]{0:T(128)S(1)} %copy-done.2), custom_call_target="tpu_custom_call" | custom-call | flops 1048576 | bytes 4096 | tf_op jit(solution)/shard_map/pallas_call | solution.py:375
  13.1 8.7 %all-to-all-done = bf16[16,192,128]{2,1,0:T(8,128)(2,1)S(1)} async-done(((bf16[16,192,128]{2,1,0:T(8,128)(2,1)}), bf16[16,192,128]{2,1,0:T(8,128)(2,1)S(1)}, u32[]{:S(2)}, u32[]{:S(2)}) %all-to-all-start) | async-done | bytes 786464 | tf_op jit(solution)/shard_map/all_to_all | solution.py:369
  21.8 0.1 broadcast_select_fusion
  21.8 4.2 %collective-permute-start.2 = (bf16[1024,128]{1,0:T(8,128)(2,1)S(1)}, bf16[1024,128]{1,0:T(8,128)(2,1)S(1)}, u32[]{:S(2)}, u32[]{:S(2)}) collective-permute-start(bf16[1024,128]{1,0:T(8,128)(2,1)S(1)} %get-tuple-element.33.outer_ref.rest_2_), channel_id=1, source_target_pairs={{0,240},{16,32},{32,16},{48,64},{64,48},{80,96},{96,80},{112,128},... | collective-permute-start | bytes 786440 | tf_op jit(solution)/shard_map/ppermute | solution.py:337
  26.0 0.0 collective-permute-start
  26.0 5.1 %shard_map.57 = (bf16[1024,128]{1,0:T(8,128)(2,1)S(1)}, f32[2,1024,128]{2,1,0:T(8,128)S(1)}, bf16[24,11,128,128]{3,2,1,0:T(8,128)(2,1)S(1)}) custom-call(s32[266]{0:T(512)S(1)} %get-tuple-element.24.near_ref, bf16[24,11,128,128]{3,2,1,0:T(8,128)(2,1)} %ham_ref.1, bf16[1024,128]{1,0:T(8,128)(2,1)S(1)} %get-tuple-element.35.inner_ref.rest_0_, ...), custom_call_target="tpu_custom_call" | custom-call | flops 1107296256 | bytes 8650752 | tf_op jit(solution)/shard_map/pallas_call | solution.py:399
  31.2 0.0 collective-permute-done.2.halo_ref
  31.2 1.1 shard_map.59.outer_ref.rest_2_
  32.3 2.1 %collective-permute-start.4 = (bf16[1024,128]{1,0:T(8,128)(2,1)S(1)}, bf16[1024,128]{1,0:T(8,128)(2,1)S(1)}, u32[]{:S(2)}, u32[]{:S(2)}) collective-permute-start(bf16[1024,128]{1,0:T(8,128)(2,1)S(1)} %shard_map.59.outer_ref.rest_2_), channel_id=1, source_target_pairs={{0,240},{16,32},{32,16},{48,64},{64,48},{80,96},{96,80},{112,128},... | collective-permute-start | bytes 786440 | tf_op jit(solution)/shard_map/ppermute | solution.py:337
  34.4 0.0 collective-permute-done.halo_ref
  34.4 1.1 shard_map.58.inner_ref.rest_0_
  35.5 0.1 collective-permute-start.1
  35.6 3.2 %shard_map.60 = (bf16[1024,128]{1,0:T(8,128)(2,1)S(1)}, f32[2,1024,128]{2,1,0:T(8,128)S(1)}) custom-call(s32[266]{0:T(512)S(1)} %get-tuple-element.24.near_ref, bf16[24,11,128,128]{3,2,1,0:T(8,128)(2,1)S(1)} %get-tuple-element.26.ham_ref, bf16[1024,128]{1,0:T(8,128)(2,1)S(1)} %shard_map.58.inner_ref.rest_0_, ...), custom_call_target="tpu_custom_call" | custom-call | flops 1107296256 | bytes 11534336 | tf_op jit(solution)/shard_map/pallas_call | solution.py:37
  38.8 0.0 collective-permute-done.4.halo_ref
  38.8 1.1 shard_map.62.outer_ref
  39.9 3.3 %collective-permute-start.5 = (bf16[1024,128]{1,0:T(8,128)(2,1)S(1)}, bf16[1024,128]{1,0:T(8,128)(2,1)S(1)}, u32[]{:S(2)}, u32[]{:S(2)}) collective-permute-start(bf16[1024,128]{1,0:T(8,128)(2,1)S(1)} %shard_map.62.outer_ref), channel_id=1, source_target_pairs={{0,240},{16,32},{32,16},{48,64},{64,48},{80,96},{96,80},{112,128},... | collective-permute-start | bytes 786440 | tf_op jit(solution)/shard_map/ppermute | solution.py:337
  43.2 0.0 collective-permute-done.1.halo_ref
  43.2 1.1 shard_map.61.inner_ref
  44.3 0.3 collective-permute-start.3
  44.6 3.2 %shard_map.63 = (bf16[1024,128]{1,0:T(8,128)(2,1)S(1)}, f32[2,1024,128]{2,1,0:T(8,128)S(1)}) custom-call(s32[266]{0:T(512)S(1)} %get-tuple-element.24.near_ref, bf16[24,11,128,128]{3,2,1,0:T(8,128)(2,1)S(1)} %get-tuple-element.26.ham_ref, bf16[1024,128]{1,0:T(8,128)(2,1)S(1)} %shard_map.61.inner_ref, bf16[1024,128]{1,0:T(8,128)(2,1)S(1)} %get-tuple-element.30.mid_ref, ...), custom_call_target="tpu_custom_call" | custom-call | flops 1107296256 | bytes 11534336 | tf_op jit(solution)/shard_map/pallas_call | solution.py:37
  47.8 0.0 collective-permute-done.5.outer_ref
  47.8 0.0 collective-permute-done.3.inner_ref
  47.8 1.4 %shard_map.64 = bf16[3072,128]{1,0:T(8,128)(2,1)S(1)} custom-call(s32[129]{0:T(256)S(1)} %get-tuple-element.23.far_ref, bf16[24,11,128,128]{3,2,1,0:T(8,128)(2,1)S(1)} %get-tuple-element.26.ham_ref, bf16[1024,128]{1,0:T(8,128)(2,1)S(1)} %collective-permute-done.3.inner_ref, bf16[1024,128]{1,0:T(8,128)(2,1)S(1)} %collective-permute-done.5.outer_ref, ...), custom_call_target="tpu_custom_call" | custom-call | flops 276824064 | bytes 11272192 | tf_op jit(solution)/shard_map/pallas_call | solution.py:37
  49.3 16.1 %all_to_all.20.field_ref = bf16[16,192,128]{2,1,0:T(8,128)(2,1)S(1)} all-to-all(bf16[16,192,128]{2,1,0:T(8,128)(2,1)S(1)} %bitcast.8), channel_id=1, replica_groups=mesh['row'=16,'cuts'=16] {'cuts'}, dimensions={0} | all-to-all | bytes 1572864 | tf_op jit(solution)/shard_map/all_to_all | solution.py:457
  65.4 1.1 shard_map.66
  66.5 1.9 %collective-permute-start.6 = (bf16[18,128,128]{2,1,0:T(8,128)(2,1)S(1)}, bf16[18,128,128]{2,1,0:T(8,128)(2,1)S(1)}, u32[]{:S(2)}, u32[]{:S(2)}) collective-permute-start(bf16[18,128,128]{2,1,0:T(8,128)(2,1)S(1)} %shard_map.66), channel_id=1, source_target_pairs={{0,16},{16,0},{32,48},{48,32},{64,80},{80,64},{96,112},{112,96},{1... | collective-permute-start | bytes 1769480 | tf_op jit(solution)/shard_map/ppermute | solution.py:332
  68.4 1.1 shard_map.65
  69.5 0.6 collective-permute-done.6
  70.0 0.1 add_convert_fusion
  70.2 14.7 %all_to_all.21 = bf16[16,144,128]{2,1,0:T(8,128)(2,1)S(1)} all-to-all(bf16[16,144,128]{2,1,0:T(8,128)(2,1)S(1)} %bitcast.13), channel_id=1, replica_groups=mesh['row'=16,'cuts'=16] {'cuts'}, dimensions={0} | all-to-all | bytes 1179648 | tf_op jit(solution)/shard_map/all_to_all | solution.py:479
  84.9 0.1 reduce_sum.12
  84.9 1.5 %collective-permute-start.7 = (bf16[144,128]{1,0:T(8,128)(2,1)S(1)}, bf16[144,128]{1,0:T(8,128)(2,1)S(1)}, u32[]{:S(2)}, u32[]{:S(2)}) collective-permute-start(bf16[144,128]{1,0:T(8,128)(2,1)S(1)} %reduce_sum.12), channel_id=1, source_target_pairs={{0,224},{16,48},{32,0},{48,80},{64,32},{80,112},{96,64},{112,144},... | collective-permute-start | bytes 110600 | tf_op jit(solution)/shard_map/ppermute | solution.py:326
  86.5 0.4 collective-permute-start.8
  86.8 1.3 %collective-permute-done.7 = bf16[144,128]{1,0:T(8,128)(2,1)S(1)} collective-permute-done((bf16[144,128]{1,0:T(8,128)(2,1)S(1)}, bf16[144,128]{1,0:T(8,128)(2,1)S(1)}, u32[]{:S(2)}, u32[]{:S(2)}) %collective-permute-start.7) | collective-permute-done | bytes 36896 | tf_op jit(solution)/shard_map/ppermute | solution.py:326
  88.1 2.5 %collective-permute-done.8 = bf16[144,128]{1,0:T(8,128)(2,1)S(1)} collective-permute-done((bf16[144,128]{1,0:T(8,128)(2,1)S(1)}, bf16[144,128]{1,0:T(8,128)(2,1)S(1)}, u32[]{:S(2)}, u32[]{:S(2)}) %collective-permute-start.8) | collective-permute-done | bytes 36896 | tf_op jit(solution)/shard_map/ppermute | solution.py:326
  90.6 2.2 %collective-permute-start.10 = (bf16[144,128]{1,0:T(8,128)(2,1)S(1)}, bf16[144,128]{1,0:T(8,128)(2,1)S(1)}, u32[]{:S(2)}, u32[]{:S(2)}) collective-permute-start(bf16[144,128]{1,0:T(8,128)(2,1)S(1)} %get-tuple-element.37), channel_id=1, source_target_pairs={{0,96},{16,176},{32,128},{48,208},{64,160},{80,240},{96,192},{112,... | collective-permute-start | bytes 110600 | tf_op jit(solution)/shard_map/ppermute | solution.py:326
  92.8 2.4 %collective-permute-start.9 = (bf16[144,128]{1,0:T(8,128)(2,1)S(1)}, bf16[144,128]{1,0:T(8,128)(2,1)S(1)}, u32[]{:S(2)}, u32[]{:S(2)}) collective-permute-start(bf16[144,128]{1,0:T(8,128)(2,1)S(1)} %get-tuple-element.36), channel_id=1, source_target_pairs={{0,160},{16,112},{32,192},{48,144},{64,224},{80,176},{96,0},{112,2... | collective-permute-start | bytes 110600 | tf_op jit(solution)/shard_map/ppermute | solution.py:326
  95.2 1.3 %collective-permute-done.10 = bf16[144,128]{1,0:T(8,128)(2,1)S(1)} collective-permute-done((bf16[144,128]{1,0:T(8,128)(2,1)S(1)}, bf16[144,128]{1,0:T(8,128)(2,1)S(1)}, u32[]{:S(2)}, u32[]{:S(2)}) %collective-permute-start.10) | collective-permute-done | bytes 36896 | tf_op jit(solution)/shard_map/ppermute | solution.py:326
  96.5 2.1 %collective-permute-done.9 = bf16[144,128]{1,0:T(8,128)(2,1)S(1)} collective-permute-done((bf16[144,128]{1,0:T(8,128)(2,1)S(1)}, bf16[144,128]{1,0:T(8,128)(2,1)S(1)}, u32[]{:S(2)}, u32[]{:S(2)}) %collective-permute-start.9) | collective-permute-done | bytes 36896 | tf_op jit(solution)/shard_map/ppermute | solution.py:326
  98.7 0.1 broadcast_in_dim.2
  98.7 13.3 %all_to_all.22 = bf16[16,144,128]{2,1,0:T(8,128)(2,1)S(1)} all-to-all(bf16[16,144,128]{2,1,0:T(8,128)(2,1)S(1)} %broadcast_in_dim.2), channel_id=1, replica_groups=mesh['row'=16,'cuts'=16] {'cuts'}, dimensions={0} | all-to-all | bytes 1179648 | tf_op jit(solution)/shard_map/all_to_all | solution.py:482
  112.1 7.5 %collective-permute-start.11 = (bf16[18,128,128]{2,1,0:T(8,128)(2,1)S(1)}, bf16[18,128,128]{2,1,0:T(8,128)(2,1)S(1)}, u32[]{:S(2)}, u32[]{:S(2)}) collective-permute-start(bf16[18,128,128]{2,1,0:T(8,128)(2,1)S(1)} %bitcast.9), channel_id=1, source_target_pairs={{0,16},{16,0},{32,48},{48,32},{64,80},{80,64},{96,112},{112,96},{1... | collective-permute-start | bytes 1769480 | tf_op jit(solution)/shard_map/ppermute | solution.py:332
  119.6 1.6 %collective-permute-done.11.other_ref = bf16[18,128,128]{2,1,0:T(8,128)(2,1)S(1)} collective-permute-done((bf16[18,128,128]{2,1,0:T(8,128)(2,1)S(1)}, bf16[18,128,128]{2,1,0:T(8,128)(2,1)S(1)}, u32[]{:S(2)}, u32[]{:S(2)}) %collective-permute-start.11) | collective-permute-done | bytes 589856 | tf_op jit(solution)/shard_map/ppermute | solution.py:332
  121.2 3.2 %shard_map.67 = bf16[192,2048]{1,0:T(8,128)(2,1)} custom-call(s32[127]{0:T(128)S(1)} %get-tuple-element.22.table_ref.pair_ref, bf16[16,192,128]{2,1,0:T(8,128)(2,1)S(1)} %all_to_all.20.field_ref, bf16[18,128,128]{2,1,0:T(8,128)(2,1)S(1)} %bitcast.10, bf16[18,128,128]{2,1,0:T(8,128)(2,1)S(1)} %collective-permute-done.11.other_ref), custom_call_target="tpu_custom_call" | custom-call | flops 536870912 | bytes 2752512 | tf_op jit(solution)/shard_map/pallas_call | solution.py:37
  (2 shorter events, 0.1 us)
Async XLA Ops:
  2.1 7.0 %copy-start = (s32[24,11]{0,1:T(8,128)S(1)}, s32[24,11]{0,1:T(8,128)}, u32[]{:S(2)}) copy-start(s32[24,11]{0,1:T(8,128)} %param.6) | copy-start | bytes 3172
  2.1 7.0 %copy-start.1 = (s32[12]{0:T(128)S(1)}, s32[12]{0:T(128)}, u32[]{:S(2)}) copy-start(s32[12]{0:T(128)} %width_ref.1) | copy-start | bytes 148
  2.1 7.0 %copy-start.2 = (s32[12]{0:T(128)S(1)}, s32[12]{0:T(128)}, u32[]{:S(2)}) copy-start(s32[12]{0:T(128)} %interval_ref.1) | copy-start | bytes 148
  2.1 19.7 %all-to-all-start = ((bf16[16,192,128]{2,1,0:T(8,128)(2,1)}), bf16[16,192,128]{2,1,0:T(8,128)(2,1)S(1)}, u32[]{:S(2)}, u32[]{:S(2)}) async-start(bf16[16,192,128]{2,1,0:T(8,128)(2,1)} %shard_map.55), calls=%async_computation | async-start | bytes 1572864 | tf_op jit(solution)/shard_map/all_to_all | solution.py:369
  21.8 9.3 %collective-permute-start.2 = (bf16[1024,128]{1,0:T(8,128)(2,1)S(1)}, bf16[1024,128]{1,0:T(8,128)(2,1)S(1)}, u32[]{:S(2)}, u32[]{:S(2)}) collective-permute-start(bf16[1024,128]{1,0:T(8,128)(2,1)S(1)} %get-tuple-element.33.outer_ref.rest_2_), channel_id=1, source_target_pairs={{0,240},{16,32},{32,16},{48,64},{64,48},{80,96},{96,80},{112,128},... | collective-permute-start | bytes 786440 | tf_op jit(solution)/shard_map/ppermute | solution.py:337
  26.0 8.4 %collective-permute-start = (bf16[1024,128]{1,0:T(8,128)(2,1)S(1)}, bf16[1024,128]{1,0:T(8,128)(2,1)S(1)}, u32[]{:S(2)}, u32[]{:S(2)}) collective-permute-start(bf16[1024,128]{1,0:T(8,128)(2,1)S(1)} %get-tuple-element.35.inner_ref.rest_0_), channel_id=1, source_target_pairs={{0,16},{16,0},{32,48},{48,32},{64,80},{80,64},{96,112},{112,96},{1... | collective-permute-start | bytes 786440 | tf_op jit(solution)/shard_map/ppermute | solution.py:332
  32.3 6.6 %collective-permute-start.4 = (bf16[1024,128]{1,0:T(8,128)(2,1)S(1)}, bf16[1024,128]{1,0:T(8,128)(2,1)S(1)}, u32[]{:S(2)}, u32[]{:S(2)}) collective-permute-start(bf16[1024,128]{1,0:T(8,128)(2,1)S(1)} %shard_map.59.outer_ref.rest_2_), channel_id=1, source_target_pairs={{0,240},{16,32},{32,16},{48,64},{64,48},{80,96},{96,80},{112,128},... | collective-permute-start | bytes 786440 | tf_op jit(solution)/shard_map/ppermute | solution.py:337
  35.5 7.7 %collective-permute-start.1 = (bf16[1024,128]{1,0:T(8,128)(2,1)S(1)}, bf16[1024,128]{1,0:T(8,128)(2,1)S(1)}, u32[]{:S(2)}, u32[]{:S(2)}) collective-permute-start(bf16[1024,128]{1,0:T(8,128)(2,1)S(1)} %shard_map.58.inner_ref.rest_0_), channel_id=1, source_target_pairs={{0,16},{16,0},{32,48},{48,32},{64,80},{80,64},{96,112},{112,96},{1... | collective-permute-start | bytes 786440 | tf_op jit(solution)/shard_map/ppermute | solution.py:332
  39.9 7.9 %collective-permute-start.5 = (bf16[1024,128]{1,0:T(8,128)(2,1)S(1)}, bf16[1024,128]{1,0:T(8,128)(2,1)S(1)}, u32[]{:S(2)}, u32[]{:S(2)}) collective-permute-start(bf16[1024,128]{1,0:T(8,128)(2,1)S(1)} %shard_map.62.outer_ref), channel_id=1, source_target_pairs={{0,240},{16,32},{32,16},{48,64},{64,48},{80,96},{96,80},{112,128},... | collective-permute-start | bytes 786440 | tf_op jit(solution)/shard_map/ppermute | solution.py:337
  44.3 3.5 %collective-permute-start.3 = (bf16[1024,128]{1,0:T(8,128)(2,1)S(1)}, bf16[1024,128]{1,0:T(8,128)(2,1)S(1)}, u32[]{:S(2)}, u32[]{:S(2)}) collective-permute-start(bf16[1024,128]{1,0:T(8,128)(2,1)S(1)} %shard_map.61.inner_ref), channel_id=1, source_target_pairs={{0,16},{16,0},{32,48},{48,32},{64,80},{80,64},{96,112},{112,96},{1... | collective-permute-start | bytes 786440 | tf_op jit(solution)/shard_map/ppermute | solution.py:332
  66.5 3.5 %collective-permute-start.6 = (bf16[18,128,128]{2,1,0:T(8,128)(2,1)S(1)}, bf16[18,128,128]{2,1,0:T(8,128)(2,1)S(1)}, u32[]{:S(2)}, u32[]{:S(2)}) collective-permute-start(bf16[18,128,128]{2,1,0:T(8,128)(2,1)S(1)} %shard_map.66), channel_id=1, source_target_pairs={{0,16},{16,0},{32,48},{48,32},{64,80},{80,64},{96,112},{112,96},{1... | collective-permute-start | bytes 1769480 | tf_op jit(solution)/shard_map/ppermute | solution.py:332
  84.9 3.2 %collective-permute-start.7 = (bf16[144,128]{1,0:T(8,128)(2,1)S(1)}, bf16[144,128]{1,0:T(8,128)(2,1)S(1)}, u32[]{:S(2)}, u32[]{:S(2)}) collective-permute-start(bf16[144,128]{1,0:T(8,128)(2,1)S(1)} %reduce_sum.12), channel_id=1, source_target_pairs={{0,224},{16,48},{32,0},{48,80},{64,32},{80,112},{96,64},{112,144},... | collective-permute-start | bytes 110600 | tf_op jit(solution)/shard_map/ppermute | solution.py:326
  86.5 4.1 %collective-permute-start.8 = (bf16[144,128]{1,0:T(8,128)(2,1)S(1)}, bf16[144,128]{1,0:T(8,128)(2,1)S(1)}, u32[]{:S(2)}, u32[]{:S(2)}) collective-permute-start(bf16[144,128]{1,0:T(8,128)(2,1)S(1)} %reduce_sum.12), channel_id=1, source_target_pairs={{0,32},{16,240},{32,64},{48,16},{64,96},{80,48},{96,128},{112,80},... | collective-permute-start | bytes 110600 | tf_op jit(solution)/shard_map/ppermute | solution.py:326
  90.6 5.9 %collective-permute-start.10 = (bf16[144,128]{1,0:T(8,128)(2,1)S(1)}, bf16[144,128]{1,0:T(8,128)(2,1)S(1)}, u32[]{:S(2)}, u32[]{:S(2)}) collective-permute-start(bf16[144,128]{1,0:T(8,128)(2,1)S(1)} %get-tuple-element.37), channel_id=1, source_target_pairs={{0,96},{16,176},{32,128},{48,208},{64,160},{80,240},{96,192},{112,... | collective-permute-start | bytes 110600 | tf_op jit(solution)/shard_map/ppermute | solution.py:326
  92.8 5.8 %collective-permute-start.9 = (bf16[144,128]{1,0:T(8,128)(2,1)S(1)}, bf16[144,128]{1,0:T(8,128)(2,1)S(1)}, u32[]{:S(2)}, u32[]{:S(2)}) collective-permute-start(bf16[144,128]{1,0:T(8,128)(2,1)S(1)} %get-tuple-element.36), channel_id=1, source_target_pairs={{0,160},{16,112},{32,192},{48,144},{64,224},{80,176},{96,0},{112,2... | collective-permute-start | bytes 110600 | tf_op jit(solution)/shard_map/ppermute | solution.py:326
  112.1 9.2 %collective-permute-start.11 = (bf16[18,128,128]{2,1,0:T(8,128)(2,1)S(1)}, bf16[18,128,128]{2,1,0:T(8,128)(2,1)S(1)}, u32[]{:S(2)}, u32[]{:S(2)}) collective-permute-start(bf16[18,128,128]{2,1,0:T(8,128)(2,1)S(1)} %bitcast.9), channel_id=1, source_target_pairs={{0,16},{16,0},{32,48},{48,32},{64,80},{80,64},{96,112},{112,96},{1... | collective-permute-start | bytes 1769480 | tf_op jit(solution)/shard_map/ppermute | solution.py:332

commit v7 on v6

--- a/solution.py
+++ b/solution.py
@@ -32,14 +32,19 @@
     return [pl.BlockSpec(memory_space=SMEM)] * count
 
 
-def call(kernel, outs, scalars, arrays, scratch=(), flops=0, limit=24 << 20):
+def anywhere(count):
+    return [pl.BlockSpec(memory_space=pl.ANY)] * count
+
+
+def call(kernel, outs, scalars, arrays, scratch=(), flops=0, limit=24 << 20, fetch=False):
     moved = sum(a.size * a.dtype.itemsize for a in (*arrays, *outs))
     return pl.pallas_call(
         kernel,
         out_shape=tuple(outs),
-        in_specs=smem(len(scalars)) + vmem(len(arrays)),
+        in_specs=(anywhere(1) if fetch else smem(len(scalars))) + vmem(len(arrays)),
         out_specs=tuple(vmem(len(outs))),
-        scratch_shapes=list(scratch),
+        scratch_shapes=list(scratch)
+        + [SMEM(scalars[0].shape, jnp.int32), pltpu.SemaphoreType.DMA((1,))] * fetch,
         compiler_params=pltpu.CompilerParams(vmem_limit_bytes=limit),
         cost_estimate=pl.CostEstimate(flops=flops, bytes_accessed=moved, transcendentals=0),
     )(*scalars, *arrays)
@@ -195,49 +200,74 @@
             edge_out[part // 2, here, :] = value
 
 
-def add_halo(scale, far_ref, ham_ref, stack, edge_ref, side, k, edge):
-    index = k + side * (edge - 1 - 2 * k)
-    b = k + side * (3 * edge - 1 - 2 * k)
+def own_core():
+    return lax.rem(lax.axis_index("row"), 2)
+
+
+def lines_of(side, k, edge):
+    return k + side * (edge - 1 - 2 * k), k + side * (3 * edge - 1 - 2 * k)
+
+
+def add_outermost(scale, ham_ref, stack, edge_ref, total_ref, side, k, edge):
+    index, b = lines_of(side, k, edge)
+    here = pl.ds(pl.multiple_of(index * BS, BS), BS)
+    part = jnp.dot(ham_ref[b, 2 - side], stack[here, :], preferred_element_type=F32)
+    total_ref[k] = edge_ref[side, here, :] + scale * part
+
+
+def add_listed(scale, far_ref, ham_ref, stack, total_ref, side, k, edge):
+    index, b = lines_of(side, k, edge)
     left, right = [], []
-    for slot_at in range(edge - k):
+    for slot_at in range(1, edge - k):
         entry = far_ref[(side * edge + index) * HB + slot_at]
         slot = entry // 16
         left.append(ham_ref[b, slot])
         start = pl.multiple_of((entry - slot * 16) * BS, BS)
         right.append(stack[pl.ds(start, BS), :])
-    here = pl.ds(pl.multiple_of(index * BS, BS), BS)
-    total = edge_ref[side, here, :]
-    for slot_at in range(0, edge - k, 2):
-        lhs = jnp.concatenate(left[slot_at : slot_at + 2], axis=1)
-        rhs = jnp.concatenate(right[slot_at : slot_at + 2], axis=0)
+    total = total_ref[k]
+    for at in range(0, len(left), 2):
+        lhs = jnp.concatenate(left[at : at + 2], axis=1)
+        rhs = jnp.concatenate(right[at : at + 2], axis=0)
         total += scale * jnp.dot(lhs, rhs, preferred_element_type=F32)
     return index, total.astype(BF16)
 
 
-def edge_kernel(scale, outer, far_ref, ham_ref, halo_ref, edge_ref, out_ref, stack):
+def edge_kernel(scale, outer, table_ref, ham_ref, halo_ref, edge_ref, out_ref, stack, total_ref, far_ref, fetched):
+    fetch = pltpu.make_async_copy(table_ref, far_ref, fetched.at[0])
+    fetch.start()
     span = halo_ref.shape[0]
     edge = span // BS
-    core = far_ref[2 * edge * HB]
+    core = own_core()
     side = core if outer else 1 - core
     stack[:span] = halo_ref[...]
     stack[span:] = jnp.zeros((BS, TILE), BF16)
     for k in range(edge):
-        index, value = add_halo(scale, far_ref, ham_ref, stack, edge_ref, side, k, edge)
+        add_outermost(scale, ham_ref, stack, edge_ref, total_ref, side, k, edge)
+    fetch.wait()
+    for k in range(edge):
+        index, value = add_listed(scale, far_ref, ham_ref, stack, total_ref, side, k, edge)
         out_ref[pl.ds(pl.multiple_of(index * BS, BS), BS), :] = value
 
 
-def joined_kernel(scale, far_ref, ham_ref, inner_ref, outer_ref, edge_ref, mid_ref, out_ref, stack):
+def joined_kernel(scale, table_ref, ham_ref, inner_ref, outer_ref, edge_ref, mid_ref, out_ref, stack, total_ref, far_ref, fetched):
+    fetch = pltpu.make_async_copy(table_ref, far_ref, fetched.at[0])
+    fetch.start()
     span = inner_ref.shape[0]
     edge = span // BS
-    core = far_ref[2 * edge * HB]
+    core = own_core()
     for side, ref in ((1 - core, inner_ref), (core, outer_ref)):
         stack[side, :span] = ref[...]
         stack[side, span:] = jnp.zeros((BS, TILE), BF16)
     out_ref[span : 2 * span, :] = mid_ref[...]
     for side in range(2):
         for k in range(edge):
-            index, value = add_halo(
-                scale, far_ref, ham_ref, stack.at[side], edge_ref, side, k, edge
+            total = total_ref.at[side]
+            add_outermost(scale, ham_ref, stack.at[side], edge_ref, total, side, k, edge)
+    fetch.wait()
+    for side in range(2):
+        for k in range(edge):
+            index, value = add_listed(
+                scale, far_ref, ham_ref, stack.at[side], total_ref.at[side], side, k, edge
             )
             at = side * 2 * span + index * BS
             out_ref[at : at + BS, :] = value
@@ -279,9 +309,11 @@
         out_ref[DIAG + 1 + m] = block(low, high).astype(out_ref.dtype)
 
 
-def correct_kernel(rows_all, pair_ref, field_ref, mine_ref, other_ref, out_ref, gram, own, scaled, norm):
+def correct_kernel(rows_all, table_ref, field_ref, mine_ref, other_ref, out_ref, gram, own, scaled, norm, pair_ref, fetched):
+    fetch = pltpu.make_async_copy(table_ref, pair_ref, fetched.at[0])
+    fetch.start()
     tiles = field_ref.shape[0]
-    core = pair_ref[tiles * REACH]
+    core = own_core()
     gram[pl.ds(core * HALF, HALF)] = mine_ref[...]
     gram[pl.ds(HALF - core * HALF, HALF)] = other_ref[...]
     gram[ZERO] = jnp.zeros((TILE, TILE), BF16)
@@ -303,6 +335,7 @@
         squares = gram[half * HALF + DIAG].astype(F32)[k : k + 1, :]
         lower = jnp.where(at_row > at_col, packed, flipped)
         prepare(2 * q + 1, jnp.where(at_row == at_col, squares, lower), squares)
+    fetch.wait()
     for j in range(tiles):
         below = range(max(0, j - REACH + 1), j)
         left = jnp.concatenate([scaled[i] for i in below] + [scaled[j]], axis=1)
@@ -376,7 +409,7 @@
         table_kernel,
         out_shape=(
             shape((slots * blocks + 2,), jnp.int32),
-            shape((2 * blocks // 3 * HB + 1,), jnp.int32),
+            shape((2 * blocks // 3 * HB + 128,), jnp.int32),
             shape((tiles * REACH + LISTED,), jnp.int32),
         ),
         in_specs=smem(4),
@@ -430,8 +463,9 @@
                 [shape((span, TILE))],
                 [far],
                 [ham, halo, edges],
-                [VMEM((span + BS, TILE), BF16)],
+                [VMEM((span + BS, TILE), BF16), VMEM((span // BS, BS, TILE), F32)],
                 work // 8,
+                fetch=True,
             )
             return out
 
@@ -450,8 +484,9 @@
         [shape((panel_rows, TILE))],
         [far],
         [ham, from_inner, from_outer, edges, mid],
-        [VMEM((2, span + BS, TILE), BF16)],
+        [VMEM((2, span + BS, TILE), BF16), VMEM((2, span // BS, BS, TILE), F32)],
         work // 4,
+        fetch=True,
     )
 
     field = lax.all_to_all(filtered.reshape(tiles, rows_mine, TILE), "cuts", 0, 0)
@@ -493,6 +528,7 @@
             VMEM((tiles, TILE), F32),
         ],
         1 << 29,
+        fetch=True,
     )
     return corrected
 

time: 125 us -> 125 us (level)
  no operation moved by 1% of the time
where the time goes in v7:
time: 125 us; the launch traced here: 124 us
  blocking collectives  44.1 us (35%)
  starting transfers between devices  32.8 us (26%)
  Pallas kernels  28.5 us (23%)
  waiting for transfers between devices  18.1 us (14%)
    all_to_all x1, blocking collectives, body(): lax.all_to_all(filtered.reshape(tiles, rows_mine, TILE), 'cuts', 0, 0)  16.1 us
    pallas_call x8, Pallas kernels, call(): pl.pallas_call(kernel, out_shape=tuple(outs), in_specs=(anywhere(1) if fe...  15.2 us
    all_to_all x1, blocking collectives, body(): lax.all_to_all(partial.reshape(cut_count, share, TILE), 'cuts', 0, 0)  14.7 us
    all_to_all x1, blocking collectives, body(): mine = lax.all_to_all(spread, 'cuts', 0, 0).reshape(HALF, TILE, TILE)  13.3 us
    ppermute x5, starting transfers between devices, exchange(): lax.ppermute(array, 'row', [(i, i ^ 1) for i in range(lax.axis_size('row'...  9.86 us
    ppermute x3, starting transfers between devices, swap_outer(): lax.ppermute(array, 'row', [(i, (i - 1 + 2 * (i % 2)) % size) for i in ra...  9.58 us
    all_to_all x1, waiting for transfers between devices, body(): panel = lax.all_to_all(turned, 'cuts', 0, 0).reshape(panel_rows, TILE)  8.68 us
    ppermute x4, waiting for transfers between devices, shift(): lax.ppermute(array, 'row', [(i, (i + 2 * chips * (1 - 2 * (i % 2))) % siz...  7.2 us
  transfers between devices with their start and end apart: 13, of which 7 were waited for; matrix products, arithmetic and copies ran while one was open for 0% of the time, Pallas kernels for 17%

profile of v7, /device:TPU:33, one launch (start us, length us, event | category | flops | bytes accessed | tf_op | source)
XLA Modules:
  0.0 124.4 jit_solution(497650883027250459)
XLA Ops:
  0.0 2.0 %shard_map.55 = bf16[16,192,128]{2,1,0:T(8,128)(2,1)} custom-call(bf16[192,2048]{1,0:T(8,128)(2,1)} %start_ref.1), custom_call_target="tpu_custom_call" | custom-call | tf_op jit(solution)/shard_map/pallas_call | solution.py:390
  2.1 0.0 copy-start
  2.1 0.0 copy-start.1
  2.1 0.0 copy-start.2
  2.1 6.9 %all-to-all-start = ((bf16[16,192,128]{2,1,0:T(8,128)(2,1)}), bf16[16,192,128]{2,1,0:T(8,128)(2,1)S(1)}, u32[]{:S(2)}, u32[]{:S(2)}) async-start(bf16[16,192,128]{2,1,0:T(8,128)(2,1)} %shard_map.55), calls=%async_computation | async-start | bytes 1572864 | tf_op jit(solution)/shard_map/all_to_all | solution.py:402
  9.0 0.1 pad_add_fusion.where_ref
  9.1 0.0 copy-done
  9.1 0.0 copy-done.1
  9.1 0.0 copy-done.2
  9.1 4.0 %shard_map.56 = (s32[266]{0:T(512)S(1)}, s32[256]{0:T(256)S(1)}, s32[127]{0:T(128)S(1)}) custom-call(s32[4]{0:T(128)S(1)} %pad_add_fusion.where_ref, s32[11,24]{1,0:T(8,128)S(1)} %bitcast.11, s32[12]{0:T(128)S(1)} %copy-done.1, s32[12]{0:T(128)S(1)} %copy-done.2), custom_call_target="tpu_custom_call" | custom-call | flops 1048576 | bytes 4096 | tf_op jit(solution)/shard_map/pallas_call | solution.py:408
  13.1 8.7 %all-to-all-done = bf16[16,192,128]{2,1,0:T(8,128)(2,1)S(1)} async-done(((bf16[16,192,128]{2,1,0:T(8,128)(2,1)}), bf16[16,192,128]{2,1,0:T(8,128)(2,1)S(1)}, u32[]{:S(2)}, u32[]{:S(2)}) %all-to-all-start) | async-done | bytes 786464 | tf_op jit(solution)/shard_map/all_to_all | solution.py:402
  21.8 0.1 broadcast_select_fusion
  21.8 4.2 %collective-permute-start.2 = (bf16[1024,128]{1,0:T(8,128)(2,1)S(1)}, bf16[1024,128]{1,0:T(8,128)(2,1)S(1)}, u32[]{:S(2)}, u32[]{:S(2)}) collective-permute-start(bf16[1024,128]{1,0:T(8,128)(2,1)S(1)} %get-tuple-element.33.outer_ref.rest_2_), channel_id=1, source_target_pairs={{0,240},{16,32},{32,16},{48,64},{64,48},{80,96},{96,80},{112,128},... | collective-permute-start | bytes 786440 | tf_op jit(solution)/shard_map/ppermute | solution.py:370
  26.0 0.0 collective-permute-start
  26.0 5.1 %shard_map.57 = (bf16[1024,128]{1,0:T(8,128)(2,1)S(1)}, f32[2,1024,128]{2,1,0:T(8,128)S(1)}, bf16[24,11,128,128]{3,2,1,0:T(8,128)(2,1)S(1)}) custom-call(s32[266]{0:T(512)S(1)} %get-tuple-element.24.near_ref, bf16[24,11,128,128]{3,2,1,0:T(8,128)(2,1)} %ham_ref.1, bf16[1024,128]{1,0:T(8,128)(2,1)S(1)} %get-tuple-element.35.inner_ref.rest_0_, ...), custom_call_target="tpu_custom_call" | custom-call | flops 1107296256 | bytes 8650752 | tf_op jit(solution)/shard_map/pallas_call | solution.py:432
  31.2 0.0 collective-permute-done.2.halo_ref
  31.2 1.1 shard_map.59.outer_ref.rest_2_
  32.3 2.1 %collective-permute-start.4 = (bf16[1024,128]{1,0:T(8,128)(2,1)S(1)}, bf16[1024,128]{1,0:T(8,128)(2,1)S(1)}, u32[]{:S(2)}, u32[]{:S(2)}) collective-permute-start(bf16[1024,128]{1,0:T(8,128)(2,1)S(1)} %shard_map.59.outer_ref.rest_2_), channel_id=1, source_target_pairs={{0,240},{16,32},{32,16},{48,64},{64,48},{80,96},{96,80},{112,128},... | collective-permute-start | bytes 786440 | tf_op jit(solution)/shard_map/ppermute | solution.py:370
  34.4 0.0 collective-permute-done.halo_ref
  34.4 1.1 shard_map.58.inner_ref.rest_0_
  35.5 0.1 collective-permute-start.1
  35.7 3.2 %shard_map.60 = (bf16[1024,128]{1,0:T(8,128)(2,1)S(1)}, f32[2,1024,128]{2,1,0:T(8,128)S(1)}) custom-call(s32[266]{0:T(512)S(1)} %get-tuple-element.24.near_ref, bf16[24,11,128,128]{3,2,1,0:T(8,128)(2,1)S(1)} %get-tuple-element.26.ham_ref, bf16[1024,128]{1,0:T(8,128)(2,1)S(1)} %shard_map.58.inner_ref.rest_0_, ...), custom_call_target="tpu_custom_call" | custom-call | flops 1107296256 | bytes 11534336 | tf_op jit(solution)/shard_map/pallas_call | solution.py:41
  38.9 0.0 collective-permute-done.4.halo_ref
  38.9 1.0 shard_map.62.outer_ref
  40.0 3.3 %collective-permute-start.5 = (bf16[1024,128]{1,0:T(8,128)(2,1)S(1)}, bf16[1024,128]{1,0:T(8,128)(2,1)S(1)}, u32[]{:S(2)}, u32[]{:S(2)}) collective-permute-start(bf16[1024,128]{1,0:T(8,128)(2,1)S(1)} %shard_map.62.outer_ref), channel_id=1, source_target_pairs={{0,240},{16,32},{32,16},{48,64},{64,48},{80,96},{96,80},{112,128},... | collective-permute-start | bytes 786440 | tf_op jit(solution)/shard_map/ppermute | solution.py:370
  43.2 0.0 collective-permute-done.1.halo_ref
  43.3 1.1 shard_map.61.inner_ref
  44.3 0.3 collective-permute-start.3
  44.6 3.2 %shard_map.63 = (bf16[1024,128]{1,0:T(8,128)(2,1)S(1)}, f32[2,1024,128]{2,1,0:T(8,128)S(1)}) custom-call(s32[266]{0:T(512)S(1)} %get-tuple-element.24.near_ref, bf16[24,11,128,128]{3,2,1,0:T(8,128)(2,1)S(1)} %get-tuple-element.26.ham_ref, bf16[1024,128]{1,0:T(8,128)(2,1)S(1)} %shard_map.61.inner_ref, bf16[1024,128]{1,0:T(8,128)(2,1)S(1)} %get-tuple-element.30.mid_ref, ...), custom_call_target="tpu_custom_call" | custom-call | flops 1107296256 | bytes 11534336 | tf_op jit(solution)/shard_map/pallas_call | solution.py:41
  47.8 0.0 collective-permute-done.5.outer_ref
  47.9 0.0 collective-permute-done.3.inner_ref
  47.9 1.4 %shard_map.64 = bf16[3072,128]{1,0:T(8,128)(2,1)S(1)} custom-call(s32[256]{0:T(256)S(1)} %get-tuple-element.23.table_ref, bf16[24,11,128,128]{3,2,1,0:T(8,128)(2,1)S(1)} %get-tuple-element.26.ham_ref, bf16[1024,128]{1,0:T(8,128)(2,1)S(1)} %collective-permute-done.3.inner_ref, bf16[1024,128]{1,0:T(8,128)(2,1)S(1)} %collective-permute-done.5.outer_ref, ...), custom_call_target="tpu_custom_call" | custom-call | flops 276824064 | bytes 11272192 | tf_op jit(solution)/shard_map/pallas_call | solution.py:41
  49.3 16.1 %all_to_all.20.field_ref = bf16[16,192,128]{2,1,0:T(8,128)(2,1)S(1)} all-to-all(bf16[16,192,128]{2,1,0:T(8,128)(2,1)S(1)} %bitcast.8), channel_id=1, replica_groups=mesh['row'=16,'cuts'=16] {'cuts'}, dimensions={0} | all-to-all | bytes 1572864 | tf_op jit(solution)/shard_map/all_to_all | solution.py:492
  65.5 1.1 shard_map.66
  66.5 1.9 %collective-permute-start.6 = (bf16[18,128,128]{2,1,0:T(8,128)(2,1)S(1)}, bf16[18,128,128]{2,1,0:T(8,128)(2,1)S(1)}, u32[]{:S(2)}, u32[]{:S(2)}) collective-permute-start(bf16[18,128,128]{2,1,0:T(8,128)(2,1)S(1)} %shard_map.66), channel_id=1, source_target_pairs={{0,16},{16,0},{32,48},{48,32},{64,80},{80,64},{96,112},{112,96},{1... | collective-permute-start | bytes 1769480 | tf_op jit(solution)/shard_map/ppermute | solution.py:365
  68.5 1.1 shard_map.65
  69.5 0.6 collective-permute-done.6
  70.1 0.1 add_convert_fusion
  70.2 14.7 %all_to_all.21 = bf16[16,144,128]{2,1,0:T(8,128)(2,1)S(1)} all-to-all(bf16[16,144,128]{2,1,0:T(8,128)(2,1)S(1)} %bitcast.13), channel_id=1, replica_groups=mesh['row'=16,'cuts'=16] {'cuts'}, dimensions={0} | all-to-all | bytes 1179648 | tf_op jit(solution)/shard_map/all_to_all | solution.py:514
  84.9 0.1 reduce_sum.12
  85.0 1.5 %collective-permute-start.7 = (bf16[144,128]{1,0:T(8,128)(2,1)S(1)}, bf16[144,128]{1,0:T(8,128)(2,1)S(1)}, u32[]{:S(2)}, u32[]{:S(2)}) collective-permute-start(bf16[144,128]{1,0:T(8,128)(2,1)S(1)} %reduce_sum.12), channel_id=1, source_target_pairs={{0,224},{16,48},{32,0},{48,80},{64,32},{80,112},{96,64},{112,144},... | collective-permute-start | bytes 110600 | tf_op jit(solution)/shard_map/ppermute | solution.py:359
  86.5 0.3 collective-permute-start.8
  86.9 1.3 %collective-permute-done.7 = bf16[144,128]{1,0:T(8,128)(2,1)S(1)} collective-permute-done((bf16[144,128]{1,0:T(8,128)(2,1)S(1)}, bf16[144,128]{1,0:T(8,128)(2,1)S(1)}, u32[]{:S(2)}, u32[]{:S(2)}) %collective-permute-start.7) | collective-permute-done | bytes 36896 | tf_op jit(solution)/shard_map/ppermute | solution.py:359
  88.1 2.5 %collective-permute-done.8 = bf16[144,128]{1,0:T(8,128)(2,1)S(1)} collective-permute-done((bf16[144,128]{1,0:T(8,128)(2,1)S(1)}, bf16[144,128]{1,0:T(8,128)(2,1)S(1)}, u32[]{:S(2)}, u32[]{:S(2)}) %collective-permute-start.8) | collective-permute-done | bytes 36896 | tf_op jit(solution)/shard_map/ppermute | solution.py:359
  90.6 2.2 %collective-permute-start.10 = (bf16[144,128]{1,0:T(8,128)(2,1)S(1)}, bf16[144,128]{1,0:T(8,128)(2,1)S(1)}, u32[]{:S(2)}, u32[]{:S(2)}) collective-permute-start(bf16[144,128]{1,0:T(8,128)(2,1)S(1)} %get-tuple-element.37), channel_id=1, source_target_pairs={{0,96},{16,176},{32,128},{48,208},{64,160},{80,240},{96,192},{112,... | collective-permute-start | bytes 110600 | tf_op jit(solution)/shard_map/ppermute | solution.py:359
  92.8 2.4 %collective-permute-start.9 = (bf16[144,128]{1,0:T(8,128)(2,1)S(1)}, bf16[144,128]{1,0:T(8,128)(2,1)S(1)}, u32[]{:S(2)}, u32[]{:S(2)}) collective-permute-start(bf16[144,128]{1,0:T(8,128)(2,1)S(1)} %get-tuple-element.36), channel_id=1, source_target_pairs={{0,160},{16,112},{32,192},{48,144},{64,224},{80,176},{96,0},{112,2... | collective-permute-start | bytes 110600 | tf_op jit(solution)/shard_map/ppermute | solution.py:359
  95.2 1.3 %collective-permute-done.10 = bf16[144,128]{1,0:T(8,128)(2,1)S(1)} collective-permute-done((bf16[144,128]{1,0:T(8,128)(2,1)S(1)}, bf16[144,128]{1,0:T(8,128)(2,1)S(1)}, u32[]{:S(2)}, u32[]{:S(2)}) %collective-permute-start.10) | collective-permute-done | bytes 36896 | tf_op jit(solution)/shard_map/ppermute | solution.py:359
  96.5 2.1 %collective-permute-done.9 = bf16[144,128]{1,0:T(8,128)(2,1)S(1)} collective-permute-done((bf16[144,128]{1,0:T(8,128)(2,1)S(1)}, bf16[144,128]{1,0:T(8,128)(2,1)S(1)}, u32[]{:S(2)}, u32[]{:S(2)}) %collective-permute-start.9) | collective-permute-done | bytes 36896 | tf_op jit(solution)/shard_map/ppermute | solution.py:359
  98.7 0.1 broadcast_in_dim.2
  98.8 13.3 %all_to_all.22 = bf16[16,144,128]{2,1,0:T(8,128)(2,1)S(1)} all-to-all(bf16[16,144,128]{2,1,0:T(8,128)(2,1)S(1)} %broadcast_in_dim.2), channel_id=1, replica_groups=mesh['row'=16,'cuts'=16] {'cuts'}, dimensions={0} | all-to-all | bytes 1179648 | tf_op jit(solution)/shard_map/all_to_all | solution.py:517
  112.1 7.5 %collective-permute-start.11 = (bf16[18,128,128]{2,1,0:T(8,128)(2,1)S(1)}, bf16[18,128,128]{2,1,0:T(8,128)(2,1)S(1)}, u32[]{:S(2)}, u32[]{:S(2)}) collective-permute-start(bf16[18,128,128]{2,1,0:T(8,128)(2,1)S(1)} %bitcast.9), channel_id=1, source_target_pairs={{0,16},{16,0},{32,48},{48,32},{64,80},{80,64},{96,112},{112,96},{1... | collective-permute-start | bytes 1769480 | tf_op jit(solution)/shard_map/ppermute | solution.py:365
  119.6 1.6 %collective-permute-done.11.other_ref = bf16[18,128,128]{2,1,0:T(8,128)(2,1)S(1)} collective-permute-done((bf16[18,128,128]{2,1,0:T(8,128)(2,1)S(1)}, bf16[18,128,128]{2,1,0:T(8,128)(2,1)S(1)}, u32[]{:S(2)}, u32[]{:S(2)}) %collective-permute-start.11) | collective-permute-done | bytes 589856 | tf_op jit(solution)/shard_map/ppermute | solution.py:365
  121.3 3.0 %shard_map.67 = bf16[192,2048]{1,0:T(8,128)(2,1)} custom-call(s32[127]{0:T(128)S(1)} %get-tuple-element.22.table_ref, bf16[16,192,128]{2,1,0:T(8,128)(2,1)S(1)} %all_to_all.20.field_ref, bf16[18,128,128]{2,1,0:T(8,128)(2,1)S(1)} %bitcast.10, bf16[18,128,128]{2,1,0:T(8,128)(2,1)S(1)} %collective-permute-done.11.other_ref), custom_call_target="tpu_custom_call" | custom-call | flops 536870912 | bytes 2752512 | tf_op jit(solution)/shard_map/pallas_call | solution.py:41
  (2 shorter events, 0.1 us)
Async XLA Ops:
  2.1 7.0 %copy-start = (s32[24,11]{0,1:T(8,128)S(1)}, s32[24,11]{0,1:T(8,128)}, u32[]{:S(2)}) copy-start(s32[24,11]{0,1:T(8,128)} %param.6) | copy-start | bytes 3172
  2.1 7.0 %copy-start.1 = (s32[12]{0:T(128)S(1)}, s32[12]{0:T(128)}, u32[]{:S(2)}) copy-start(s32[12]{0:T(128)} %width_ref.1) | copy-start | bytes 148
  2.1 7.0 %copy-start.2 = (s32[12]{0:T(128)S(1)}, s32[12]{0:T(128)}, u32[]{:S(2)}) copy-start(s32[12]{0:T(128)} %interval_ref.1) | copy-start | bytes 148
  2.1 19.7 %all-to-all-start = ((bf16[16,192,128]{2,1,0:T(8,128)(2,1)}), bf16[16,192,128]{2,1,0:T(8,128)(2,1)S(1)}, u32[]{:S(2)}, u32[]{:S(2)}) async-start(bf16[16,192,128]{2,1,0:T(8,128)(2,1)} %shard_map.55), calls=%async_computation | async-start | bytes 1572864 | tf_op jit(solution)/shard_map/all_to_all | solution.py:402
  21.8 9.3 %collective-permute-start.2 = (bf16[1024,128]{1,0:T(8,128)(2,1)S(1)}, bf16[1024,128]{1,0:T(8,128)(2,1)S(1)}, u32[]{:S(2)}, u32[]{:S(2)}) collective-permute-start(bf16[1024,128]{1,0:T(8,128)(2,1)S(1)} %get-tuple-element.33.outer_ref.rest_2_), channel_id=1, source_target_pairs={{0,240},{16,32},{32,16},{48,64},{64,48},{80,96},{96,80},{112,128},... | collective-permute-start | bytes 786440 | tf_op jit(solution)/shard_map/ppermute | solution.py:370
  26.0 8.4 %collective-permute-start = (bf16[1024,128]{1,0:T(8,128)(2,1)S(1)}, bf16[1024,128]{1,0:T(8,128)(2,1)S(1)}, u32[]{:S(2)}, u32[]{:S(2)}) collective-permute-start(bf16[1024,128]{1,0:T(8,128)(2,1)S(1)} %get-tuple-element.35.inner_ref.rest_0_), channel_id=1, source_target_pairs={{0,16},{16,0},{32,48},{48,32},{64,80},{80,64},{96,112},{112,96},{1... | collective-permute-start | bytes 786440 | tf_op jit(solution)/shard_map/ppermute | solution.py:365
  32.3 6.6 %collective-permute-start.4 = (bf16[1024,128]{1,0:T(8,128)(2,1)S(1)}, bf16[1024,128]{1,0:T(8,128)(2,1)S(1)}, u32[]{:S(2)}, u32[]{:S(2)}) collective-permute-start(bf16[1024,128]{1,0:T(8,128)(2,1)S(1)} %shard_map.59.outer_ref.rest_2_), channel_id=1, source_target_pairs={{0,240},{16,32},{32,16},{48,64},{64,48},{80,96},{96,80},{112,128},... | collective-permute-start | bytes 786440 | tf_op jit(solution)/shard_map/ppermute | solution.py:370
  35.5 7.7 %collective-permute-start.1 = (bf16[1024,128]{1,0:T(8,128)(2,1)S(1)}, bf16[1024,128]{1,0:T(8,128)(2,1)S(1)}, u32[]{:S(2)}, u32[]{:S(2)}) collective-permute-start(bf16[1024,128]{1,0:T(8,128)(2,1)S(1)} %shard_map.58.inner_ref.rest_0_), channel_id=1, source_target_pairs={{0,16},{16,0},{32,48},{48,32},{64,80},{80,64},{96,112},{112,96},{1... | collective-permute-start | bytes 786440 | tf_op jit(solution)/shard_map/ppermute | solution.py:365
  40.0 7.9 %collective-permute-start.5 = (bf16[1024,128]{1,0:T(8,128)(2,1)S(1)}, bf16[1024,128]{1,0:T(8,128)(2,1)S(1)}, u32[]{:S(2)}, u32[]{:S(2)}) collective-permute-start(bf16[1024,128]{1,0:T(8,128)(2,1)S(1)} %shard_map.62.outer_ref), channel_id=1, source_target_pairs={{0,240},{16,32},{32,16},{48,64},{64,48},{80,96},{96,80},{112,128},... | collective-permute-start | bytes 786440 | tf_op jit(solution)/shard_map/ppermute | solution.py:370
  44.3 3.5 %collective-permute-start.3 = (bf16[1024,128]{1,0:T(8,128)(2,1)S(1)}, bf16[1024,128]{1,0:T(8,128)(2,1)S(1)}, u32[]{:S(2)}, u32[]{:S(2)}) collective-permute-start(bf16[1024,128]{1,0:T(8,128)(2,1)S(1)} %shard_map.61.inner_ref), channel_id=1, source_target_pairs={{0,16},{16,0},{32,48},{48,32},{64,80},{80,64},{96,112},{112,96},{1... | collective-permute-start | bytes 786440 | tf_op jit(solution)/shard_map/ppermute | solution.py:365
  66.5 3.5 %collective-permute-start.6 = (bf16[18,128,128]{2,1,0:T(8,128)(2,1)S(1)}, bf16[18,128,128]{2,1,0:T(8,128)(2,1)S(1)}, u32[]{:S(2)}, u32[]{:S(2)}) collective-permute-start(bf16[18,128,128]{2,1,0:T(8,128)(2,1)S(1)} %shard_map.66), channel_id=1, source_target_pairs={{0,16},{16,0},{32,48},{48,32},{64,80},{80,64},{96,112},{112,96},{1... | collective-permute-start | bytes 1769480 | tf_op jit(solution)/shard_map/ppermute | solution.py:365
  85.0 3.1 %collective-permute-start.7 = (bf16[144,128]{1,0:T(8,128)(2,1)S(1)}, bf16[144,128]{1,0:T(8,128)(2,1)S(1)}, u32[]{:S(2)}, u32[]{:S(2)}) collective-permute-start(bf16[144,128]{1,0:T(8,128)(2,1)S(1)} %reduce_sum.12), channel_id=1, source_target_pairs={{0,224},{16,48},{32,0},{48,80},{64,32},{80,112},{96,64},{112,144},... | collective-permute-start | bytes 110600 | tf_op jit(solution)/shard_map/ppermute | solution.py:359
  86.5 4.1 %collective-permute-start.8 = (bf16[144,128]{1,0:T(8,128)(2,1)S(1)}, bf16[144,128]{1,0:T(8,128)(2,1)S(1)}, u32[]{:S(2)}, u32[]{:S(2)}) collective-permute-start(bf16[144,128]{1,0:T(8,128)(2,1)S(1)} %reduce_sum.12), channel_id=1, source_target_pairs={{0,32},{16,240},{32,64},{48,16},{64,96},{80,48},{96,128},{112,80},... | collective-permute-start | bytes 110600 | tf_op jit(solution)/shard_map/ppermute | solution.py:359
  90.6 5.9 %collective-permute-start.10 = (bf16[144,128]{1,0:T(8,128)(2,1)S(1)}, bf16[144,128]{1,0:T(8,128)(2,1)S(1)}, u32[]{:S(2)}, u32[]{:S(2)}) collective-permute-start(bf16[144,128]{1,0:T(8,128)(2,1)S(1)} %get-tuple-element.37), channel_id=1, source_target_pairs={{0,96},{16,176},{32,128},{48,208},{64,160},{80,240},{96,192},{112,... | collective-permute-start | bytes 110600 | tf_op jit(solution)/shard_map/ppermute | solution.py:359
  92.8 5.8 %collective-permute-start.9 = (bf16[144,128]{1,0:T(8,128)(2,1)S(1)}, bf16[144,128]{1,0:T(8,128)(2,1)S(1)}, u32[]{:S(2)}, u32[]{:S(2)}) collective-permute-start(bf16[144,128]{1,0:T(8,128)(2,1)S(1)} %get-tuple-element.36), channel_id=1, source_target_pairs={{0,160},{16,112},{32,192},{48,144},{64,224},{80,176},{96,0},{112,2... | collective-permute-start | bytes 110600 | tf_op jit(solution)/shard_map/ppermute | solution.py:359
  112.1 9.2 %collective-permute-start.11 = (bf16[18,128,128]{2,1,0:T(8,128)(2,1)S(1)}, bf16[18,128,128]{2,1,0:T(8,128)(2,1)S(1)}, u32[]{:S(2)}, u32[]{:S(2)}) collective-permute-start(bf16[18,128,128]{2,1,0:T(8,128)(2,1)S(1)} %bitcast.9), channel_id=1, source_target_pairs={{0,16},{16,0},{32,48},{48,32},{64,80},{80,64},{96,112},{112,96},{1... | collective-permute-start | bytes 1769480 | tf_op jit(solution)/shard_map/ppermute | solution.py:365

commit v8 on v7

--- a/solution.py
+++ b/solution.py
@@ -138,7 +138,10 @@
         store(t).wait()
 
 
-def near_kernel(scale, near_ref, ham_ref, inner_ref, mid_ref, outer_ref, *rest):
+def near_kernel(scale, table_ref, ham_ref, inner_ref, mid_ref, outer_ref, *rest):
+    *rest, near_ref, fetched = rest
+    fetch = pltpu.make_async_copy(table_ref, near_ref, fetched.at[0])
+    fetch.start()
     first = scale == 1
     blocks, slots = ham_ref.shape[:2]
     if first:
@@ -157,7 +160,7 @@
         ham = ham_ref
     third = blocks // 3
     span = third * BS
-    core = near_ref[slots * blocks]
+    core = own_core()
     inner_at, outer_at = (1 - core) * 2 * span, core * 2 * span
 
     def spread(inner, mid, outer, into):
@@ -169,6 +172,7 @@
     stack[blocks * BS :] = jnp.zeros((BS, TILE), BF16)
     if not first:
         spread(*rest[:3], before)
+    fetch.wait()
     centre = -0.5 + near_ref[slots * blocks + 1].astype(F32) * F32(1 / (NINT - 1))
 
     def tile_at(n, b):
@@ -408,7 +412,7 @@
     near, far, pair = pl.pallas_call(
         table_kernel,
         out_shape=(
-            shape((slots * blocks + 2,), jnp.int32),
+            shape((slots * blocks + 248,), jnp.int32),
             shape((2 * blocks // 3 * HB + 128,), jnp.int32),
             shape((tiles * REACH + LISTED,), jnp.int32),
         ),
@@ -432,9 +436,9 @@
         mid, edges, ham = pl.pallas_call(
             functools.partial(near_kernel, 1),
             out_shape=(*outs, shape(ham_blocks.shape)),
-            in_specs=smem(1) + [pl.BlockSpec(memory_space=pltpu.HBM)] + vmem(3),
+            in_specs=anywhere(1) + [pl.BlockSpec(memory_space=pltpu.HBM)] + vmem(3),
             out_specs=tuple(vmem(3)),
-            scratch_shapes=[stacks[1], pltpu.SemaphoreType.DMA((FLIGHT,))],
+            scratch_shapes=[stacks[1], pltpu.SemaphoreType.DMA((FLIGHT,)), SMEM(near.shape, jnp.int32), pltpu.SemaphoreType.DMA((1,))],
             compiler_params=pltpu.CompilerParams(vmem_limit_bytes=40 << 20),
             cost_estimate=pl.CostEstimate(
                 flops=work, bytes_accessed=ham_blocks.size * 2, transcendentals=0
@@ -453,6 +457,7 @@
             [ham, inner, mid, outer, *before],
             stacks,
             work,
+            fetch=True,
         )
         return from_inner, from_outer, edges, mid
 

time: 125 us -> 124 us (level)
  transfers between devices with their start and end apart: 13 -> 13, of which waited for: 7 -> 7; matrix products, arithmetic and copies ran while one was open for 0% -> 0% of each run, Pallas kernels for 17% -> 16%
where the time goes in v8:
time: 124 us
  blocking collectives  43.9 us (35%)
  starting transfers between devices  33.4 us (27%)
  Pallas kernels  27.7 us (22%)
  waiting for transfers between devices  18.1 us (15%)
    all_to_all x1, blocking collectives, body(): lax.all_to_all(filtered.reshape(tiles, rows_mine, TILE), 'cuts', 0, 0)  16.1 us
    pallas_call x8, Pallas kernels, call(): pl.pallas_call(kernel, out_shape=tuple(outs), in_specs=(anywhere(1) if fe...  14.9 us
    all_to_all x1, blocking collectives, body(): lax.all_to_all(partial.reshape(cut_count, share, TILE), 'cuts', 0, 0)  14.7 us
    all_to_all x1, blocking collectives, body(): mine = lax.all_to_all(spread, 'cuts', 0, 0).reshape(HALF, TILE, TILE)  13.1 us
    ppermute x5, starting transfers between devices, exchange(): lax.ppermute(array, 'row', [(i, i ^ 1) for i in range(lax.axis_size('row'...  9.76 us
    ppermute x3, starting transfers between devices, swap_outer(): lax.ppermute(array, 'row', [(i, (i - 1 + 2 * (i % 2)) % size) for i in ra...  9.74 us
    all_to_all x1, waiting for transfers between devices, body(): panel = lax.all_to_all(turned, 'cuts', 0, 0).reshape(panel_rows, TILE)  8.68 us
    ppermute x4, waiting for transfers between devices, shift(): lax.ppermute(array, 'row', [(i, (i + 2 * chips * (1 - 2 * (i % 2))) % siz...  7.2 us
  transfers between devices with their start and end apart: 13, of which 7 were waited for; matrix products, arithmetic and copies ran while one was open for 0% of the time, Pallas kernels for 16%

profile of v8, /device:TPU:33, one launch (start us, length us, event | category | flops | bytes accessed | tf_op | source)
XLA Modules:
  0.0 124.0 jit_solution(80406653610469598)
XLA Ops:
  0.0 2.0 %shard_map.55 = bf16[16,192,128]{2,1,0:T(8,128)(2,1)} custom-call(bf16[192,2048]{1,0:T(8,128)(2,1)} %start_ref.1), custom_call_target="tpu_custom_call" | custom-call | tf_op jit(solution)/shard_map/pallas_call | solution.py:394
  2.1 0.0 copy-start
  2.1 0.0 copy-start.1
  2.1 0.0 copy-start.2
  2.1 6.9 %all-to-all-start = ((bf16[16,192,128]{2,1,0:T(8,128)(2,1)}), bf16[16,192,128]{2,1,0:T(8,128)(2,1)S(1)}, u32[]{:S(2)}, u32[]{:S(2)}) async-start(bf16[16,192,128]{2,1,0:T(8,128)(2,1)} %shard_map.55), calls=%async_computation | async-start | bytes 1572864 | tf_op jit(solution)/shard_map/all_to_all | solution.py:406
  9.0 0.1 pad_add_fusion.where_ref
  9.1 0.0 copy-done
  9.1 0.0 copy-done.1
  9.1 0.0 copy-done.2
  9.1 4.0 %shard_map.56 = (s32[512]{0:T(512)S(1)}, s32[256]{0:T(256)S(1)}, s32[127]{0:T(128)S(1)}) custom-call(s32[4]{0:T(128)S(1)} %pad_add_fusion.where_ref, s32[11,24]{1,0:T(8,128)S(1)} %bitcast.11, s32[12]{0:T(128)S(1)} %copy-done.1, s32[12]{0:T(128)S(1)} %copy-done.2), custom_call_target="tpu_custom_call" | custom-call | flops 1048576 | bytes 4096 | tf_op jit(solution)/shard_map/pallas_call | solution.py:412
  13.1 8.7 %all-to-all-done = bf16[16,192,128]{2,1,0:T(8,128)(2,1)S(1)} async-done(((bf16[16,192,128]{2,1,0:T(8,128)(2,1)}), bf16[16,192,128]{2,1,0:T(8,128)(2,1)S(1)}, u32[]{:S(2)}, u32[]{:S(2)}) %all-to-all-start) | async-done | bytes 786464 | tf_op jit(solution)/shard_map/all_to_all | solution.py:406
  21.8 0.1 broadcast_select_fusion
  21.8 4.2 %collective-permute-start.2 = (bf16[1024,128]{1,0:T(8,128)(2,1)S(1)}, bf16[1024,128]{1,0:T(8,128)(2,1)S(1)}, u32[]{:S(2)}, u32[]{:S(2)}) collective-permute-start(bf16[1024,128]{1,0:T(8,128)(2,1)S(1)} %get-tuple-element.33.outer_ref.rest_2_), channel_id=1, source_target_pairs={{0,240},{16,32},{32,16},{48,64},{64,48},{80,96},{96,80},{112,128},... | collective-permute-start | bytes 786440 | tf_op jit(solution)/shard_map/ppermute | solution.py:374
  26.0 0.0 collective-permute-start
  26.0 4.6 %shard_map.57 = (bf16[1024,128]{1,0:T(8,128)(2,1)S(1)}, f32[2,1024,128]{2,1,0:T(8,128)S(1)}, bf16[24,11,128,128]{3,2,1,0:T(8,128)(2,1)S(1)}) custom-call(s32[512]{0:T(512)S(1)} %get-tuple-element.24.table_ref, bf16[24,11,128,128]{3,2,1,0:T(8,128)(2,1)} %ham_ref.1, bf16[1024,128]{1,0:T(8,128)(2,1)S(1)} %get-tuple-element.35.inner_ref.rest_0_, ...), custom_call_target="tpu_custom_call" | custom-call | flops 1107296256 | bytes 8650752 | tf_op jit(solution)/shard_map/pallas_call | solution.py:436
  30.6 0.0 collective-permute-done.2.halo_ref
  30.6 1.1 shard_map.59.outer_ref.rest_2_
  31.8 2.1 %collective-permute-start.4 = (bf16[1024,128]{1,0:T(8,128)(2,1)S(1)}, bf16[1024,128]{1,0:T(8,128)(2,1)S(1)}, u32[]{:S(2)}, u32[]{:S(2)}) collective-permute-start(bf16[1024,128]{1,0:T(8,128)(2,1)S(1)} %shard_map.59.outer_ref.rest_2_), channel_id=1, source_target_pairs={{0,240},{16,32},{32,16},{48,64},{64,48},{80,96},{96,80},{112,128},... | collective-permute-start | bytes 786440 | tf_op jit(solution)/shard_map/ppermute | solution.py:374
  33.9 0.0 collective-permute-done.halo_ref
  33.9 1.1 shard_map.58.inner_ref.rest_0_
  35.0 0.1 collective-permute-start.1
  35.1 3.1 %shard_map.60 = (bf16[1024,128]{1,0:T(8,128)(2,1)S(1)}, f32[2,1024,128]{2,1,0:T(8,128)S(1)}) custom-call(s32[512]{0:T(512)S(1)} %get-tuple-element.24.table_ref, bf16[24,11,128,128]{3,2,1,0:T(8,128)(2,1)S(1)} %get-tuple-element.26.ham_ref, bf16[1024,128]{1,0:T(8,128)(2,1)S(1)} %shard_map.58.inner_ref.rest_0_, ...), custom_call_target="tpu_custom_call" | custom-call | flops 1107296256 | bytes 11534336 | tf_op jit(solution)/shard_map/pallas_call | solution.py:41
  38.2 0.0 collective-permute-done.4.halo_ref
  38.2 1.0 shard_map.62.outer_ref
  39.3 3.4 %collective-permute-start.5 = (bf16[1024,128]{1,0:T(8,128)(2,1)S(1)}, bf16[1024,128]{1,0:T(8,128)(2,1)S(1)}, u32[]{:S(2)}, u32[]{:S(2)}) collective-permute-start(bf16[1024,128]{1,0:T(8,128)(2,1)S(1)} %shard_map.62.outer_ref), channel_id=1, source_target_pairs={{0,240},{16,32},{32,16},{48,64},{64,48},{80,96},{96,80},{112,128},... | collective-permute-start | bytes 786440 | tf_op jit(solution)/shard_map/ppermute | solution.py:374
  42.7 0.0 collective-permute-done.1.halo_ref
  42.7 1.1 shard_map.61.inner_ref
  43.8 0.1 collective-permute-start.3
  43.9 3.1 %shard_map.63 = (bf16[1024,128]{1,0:T(8,128)(2,1)S(1)}, f32[2,1024,128]{2,1,0:T(8,128)S(1)}) custom-call(s32[512]{0:T(512)S(1)} %get-tuple-element.24.table_ref, bf16[24,11,128,128]{3,2,1,0:T(8,128)(2,1)S(1)} %get-tuple-element.26.ham_ref, bf16[1024,128]{1,0:T(8,128)(2,1)S(1)} %shard_map.61.inner_ref, bf16[1024,128]{1,0:T(8,128)(2,1)S(1)} %get-tuple-element.30.mid_ref, ...), custom_call_target="tpu_custom_call" | custom-call | flops 1107296256 | bytes 11534336 | tf_op jit(solution)/shard_map/pallas_call | solution.py:41
  47.0 0.0 collective-permute-done.5.outer_ref
  47.0 0.0 collective-permute-done.3.inner_ref
  47.0 1.4 %shard_map.64 = bf16[3072,128]{1,0:T(8,128)(2,1)S(1)} custom-call(s32[256]{0:T(256)S(1)} %get-tuple-element.23.table_ref, bf16[24,11,128,128]{3,2,1,0:T(8,128)(2,1)S(1)} %get-tuple-element.26.ham_ref, bf16[1024,128]{1,0:T(8,128)(2,1)S(1)} %collective-permute-done.3.inner_ref, bf16[1024,128]{1,0:T(8,128)(2,1)S(1)} %collective-permute-done.5.outer_ref, ...), custom_call_target="tpu_custom_call" | custom-call | flops 276824064 | bytes 11272192 | tf_op jit(solution)/shard_map/pallas_call | solution.py:41
  48.5 16.1 %all_to_all.20.field_ref = bf16[16,192,128]{2,1,0:T(8,128)(2,1)S(1)} all-to-all(bf16[16,192,128]{2,1,0:T(8,128)(2,1)S(1)} %bitcast.8), channel_id=1, replica_groups=mesh['row'=16,'cuts'=16] {'cuts'}, dimensions={0} | all-to-all | bytes 1572864 | tf_op jit(solution)/shard_map/all_to_all | solution.py:497
  64.6 1.1 shard_map.66
  65.7 1.9 %collective-permute-start.6 = (bf16[18,128,128]{2,1,0:T(8,128)(2,1)S(1)}, bf16[18,128,128]{2,1,0:T(8,128)(2,1)S(1)}, u32[]{:S(2)}, u32[]{:S(2)}) collective-permute-start(bf16[18,128,128]{2,1,0:T(8,128)(2,1)S(1)} %shard_map.66), channel_id=1, source_target_pairs={{0,16},{16,0},{32,48},{48,32},{64,80},{80,64},{96,112},{112,96},{1... | collective-permute-start | bytes 1769480 | tf_op jit(solution)/shard_map/ppermute | solution.py:369
  67.6 1.1 shard_map.65
  68.7 0.6 collective-permute-done.6
  69.3 0.1 add_convert_fusion
  69.4 14.7 %all_to_all.21 = bf16[16,144,128]{2,1,0:T(8,128)(2,1)S(1)} all-to-all(bf16[16,144,128]{2,1,0:T(8,128)(2,1)S(1)} %bitcast.13), channel_id=1, replica_groups=mesh['row'=16,'cuts'=16] {'cuts'}, dimensions={0} | all-to-all | bytes 1179648 | tf_op jit(solution)/shard_map/all_to_all | solution.py:519
  84.1 0.1 reduce_sum.12
  84.2 2.1 %collective-permute-start.7 = (bf16[144,128]{1,0:T(8,128)(2,1)S(1)}, bf16[144,128]{1,0:T(8,128)(2,1)S(1)}, u32[]{:S(2)}, u32[]{:S(2)}) collective-permute-start(bf16[144,128]{1,0:T(8,128)(2,1)S(1)} %reduce_sum.12), channel_id=1, source_target_pairs={{0,224},{16,48},{32,0},{48,80},{64,32},{80,112},{96,64},{112,144},... | collective-permute-start | bytes 110600 | tf_op jit(solution)/shard_map/ppermute | solution.py:363
  86.2 0.4 collective-permute-start.8
  86.7 1.3 %collective-permute-done.7 = bf16[144,128]{1,0:T(8,128)(2,1)S(1)} collective-permute-done((bf16[144,128]{1,0:T(8,128)(2,1)S(1)}, bf16[144,128]{1,0:T(8,128)(2,1)S(1)}, u32[]{:S(2)}, u32[]{:S(2)}) %collective-permute-start.7) | collective-permute-done | bytes 36896 | tf_op jit(solution)/shard_map/ppermute | solution.py:363
  87.9 2.3 %collective-permute-done.8 = bf16[144,128]{1,0:T(8,128)(2,1)S(1)} collective-permute-done((bf16[144,128]{1,0:T(8,128)(2,1)S(1)}, bf16[144,128]{1,0:T(8,128)(2,1)S(1)}, u32[]{:S(2)}, u32[]{:S(2)}) %collective-permute-start.8) | collective-permute-done | bytes 36896 | tf_op jit(solution)/shard_map/ppermute | solution.py:363
  90.2 1.9 %collective-permute-start.10 = (bf16[144,128]{1,0:T(8,128)(2,1)S(1)}, bf16[144,128]{1,0:T(8,128)(2,1)S(1)}, u32[]{:S(2)}, u32[]{:S(2)}) collective-permute-start(bf16[144,128]{1,0:T(8,128)(2,1)S(1)} %get-tuple-element.37), channel_id=1, source_target_pairs={{0,96},{16,176},{32,128},{48,208},{64,160},{80,240},{96,192},{112,... | collective-permute-start | bytes 110600 | tf_op jit(solution)/shard_map/ppermute | solution.py:363
  92.2 2.6 %collective-permute-start.9 = (bf16[144,128]{1,0:T(8,128)(2,1)S(1)}, bf16[144,128]{1,0:T(8,128)(2,1)S(1)}, u32[]{:S(2)}, u32[]{:S(2)}) collective-permute-start(bf16[144,128]{1,0:T(8,128)(2,1)S(1)} %get-tuple-element.36), channel_id=1, source_target_pairs={{0,160},{16,112},{32,192},{48,144},{64,224},{80,176},{96,0},{112,2... | collective-permute-start | bytes 110600 | tf_op jit(solution)/shard_map/ppermute | solution.py:363
  94.8 1.3 %collective-permute-done.10 = bf16[144,128]{1,0:T(8,128)(2,1)S(1)} collective-permute-done((bf16[144,128]{1,0:T(8,128)(2,1)S(1)}, bf16[144,128]{1,0:T(8,128)(2,1)S(1)}, u32[]{:S(2)}, u32[]{:S(2)}) %collective-permute-start.10) | collective-permute-done | bytes 36896 | tf_op jit(solution)/shard_map/ppermute | solution.py:363
  96.1 2.3 %collective-permute-done.9 = bf16[144,128]{1,0:T(8,128)(2,1)S(1)} collective-permute-done((bf16[144,128]{1,0:T(8,128)(2,1)S(1)}, bf16[144,128]{1,0:T(8,128)(2,1)S(1)}, u32[]{:S(2)}, u32[]{:S(2)}) %collective-permute-start.9) | collective-permute-done | bytes 36896 | tf_op jit(solution)/shard_map/ppermute | solution.py:363
  98.5 0.1 broadcast_in_dim.2
  98.6 13.1 %all_to_all.22 = bf16[16,144,128]{2,1,0:T(8,128)(2,1)S(1)} all-to-all(bf16[16,144,128]{2,1,0:T(8,128)(2,1)S(1)} %broadcast_in_dim.2), channel_id=1, replica_groups=mesh['row'=16,'cuts'=16] {'cuts'}, dimensions={0} | all-to-all | bytes 1179648 | tf_op jit(solution)/shard_map/all_to_all | solution.py:522
  111.7 7.6 %collective-permute-start.11 = (bf16[18,128,128]{2,1,0:T(8,128)(2,1)S(1)}, bf16[18,128,128]{2,1,0:T(8,128)(2,1)S(1)}, u32[]{:S(2)}, u32[]{:S(2)}) collective-permute-start(bf16[18,128,128]{2,1,0:T(8,128)(2,1)S(1)} %bitcast.9), channel_id=1, source_target_pairs={{0,16},{16,0},{32,48},{48,32},{64,80},{80,64},{96,112},{112,96},{1... | collective-permute-start | bytes 1769480 | tf_op jit(solution)/shard_map/ppermute | solution.py:369
  119.3 1.6 %collective-permute-done.11.other_ref = bf16[18,128,128]{2,1,0:T(8,128)(2,1)S(1)} collective-permute-done((bf16[18,128,128]{2,1,0:T(8,128)(2,1)S(1)}, bf16[18,128,128]{2,1,0:T(8,128)(2,1)S(1)}, u32[]{:S(2)}, u32[]{:S(2)}) %collective-permute-start.11) | collective-permute-done | bytes 589856 | tf_op jit(solution)/shard_map/ppermute | solution.py:369
  120.9 3.0 %shard_map.67 = bf16[192,2048]{1,0:T(8,128)(2,1)} custom-call(s32[127]{0:T(128)S(1)} %get-tuple-element.22.table_ref, bf16[16,192,128]{2,1,0:T(8,128)(2,1)S(1)} %all_to_all.20.field_ref, bf16[18,128,128]{2,1,0:T(8,128)(2,1)S(1)} %bitcast.10, bf16[18,128,128]{2,1,0:T(8,128)(2,1)S(1)} %collective-permute-done.11.other_ref), custom_call_target="tpu_custom_call" | custom-call | flops 536870912 | bytes 2752512 | tf_op jit(solution)/shard_map/pallas_call | solution.py:41
  (2 shorter events, 0.1 us)
Async XLA Ops:
  2.1 7.0 %copy-start = (s32[24,11]{0,1:T(8,128)S(1)}, s32[24,11]{0,1:T(8,128)}, u32[]{:S(2)}) copy-start(s32[24,11]{0,1:T(8,128)} %param.6) | copy-start | bytes 3172
  2.1 7.0 %copy-start.1 = (s32[12]{0:T(128)S(1)}, s32[12]{0:T(128)}, u32[]{:S(2)}) copy-start(s32[12]{0:T(128)} %width_ref.1) | copy-start | bytes 148
  2.1 7.0 %copy-start.2 = (s32[12]{0:T(128)S(1)}, s32[12]{0:T(128)}, u32[]{:S(2)}) copy-start(s32[12]{0:T(128)} %interval_ref.1) | copy-start | bytes 148
  2.1 19.7 %all-to-all-start = ((bf16[16,192,128]{2,1,0:T(8,128)(2,1)}), bf16[16,192,128]{2,1,0:T(8,128)(2,1)S(1)}, u32[]{:S(2)}, u32[]{:S(2)}) async-start(bf16[16,192,128]{2,1,0:T(8,128)(2,1)} %shard_map.55), calls=%async_computation | async-start | bytes 1572864 | tf_op jit(solution)/shard_map/all_to_all | solution.py:406
  21.8 8.8 %collective-permute-start.2 = (bf16[1024,128]{1,0:T(8,128)(2,1)S(1)}, bf16[1024,128]{1,0:T(8,128)(2,1)S(1)}, u32[]{:S(2)}, u32[]{:S(2)}) collective-permute-start(bf16[1024,128]{1,0:T(8,128)(2,1)S(1)} %get-tuple-element.33.outer_ref.rest_2_), channel_id=1, source_target_pairs={{0,240},{16,32},{32,16},{48,64},{64,48},{80,96},{96,80},{112,128},... | collective-permute-start | bytes 786440 | tf_op jit(solution)/shard_map/ppermute | solution.py:374
  26.0 7.8 %collective-permute-start = (bf16[1024,128]{1,0:T(8,128)(2,1)S(1)}, bf16[1024,128]{1,0:T(8,128)(2,1)S(1)}, u32[]{:S(2)}, u32[]{:S(2)}) collective-permute-start(bf16[1024,128]{1,0:T(8,128)(2,1)S(1)} %get-tuple-element.35.inner_ref.rest_0_), channel_id=1, source_target_pairs={{0,16},{16,0},{32,48},{48,32},{64,80},{80,64},{96,112},{112,96},{1... | collective-permute-start | bytes 786440 | tf_op jit(solution)/shard_map/ppermute | solution.py:369
  31.8 6.5 %collective-permute-start.4 = (bf16[1024,128]{1,0:T(8,128)(2,1)S(1)}, bf16[1024,128]{1,0:T(8,128)(2,1)S(1)}, u32[]{:S(2)}, u32[]{:S(2)}) collective-permute-start(bf16[1024,128]{1,0:T(8,128)(2,1)S(1)} %shard_map.59.outer_ref.rest_2_), channel_id=1, source_target_pairs={{0,240},{16,32},{32,16},{48,64},{64,48},{80,96},{96,80},{112,128},... | collective-permute-start | bytes 786440 | tf_op jit(solution)/shard_map/ppermute | solution.py:374
  35.0 7.7 %collective-permute-start.1 = (bf16[1024,128]{1,0:T(8,128)(2,1)S(1)}, bf16[1024,128]{1,0:T(8,128)(2,1)S(1)}, u32[]{:S(2)}, u32[]{:S(2)}) collective-permute-start(bf16[1024,128]{1,0:T(8,128)(2,1)S(1)} %shard_map.58.inner_ref.rest_0_), channel_id=1, source_target_pairs={{0,16},{16,0},{32,48},{48,32},{64,80},{80,64},{96,112},{112,96},{1... | collective-permute-start | bytes 786440 | tf_op jit(solution)/shard_map/ppermute | solution.py:369
  39.3 7.7 %collective-permute-start.5 = (bf16[1024,128]{1,0:T(8,128)(2,1)S(1)}, bf16[1024,128]{1,0:T(8,128)(2,1)S(1)}, u32[]{:S(2)}, u32[]{:S(2)}) collective-permute-start(bf16[1024,128]{1,0:T(8,128)(2,1)S(1)} %shard_map.62.outer_ref), channel_id=1, source_target_pairs={{0,240},{16,32},{32,16},{48,64},{64,48},{80,96},{96,80},{112,128},... | collective-permute-start | bytes 786440 | tf_op jit(solution)/shard_map/ppermute | solution.py:374
  43.8 3.2 %collective-permute-start.3 = (bf16[1024,128]{1,0:T(8,128)(2,1)S(1)}, bf16[1024,128]{1,0:T(8,128)(2,1)S(1)}, u32[]{:S(2)}, u32[]{:S(2)}) collective-permute-start(bf16[1024,128]{1,0:T(8,128)(2,1)S(1)} %shard_map.61.inner_ref), channel_id=1, source_target_pairs={{0,16},{16,0},{32,48},{48,32},{64,80},{80,64},{96,112},{112,96},{1... | collective-permute-start | bytes 786440 | tf_op jit(solution)/shard_map/ppermute | solution.py:369
  65.7 3.6 %collective-permute-start.6 = (bf16[18,128,128]{2,1,0:T(8,128)(2,1)S(1)}, bf16[18,128,128]{2,1,0:T(8,128)(2,1)S(1)}, u32[]{:S(2)}, u32[]{:S(2)}) collective-permute-start(bf16[18,128,128]{2,1,0:T(8,128)(2,1)S(1)} %shard_map.66), channel_id=1, source_target_pairs={{0,16},{16,0},{32,48},{48,32},{64,80},{80,64},{96,112},{112,96},{1... | collective-permute-start | bytes 1769480 | tf_op jit(solution)/shard_map/ppermute | solution.py:369
  84.2 3.8 %collective-permute-start.7 = (bf16[144,128]{1,0:T(8,128)(2,1)S(1)}, bf16[144,128]{1,0:T(8,128)(2,1)S(1)}, u32[]{:S(2)}, u32[]{:S(2)}) collective-permute-start(bf16[144,128]{1,0:T(8,128)(2,1)S(1)} %reduce_sum.12), channel_id=1, source_target_pairs={{0,224},{16,48},{32,0},{48,80},{64,32},{80,112},{96,64},{112,144},... | collective-permute-start | bytes 110600 | tf_op jit(solution)/shard_map/ppermute | solution.py:363
  86.2 4.0 %collective-permute-start.8 = (bf16[144,128]{1,0:T(8,128)(2,1)S(1)}, bf16[144,128]{1,0:T(8,128)(2,1)S(1)}, u32[]{:S(2)}, u32[]{:S(2)}) collective-permute-start(bf16[144,128]{1,0:T(8,128)(2,1)S(1)} %reduce_sum.12), channel_id=1, source_target_pairs={{0,32},{16,240},{32,64},{48,16},{64,96},{80,48},{96,128},{112,80},... | collective-permute-start | bytes 110600 | tf_op jit(solution)/shard_map/ppermute | solution.py:363
  90.2 5.9 %collective-permute-start.10 = (bf16[144,128]{1,0:T(8,128)(2,1)S(1)}, bf16[144,128]{1,0:T(8,128)(2,1)S(1)}, u32[]{:S(2)}, u32[]{:S(2)}) collective-permute-start(bf16[144,128]{1,0:T(8,128)(2,1)S(1)} %get-tuple-element.37), channel_id=1, source_target_pairs={{0,96},{16,176},{32,128},{48,208},{64,160},{80,240},{96,192},{112,... | collective-permute-start | bytes 110600 | tf_op jit(solution)/shard_map/ppermute | solution.py:363
  92.2 6.3 %collective-permute-start.9 = (bf16[144,128]{1,0:T(8,128)(2,1)S(1)}, bf16[144,128]{1,0:T(8,128)(2,1)S(1)}, u32[]{:S(2)}, u32[]{:S(2)}) collective-permute-start(bf16[144,128]{1,0:T(8,128)(2,1)S(1)} %get-tuple-element.36), channel_id=1, source_target_pairs={{0,160},{16,112},{32,192},{48,144},{64,224},{80,176},{96,0},{112,2... | collective-permute-start | bytes 110600 | tf_op jit(solution)/shard_map/ppermute | solution.py:363
  111.7 9.2 %collective-permute-start.11 = (bf16[18,128,128]{2,1,0:T(8,128)(2,1)S(1)}, bf16[18,128,128]{2,1,0:T(8,128)(2,1)S(1)}, u32[]{:S(2)}, u32[]{:S(2)}) collective-permute-start(bf16[18,128,128]{2,1,0:T(8,128)(2,1)S(1)} %bitcast.9), channel_id=1, source_target_pairs={{0,16},{16,0},{32,48},{48,32},{64,80},{80,64},{96,112},{112,96},{1... | collective-permute-start | bytes 1769480 | tf_op jit(solution)/shard_map/ppermute | solution.py:369
